TPU v7x, 32 devices: a whole 2x2x4 slice. The times are simulated.
32 devices in a mesh: groups: 2 (over y), req: 8 (over z, core), head: 2 (over x), rep: 1.
Axes of the slice: x: 2, y: 2, z: 4, core: 2. Of those that a mesh axis runs over, the one named last changes fastest.
Arguments:
- candidates: bfloat16 [32768, 1024], P(('groups', 'req', 'rep')), parts along dimension 0, may hold values from -6 to 6
- candidate_request: int32 [16, 2048], P(('groups', 'req'), 'rep'), parts along dimension 0, may hold values from 0 to 7, never falling along the last dimension, each value on 1 to 512 neighbouring positions
- request_owner: int32 [128, 1], P(('groups', 'req')), parts along dimension 0, may hold values from 0 to 7; in each aligned block of 8 rows (0 to 7, 8 to 15, ...) no two rows name the same one
- request_user: int32 [128], P(('groups', 'req')), parts along dimension 0, may hold values from 0 to 7
- request_blocks: int32 [16, 8], P(('groups', 'req')), parts along dimension 0, may hold values from 1 to 4, 24 in all within a row
- kv_cache: bfloat16 [128, 512, 2048], P(('groups', 'req'), None, 'head'), parts along dimension 0, may hold values from -6 to 6
- w_in: bfloat16 [1024, 4096], P(None, 'head'), may hold values from -0.1875 to 0.1875
- w_out: bfloat16 [1024, 1024], P('head'), may hold values from -0.1875 to 0.1875
Outputs:
- ranked: bfloat16 [32768, 1024], P(('groups', 'req', 'rep'), 'head'), parts along dimension 0
There are 2 independent parts, one for each index of `groups`. A program takes and returns all parts, laid end to end along the dimension named above; an argument that names none is the same for every part. Nothing has to cross between parts.
Inputs may be any that keep to these rules, and one draw needn't show every extreme that they name: `request_owner`: among the 8 requests of one req index at most 1 name the same owner, a bound that some block reaches of them. `request_blocks`: the 8 lengths of one req index sum to 24; some request has 4. `candidate_request`: never falls along the 2048 candidates of one req index; every request has 1 to 512 candidates, one exactly 512.
All inputs are finite; a program needn't handle non-finite values.
Results may differ from a plain program's by a relative error of at most 0.0056.
Values may be sent and summed in bfloat16 or wider, within the bound.
A program may use at most 128 MiB of HBM per device.

v0:
```python
import math

import jax
import jax.numpy as jnp
from jax import lax
from jax.experimental import pallas as pl
from jax.experimental.pallas import tpu as pltpu
from jax.sharding import PartitionSpec as P

HD = 128
BLOCK = 128
MOSTC = 512
EPSILON = 1e-05
VMEM_LIMIT = 58 * 1024 * 1024


def silu_half(y):
    return y + y * jnp.tanh(y)


def normalize(values):
    center = values - jnp.mean(values, axis=-1, keepdims=True)
    spread = jnp.mean(center * center, axis=-1, keepdims=True)
    return center * lax.rsqrt(spread + EPSILON)


def project_kernel(cand_ref, w_ref, q_ref, g_ref, self_ref):
    heads = q_ref.shape[1] // HD
    scale = 1.0 / math.sqrt(HD)
    normed = normalize(cand_ref[...].astype(jnp.float32)).astype(jnp.bfloat16)
    for h in range(heads):
        part = jnp.dot(
            normed, w_ref[:, h * 4 * HD : (h + 1) * 4 * HD], preferred_element_type=jnp.float32
        )
        part = silu_half(0.5 * part).astype(jnp.bfloat16)
        columns = slice(h * HD, (h + 1) * HD)
        query = part[:, 2 * HD : 3 * HD]
        g_ref[:, columns] = part[:, :HD]
        q_ref[:, columns] = query
        score = jnp.sum(
            query.astype(jnp.float32) * part[:, 3 * HD :].astype(jnp.float32), axis=-1, keepdims=True
        )
        weight = silu_half(score * (0.5 * scale))
        self_ref[:, columns] = weight * part[:, HD : 2 * HD].astype(jnp.float32)


def project(candidates, w_in):
    rows, width = candidates.shape
    columns = w_in.shape[1] // 4
    tile = min(256, rows)
    return pl.pallas_call(
        project_kernel,
        grid=(rows // tile,),
        in_specs=[
            pl.BlockSpec((tile, width), lambda i: (i, 0)),
            pl.BlockSpec(w_in.shape, lambda i: (0, 0), pipeline_mode=pl.Buffered(1)),
        ],
        out_specs=[pl.BlockSpec((tile, columns), lambda i: (i, 0))] * 3,
        out_shape=[
            jax.ShapeDtypeStruct((rows, columns), jnp.bfloat16),
            jax.ShapeDtypeStruct((rows, columns), jnp.bfloat16),
            jax.ShapeDtypeStruct((rows, columns), jnp.float32),
        ],
        cost_estimate=pl.CostEstimate(
            flops=2 * rows * width * 4 * columns,
            bytes_accessed=2 * (rows * width + width * 4 * columns + 4 * rows * columns),
            transcendentals=rows * 4 * columns,
        ),
        compiler_params=pltpu.CompilerParams(vmem_limit_bytes=VMEM_LIMIT),
        name="project",
    )(candidates, w_in)


def attend_kernel(tile, m, place, infos, q_ref, g_ref, self_ref, kv_ref, w_ref, own_ref, *rest):
    peer_refs, gated = rest[:-1], rest[-1]
    window, width = q_ref.shape
    heads = width // HD
    tokens = kv_ref.shape[1]
    columns = own_ref.shape[1]
    scale = 1.0 / math.sqrt(HD)
    who = jnp.bitwise_xor(place[0], m)
    first, start, end = infos[0, who], infos[1, who], infos[2, who]
    live = lax.broadcasted_iota(jnp.int32, (1, tokens), 1) < infos[3, who]

    def one_tile(t):
        rows = slice(t * tile, (t + 1) * tile)
        for h in range(heads):
            cols = slice(h * HD, (h + 1) * HD)
            keys = kv_ref[0, :, 2 * h * HD : (2 * h + 1) * HD]
            values = kv_ref[0, :, (2 * h + 1) * HD : (2 * h + 2) * HD]
            scores = lax.dot_general(
                q_ref[rows, cols], keys, (((1,), (1,)), ((), ())), preferred_element_type=jnp.float32
            )
            weights = silu_half(scores * (0.5 * scale))
            weights = jnp.where(live, weights, 0.0).astype(jnp.bfloat16)
            mixed = jnp.dot(weights, values, preferred_element_type=jnp.float32)
            normed = normalize(self_ref[rows, cols] + mixed)
            gated[rows, cols] = (normed * g_ref[rows, cols].astype(jnp.float32)).astype(jnp.bfloat16)
        partial = jnp.dot(gated[rows, :], w_ref[...], preferred_element_type=jnp.float32)
        own_ref[rows, :] = partial[:, :columns]
        for k, peer_ref in enumerate(peer_refs, 1):
            peer_ref[rows, :] = partial[:, k * columns : (k + 1) * columns].astype(jnp.bfloat16)

    for t in range(window // tile):
        low = first + t * tile
        pl.when(jnp.logical_and(low < end, low + tile > start))(lambda t=t: one_tile(t))


def attend(place, infos, m, queries, gates, selfs, cached, w_turned, window, ways):
    width = queries.shape[1]
    columns = w_turned.shape[1] // ways
    tokens, kvw = cached.shape[1:]
    tile = window // 3 if window % 48 == 0 else window
    rows = lambda i, place, infos: (
        pl.multiple_of(infos[0, jnp.bitwise_xor(place[0], m)], 16),
        0,
    )
    view = pl.BlockSpec((pl.Element(window), pl.Element(width)), rows)
    whole = pl.BlockSpec((window, columns), lambda i, place, infos: (0, 0))
    return pl.pallas_call(
        lambda *refs: attend_kernel(tile, m, *refs),
        grid_spec=pltpu.PrefetchScalarGridSpec(
            num_scalar_prefetch=2,
            grid=(1,),
            in_specs=[
                view,
                view,
                view,
                pl.BlockSpec((1, tokens, kvw), lambda i, place, infos: (0, 0, 0)),
                pl.BlockSpec(w_turned.shape, lambda i, place, infos: (0, 0)),
            ],
            out_specs=[whole] * ways,
            scratch_shapes=[pltpu.VMEM((window, width), jnp.bfloat16)],
        ),
        out_shape=[jax.ShapeDtypeStruct((window, columns), jnp.float32)]
        + [jax.ShapeDtypeStruct((window, columns), jnp.bfloat16)] * (ways - 1),
        cost_estimate=pl.CostEstimate(
            flops=4 * window * tokens * width + 2 * window * width * ways * columns,
            bytes_accessed=8 * window * width + 2 * tokens * kvw + 6 * window * ways * columns,
            transcendentals=window * tokens * width // HD,
        ),
        compiler_params=pltpu.CompilerParams(vmem_limit_bytes=VMEM_LIMIT),
        name="attend",
    )(place, infos, queries, gates, selfs, cached, w_turned)


def finish_kernel(m, ways, place, infos, total_ref, own_ref, *rest):
    peer_refs, out_ref = rest[: ways - 1], rest[-1]
    who = jnp.bitwise_xor(place[0], m)
    window = own_ref.shape[0]
    position = infos[0, who] + lax.broadcasted_iota(jnp.int32, (window, 1), 0)
    mine = jnp.logical_and(position >= infos[1, who], position < infos[2, who])
    before = total_ref[...].astype(jnp.float32)
    total = own_ref[...]
    for peer_ref in peer_refs:
        total = total + peer_ref[...].astype(jnp.float32)
    out_ref[...] = jnp.where(mine, total + before, before).astype(out_ref.dtype)


def finish(place, infos, m, own, peers, total, after=None):
    window, columns = own.shape
    late = [] if after is None else [after]
    rows = lambda i, place, infos: (
        pl.multiple_of(infos[0, jnp.bitwise_xor(place[0], m)], 16),
        0,
    )
    view = pl.BlockSpec((pl.Element(window), pl.Element(columns)), rows)
    whole = pl.BlockSpec((window, columns), lambda i, place, infos: (0, 0))
    return pl.pallas_call(
        lambda *refs: finish_kernel(m, 1 + len(peers), *refs),
        grid_spec=pltpu.PrefetchScalarGridSpec(
            num_scalar_prefetch=2,
            grid=(1,),
            in_specs=[view]
            + [whole] * (1 + len(peers))
            + [pl.BlockSpec(memory_space=pl.ANY)] * len(late),
            out_specs=view,
        ),
        out_shape=jax.ShapeDtypeStruct(total.shape, total.dtype),
        input_output_aliases={2: 0},
        cost_estimate=pl.CostEstimate(
            flops=3 * window * columns, bytes_accessed=10 * window * columns, transcendentals=0
        ),
        compiler_params=pltpu.CompilerParams(vmem_limit_bytes=VMEM_LIMIT),
        name="finish",
    )(place, infos, total, own, *peers, *late)


def pick_kernel(place, table, kv_ref, *rest):
    rest[-1][...] = kv_ref[...]


def pick(place, table, kv_cache, m, after):
    user = lambda i, place, table: (table[jnp.bitwise_xor(place[0], m), place[0]], 0, 0)
    block = (1,) + kv_cache.shape[1:]
    return pl.pallas_call(
        pick_kernel,
        grid_spec=pltpu.PrefetchScalarGridSpec(
            num_scalar_prefetch=2,
            grid=(1,),
            in_specs=[pl.BlockSpec(block, user)] + [pl.BlockSpec(memory_space=pl.ANY)] * len(after),
            out_specs=pl.BlockSpec(block, lambda i, place, table: (0, 0, 0)),
        ),
        out_shape=jax.ShapeDtypeStruct(block, kv_cache.dtype),
        compiler_params=pltpu.CompilerParams(vmem_limit_bytes=VMEM_LIMIT),
        name="pick",
    )(place, table, kv_cache, *after)


def exchange_order(count):
    far = [m for m in range(count) if 2 * m >= count][::-1]
    near = [m for m in range(2, count) if 2 * m < count][::-1]
    order = []
    while far or near:
        order += far[:1] + (near[:1] if len(far) > 2 or not far else [])
        near = near[1:] if len(far) > 2 or not far else near
        far = far[1:]
    return order


def per_device(
    candidates,
    candidate_request,
    request_owner,
    request_user,
    request_blocks,
    kv_cache,
    w_in,
    w_out,
):
    rows, width = candidates.shape
    count = lax.axis_size("req")
    ways = lax.axis_size("head")
    myself = lax.axis_index("req")
    side = lax.axis_index("head")
    columns = width // ways
    window = min(MOSTC + 16, rows)
    owners = request_owner[:, 0]
    everyone = jnp.arange(count, dtype=jnp.int32)
    names = (owners[None, :] == everyone[:, None]).astype(jnp.int32)
    wanted = jnp.sum(names * request_user[None, :], axis=1)
    table = lax.all_gather(wanted, "req", axis=0, tiled=False)
    place = myself[None].astype(jnp.int32)

    order = exchange_order(count)
    arrived = {}
    after = []
    for m in order + [1, 0]:
        picked = pick(place, table, kv_cache, m, after)
        after = [picked]
        if m:
            picked = lax.ppermute(picked, "req", [(i, i ^ m) for i in range(count)])
        arrived[m] = picked

    segment = candidate_request[0]
    served = jnp.sum(names * jnp.arange(owners.shape[0], dtype=jnp.int32)[None, :], axis=1)
    starts = jnp.sum((segment[None, :] < served[:, None]).astype(jnp.int32), axis=1)
    ends = jnp.sum((segment[None, :] <= served[:, None]).astype(jnp.int32), axis=1)
    exists = jnp.sum(names, axis=1) > 0
    ends = jnp.where(exists, ends, starts)
    live = jnp.sum(names * request_blocks[0][None, :], axis=1) * BLOCK
    firsts = jnp.minimum(starts // 16 * 16, rows - window)
    infos = jnp.stack([firsts, starts, ends, live])

    queries, gates, selfs = project(candidates, w_in)
    turned = jnp.concatenate(
        [
            lax.dynamic_slice_in_dim(w_out, ((side + k) % ways) * columns, columns, 1)
            for k in range(ways)
        ],
        axis=1,
    )
    ranked = lax.dynamic_slice_in_dim(candidates, side * columns, columns, 1)
    sequence = [0, 1] + order
    pending = []
    ready = []
    for m in sequence:
        if ready:
            table_in, *ready = lax.optimization_barrier((infos, *ready))
        else:
            table_in = infos
        own, *peers = attend(
            place, table_in, m, queries, gates, selfs, arrived[m], turned, window, ways
        )
        landed = [
            lax.ppermute(peer, "head", [(i, (i + k) % ways) for i in range(ways)])
            for k, peer in enumerate(peers, 1)
        ]
        if pending:
            ranked = finish(place, infos, *pending.pop(), ranked, after=own)
        pending.append((m, own, landed))
        ready = [own, ranked]
    return finish(place, infos, *pending.pop(), ranked)


def solution(mesh):
    placed = (
        P(("groups", "req", "rep"), None),
        P(("groups", "req"), "rep"),
        P(("groups", "req"), None),
        P(("groups", "req")),
        P(("groups", "req"), None),
        P(("groups", "req"), None, "head"),
        P(None, "head"),
        P("head", None),
    )

    return jax.shard_map(
        per_device,
        mesh=mesh,
        in_specs=placed,
        out_specs=P(("groups", "req", "rep"), "head"),
        check_vma=False,
    )
```

profile of v0, /device:TPU:0, one launch (start us, length us, event | category | flops | bytes accessed | tf_op | source)
XLA Modules:
  0.0 243.6 jit_solution(134559993165339717)
XLA Ops:
  0.0 1.2 dynamic-slice
  3.0 10.6 %all-reduce = s32[64]{0:T(128)S(1)} all-reduce(s32[64]{0:T(128)S(1)} %dynamic-update-slice), channel_id=2, replica_groups=mesh['groups'=2,'req'=8,'head'=2,'rep'=1] {'req'}, use_global_device_ids=true, to_apply=%add | all-reduce | flops 64 | bytes 512
  14.3 3.0 %pick.8.rest_0_ = bf16[1,512,1024]{2,1,0:T(8,128)(2,1)} custom-call(s32[1]{0:T(128)} %bitcast.place.refs_0_, s32[8,8]{1,0:T(8,128)} %reshape.87.table, bf16[8,512,1024]{2,1,0:T(8,128)(2,1)} %kv_ref.15), custom_call_target="tpu_custom_call" | custom-call | tf_op jit(solution)/shard_map/pick/pallas_call | solution.py:196
  17.3 3.0 %pick.9.rest_0_ = bf16[1,512,1024]{2,1,0:T(8,128)(2,1)} custom-call(s32[1]{0:T(128)} %bitcast.place.refs_0_, s32[8,8]{1,0:T(8,128)} %reshape.87.table, bf16[8,512,1024]{2,1,0:T(8,128)(2,1)} %kv_ref.15, bf16[1,512,1024]{2,1,0:T(8,128)(2,1)} %pick.8.rest_0_), custom_call_target="tpu_custom_call" | custom-call | tf_op jit(solution)/shard_map/pick/pallas_call | solution.py:196
  20.9 3.0 %pick.10.rest_0_ = bf16[1,512,1024]{2,1,0:T(8,128)(2,1)} custom-call(s32[1]{0:T(128)} %bitcast.place.refs_0_, s32[8,8]{1,0:T(8,128)} %reshape.87.table, bf16[8,512,1024]{2,1,0:T(8,128)(2,1)} %kv_ref.15, bf16[1,512,1024]{2,1,0:T(8,128)(2,1)} %pick.9.rest_0_), custom_call_target="tpu_custom_call" | custom-call | tf_op jit(solution)/shard_map/pick/pallas_call | solution.py:196
  23.9 3.0 %pick.11.rest_0_ = bf16[1,512,1024]{2,1,0:T(8,128)(2,1)} custom-call(s32[1]{0:T(128)} %bitcast.place.refs_0_, s32[8,8]{1,0:T(8,128)} %reshape.87.table, bf16[8,512,1024]{2,1,0:T(8,128)(2,1)} %kv_ref.15, bf16[1,512,1024]{2,1,0:T(8,128)(2,1)} %pick.10.rest_0_), custom_call_target="tpu_custom_call" | custom-call | tf_op jit(solution)/shard_map/pick/pallas_call | solution.py:196
  26.9 3.0 %pick.12.rest_0_ = bf16[1,512,1024]{2,1,0:T(8,128)(2,1)} custom-call(s32[1]{0:T(128)} %bitcast.place.refs_0_, s32[8,8]{1,0:T(8,128)} %reshape.87.table, bf16[8,512,1024]{2,1,0:T(8,128)(2,1)} %kv_ref.15, bf16[1,512,1024]{2,1,0:T(8,128)(2,1)} %pick.11.rest_0_), custom_call_target="tpu_custom_call" | custom-call | tf_op jit(solution)/shard_map/pick/pallas_call | solution.py:196
  30.0 3.0 %pick.13.rest_0_ = bf16[1,512,1024]{2,1,0:T(8,128)(2,1)} custom-call(s32[1]{0:T(128)} %bitcast.place.refs_0_, s32[8,8]{1,0:T(8,128)} %reshape.87.table, bf16[8,512,1024]{2,1,0:T(8,128)(2,1)} %kv_ref.15, bf16[1,512,1024]{2,1,0:T(8,128)(2,1)} %pick.12.rest_0_), custom_call_target="tpu_custom_call" | custom-call | tf_op jit(solution)/shard_map/pick/pallas_call | solution.py:196
  33.0 3.2 %pick.14.rest_0_ = bf16[1,512,1024]{2,1,0:T(8,128)(2,1)} custom-call(s32[1]{0:T(128)} %bitcast.place.refs_0_, s32[8,8]{1,0:T(8,128)} %reshape.87.table, bf16[8,512,1024]{2,1,0:T(8,128)(2,1)} %kv_ref.15, bf16[1,512,1024]{2,1,0:T(8,128)(2,1)} %pick.13.rest_0_), custom_call_target="tpu_custom_call" | custom-call | tf_op jit(solution)/shard_map/pick/pallas_call | solution.py:196
  36.6 1.1 pad_maximum_fusion.refs_6_
  37.8 18.5 %project.1 = (bf16[2048,512]{1,0:T(8,128)(2,1)}, bf16[2048,512]{1,0:T(8,128)(2,1)}, f32[2048,512]{1,0:T(8,128)}) custom-call(bf16[2048,1024]{1,0:T(8,128)(2,1)} %cand_ref.1, bf16[1024,2048]{1,0:T(8,128)(2,1)} %w_ref.1), custom_call_target="tpu_custom_call" | custom-call | flops 8589934592 | bytes 16777216 | tf_op jit(solution)/shard_map/project/pallas_call | solution.py:51
  57.1 3.0 %pick.15.refs_5_ = bf16[1,512,1024]{2,1,0:T(8,128)(2,1)} custom-call(s32[1]{0:T(128)} %bitcast.place.refs_0_, s32[8,8]{1,0:T(8,128)} %reshape.87.table, bf16[8,512,1024]{2,1,0:T(8,128)(2,1)} %kv_ref.15, bf16[1,512,1024]{2,1,0:T(8,128)(2,1)} %pick.14.rest_0_), custom_call_target="tpu_custom_call" | custom-call | tf_op jit(solution)/shard_map/pick/pallas_call | solution.py:196
  60.1 8.4 %attend.8 = (f32[528,512]{1,0:T(8,128)}, bf16[528,512]{1,0:T(8,128)(2,1)}) custom-call(s32[1]{0:T(128)} %bitcast.place.refs_0_, s32[4,8]{1,0:T(4,128)} %pad_add_fusion.refs_1_, bf16[2048,512]{1,0:T(8,128)(2,1)} %get-tuple-element.31.refs_2_, bf16[2048,512]{1,0:T(8,128)(2,1)} %get-tuple-element.32.refs_3_, f32[2048,512]{1,0:T(8,128)} %get-tuple-element.33.refs_4_, ...), custom_call_target="tpu_custom_call" | custom-call | flops 1107296256 | bytes 6455296 | tf_op jit(solution)/shard_map/attend/pallas_call | solution.py:120
  68.4 1.5 collective-permute-start
  70.0 3.0 %constant_dynamic-slice_fusion.2.refs_2_ = bf16[2048,512]{1,0:T(8,128)(2,1)} fusion(bf16[2048,1024]{1,0:T(8,128)(2,1)} %cand_ref.1, s32[]{:T(128)S(6)} %select_n.44), kind=kLoop, calls=%fused_computation.16 | loop fusion | bytes 4194308 | tf_op jit(solution)/shard_map/dynamic_slice | solution.py:273
  73.0 7.1 %attend.9 = (f32[528,512]{1,0:T(8,128)}, bf16[528,512]{1,0:T(8,128)(2,1)}) custom-call(s32[1]{0:T(128)} %bitcast.place.refs_0_, s32[4,8]{1,0:T(4,128)} %pad_add_fusion.refs_1_, bf16[2048,512]{1,0:T(8,128)(2,1)} %get-tuple-element.31.refs_2_, bf16[2048,512]{1,0:T(8,128)(2,1)} %get-tuple-element.32.refs_3_, f32[2048,512]{1,0:T(8,128)} %get-tuple-element.33.refs_4_, ...), custom_call_target="tpu_custom_call" | custom-call | flops 1107296256 | bytes 6455296 | tf_op jit(solution)/shard_map/attend/pallas_call | solution.py:120
  80.7 1.1 collective-permute-done.refs_4_
  81.8 2.5 %collective-permute-start.9 = (bf16[1,512,1024]{2,1,0:T(8,128)(2,1)S(1)}, bf16[1,512,1024]{2,1,0:T(8,128)(2,1)}, u32[]{:S(2)}, u32[]{:S(2)}) collective-permute-start(bf16[1,512,1024]{2,1,0:T(8,128)(2,1)S(1)} %copy-done.2), channel_id=1, source_target_pairs={{0,4},{2,6},{4,0},{6,2},{8,12},{10,14},{12,8},{14,10},{1,5},{3,7},... | collective-permute-start | bytes 3145736 | tf_op jit(solution)/shard_map/ppermute | solution.py:252
  84.4 3.3 %finish.8.refs_2_ = bf16[2048,512]{1,0:T(8,128)(2,1)} custom-call(s32[1]{0:T(128)} %bitcast.place.refs_0_, s32[4,8]{1,0:T(4,128)} %pad_add_fusion.refs_1_, bf16[2048,512]{1,0:T(8,128)(2,1)} %constant_dynamic-slice_fusion.2.refs_2_, f32[528,512]{1,0:T(8,128)} %get-tuple-element.34.refs_3_, ...), custom_call_target="tpu_custom_call", output_to_operand_aliasing={{}: (2, {})} | custom-call | flops 811008 | bytes 2703360 | tf_op jit(solution)/shard_map/finish/pallas_call | solution.py:169
  87.7 1.0 copy-done.5
  88.7 6.9 %attend.10 = (f32[528,512]{1,0:T(8,128)}, bf16[528,512]{1,0:T(8,128)(2,1)}) custom-call(s32[1]{0:T(128)} %bitcast.place.refs_0_, s32[4,8]{1,0:T(4,128)} %pad_add_fusion.refs_1_, bf16[2048,512]{1,0:T(8,128)(2,1)} %get-tuple-element.31.refs_2_, bf16[2048,512]{1,0:T(8,128)(2,1)} %get-tuple-element.32.refs_3_, f32[2048,512]{1,0:T(8,128)} %get-tuple-element.33.refs_4_, ...), custom_call_target="tpu_custom_call" | custom-call | flops 1107296256 | bytes 6455296 | tf_op jit(solution)/shard_map/attend/pallas_call | solution.py:120
  95.6 1.6 collective-permute-start.4
  98.0 3.3 %finish.9.refs_2_ = bf16[2048,512]{1,0:T(8,128)(2,1)} custom-call(s32[1]{0:T(128)} %bitcast.place.refs_0_, s32[4,8]{1,0:T(4,128)} %pad_add_fusion.refs_1_, bf16[2048,512]{1,0:T(8,128)(2,1)} %finish.8.refs_2_, f32[528,512]{1,0:T(8,128)} %get-tuple-element.37.refs_5_.refs_3_, bf16[528,512]{1,0:T(8,128)(2,1)} %copy-done.9, ...), custom_call_target="tpu_custom_call", output_to_operand_aliasing={{}: (2, {})} | custom-call | flops 811008 | bytes 2703360 | tf_op jit(solution)/shard_map/finish/pallas_call | solution.py:169
  101.3 1.0 copy-done.4
  102.3 5.6 %attend.11 = (f32[528,512]{1,0:T(8,128)}, bf16[528,512]{1,0:T(8,128)(2,1)}) custom-call(s32[1]{0:T(128)} %bitcast.place.refs_0_, s32[4,8]{1,0:T(4,128)} %pad_add_fusion.refs_1_, bf16[2048,512]{1,0:T(8,128)(2,1)} %get-tuple-element.31.refs_2_, bf16[2048,512]{1,0:T(8,128)(2,1)} %get-tuple-element.32.refs_3_, f32[2048,512]{1,0:T(8,128)} %get-tuple-element.33.refs_4_, ...), custom_call_target="tpu_custom_call" | custom-call | flops 1107296256 | bytes 6455296 | tf_op jit(solution)/shard_map/attend/pallas_call | solution.py:120
  108.3 2.5 %collective-permute-start.11 = (bf16[1,512,1024]{2,1,0:T(8,128)(2,1)S(1)}, bf16[1,512,1024]{2,1,0:T(8,128)(2,1)}, u32[]{:S(2)}, u32[]{:S(2)}) collective-permute-start(bf16[1,512,1024]{2,1,0:T(8,128)(2,1)S(1)} %copy-done.1), channel_id=1, source_target_pairs={{0,10},{2,8},{4,14},{6,12},{8,2},{10,0},{12,6},{14,4},{1,11},{3,9}... | collective-permute-start | bytes 3145736 | tf_op jit(solution)/shard_map/ppermute | solution.py:252
  110.8 3.1 %collective-permute-start.13 = (bf16[1,512,1024]{2,1,0:T(8,128)(2,1)S(1)}, bf16[1,512,1024]{2,1,0:T(8,128)(2,1)S(1)}, u32[]{:S(2)}, u32[]{:S(2)}) collective-permute-start(bf16[1,512,1024]{2,1,0:T(8,128)(2,1)S(1)} %copy-done), channel_id=1, source_target_pairs={{0,8},{2,10},{4,12},{6,14},{8,0},{10,2},{12,4},{14,6},{1,9},{3,11}... | collective-permute-start | bytes 3145736 | tf_op jit(solution)/shard_map/ppermute | solution.py:252
  113.9 3.3 %finish.10.refs_2_ = bf16[2048,512]{1,0:T(8,128)(2,1)} custom-call(s32[1]{0:T(128)} %bitcast.place.refs_0_, s32[4,8]{1,0:T(4,128)} %pad_add_fusion.refs_1_, bf16[2048,512]{1,0:T(8,128)(2,1)} %finish.9.refs_2_, f32[528,512]{1,0:T(8,128)} %get-tuple-element.40.refs_5_.refs_3_, bf16[528,512]{1,0:T(8,128)(2,1)} %copy-done.10, ...), custom_call_target="tpu_custom_call", output_to_operand_aliasing={{}: (2, {})} | custom-call | flops 811008 | bytes 2703360 | tf_op jit(solution)/shard_map/finish/pallas_call | solution.py:169
  117.2 5.5 %attend.12 = (f32[528,512]{1,0:T(8,128)}, bf16[528,512]{1,0:T(8,128)(2,1)}) custom-call(s32[1]{0:T(128)} %bitcast.place.refs_0_, s32[4,8]{1,0:T(4,128)} %pad_add_fusion.refs_1_, bf16[2048,512]{1,0:T(8,128)(2,1)} %get-tuple-element.31.refs_2_, bf16[2048,512]{1,0:T(8,128)(2,1)} %get-tuple-element.32.refs_3_, f32[2048,512]{1,0:T(8,128)} %get-tuple-element.33.refs_4_, ...), custom_call_target="tpu_custom_call" | custom-call | flops 1107296256 | bytes 6455296 | tf_op jit(solution)/shard_map/attend/pallas_call | solution.py:120
  122.7 1.5 collective-permute-start.8
  124.2 3.3 %finish.11.refs_2_ = bf16[2048,512]{1,0:T(8,128)(2,1)} custom-call(s32[1]{0:T(128)} %bitcast.place.refs_0_, s32[4,8]{1,0:T(4,128)} %pad_add_fusion.refs_1_, bf16[2048,512]{1,0:T(8,128)(2,1)} %finish.10.refs_2_, f32[528,512]{1,0:T(8,128)} %get-tuple-element.43.refs_5_.refs_3_, ...), custom_call_target="tpu_custom_call", output_to_operand_aliasing={{}: (2, {})} | custom-call | flops 811008 | bytes 2703360 | tf_op jit(solution)/shard_map/finish/pallas_call | solution.py:169
  127.5 2.2 collective-permute-done.9.refs_5_
  129.7 8.3 %attend.13 = (f32[528,512]{1,0:T(8,128)}, bf16[528,512]{1,0:T(8,128)(2,1)}) custom-call(s32[1]{0:T(128)} %bitcast.place.refs_0_, s32[4,8]{1,0:T(4,128)} %pad_add_fusion.refs_1_, bf16[2048,512]{1,0:T(8,128)(2,1)} %get-tuple-element.31.refs_2_, bf16[2048,512]{1,0:T(8,128)(2,1)} %get-tuple-element.32.refs_3_, f32[2048,512]{1,0:T(8,128)} %get-tuple-element.33.refs_4_, ...), custom_call_target="tpu_custom_call" | custom-call | flops 1107296256 | bytes 6455296 | tf_op jit(solution)/shard_map/attend/pallas_call | solution.py:120
  138.0 1.5 collective-permute-start.10
  139.5 0.9 copy-done.12
  140.4 3.3 %finish.12.refs_2_ = bf16[2048,512]{1,0:T(8,128)(2,1)} custom-call(s32[1]{0:T(128)} %bitcast.place.refs_0_, s32[4,8]{1,0:T(4,128)} %pad_add_fusion.refs_1_, bf16[2048,512]{1,0:T(8,128)(2,1)} %finish.11.refs_2_, f32[528,512]{1,0:T(8,128)} %get-tuple-element.46.refs_5_.refs_3_, bf16[528,512]{1,0:T(8,128)(2,1)} %copy-done.12, ...), custom_call_target="tpu_custom_call", output_to_operand_aliasing={{}: (2, {})} | custom-call | flops 811008 | bytes 2703360 | tf_op jit(solution)/shard_map/finish/pallas_call | solution.py:169
  143.6 51.0 %collective-permute-done.11.refs_5_ = bf16[1,512,1024]{2,1,0:T(8,128)(2,1)} collective-permute-done((bf16[1,512,1024]{2,1,0:T(8,128)(2,1)S(1)}, bf16[1,512,1024]{2,1,0:T(8,128)(2,1)}, u32[]{:S(2)}, u32[]{:S(2)}) %collective-permute-start.11) | collective-permute-done | bytes 1048608 | tf_op jit(solution)/shard_map/ppermute | solution.py:252
  194.7 7.0 %attend.14 = (f32[528,512]{1,0:T(8,128)}, bf16[528,512]{1,0:T(8,128)(2,1)}) custom-call(s32[1]{0:T(128)} %bitcast.place.refs_0_, s32[4,8]{1,0:T(4,128)} %pad_add_fusion.refs_1_, bf16[2048,512]{1,0:T(8,128)(2,1)} %get-tuple-element.31.refs_2_, bf16[2048,512]{1,0:T(8,128)(2,1)} %get-tuple-element.32.refs_3_, f32[2048,512]{1,0:T(8,128)} %get-tuple-element.33.refs_4_, ...), custom_call_target="tpu_custom_call" | custom-call | flops 1107296256 | bytes 6455296 | tf_op jit(solution)/shard_map/attend/pallas_call | solution.py:120
  201.7 1.5 collective-permute-start.12
  203.2 0.9 copy-done.13
  204.0 3.3 %finish.13.refs_2_ = bf16[2048,512]{1,0:T(8,128)(2,1)} custom-call(s32[1]{0:T(128)} %bitcast.place.refs_0_, s32[4,8]{1,0:T(4,128)} %pad_add_fusion.refs_1_, bf16[2048,512]{1,0:T(8,128)(2,1)} %finish.12.refs_2_, f32[528,512]{1,0:T(8,128)} %get-tuple-element.49.refs_5_.refs_3_, bf16[528,512]{1,0:T(8,128)(2,1)} %copy-done.13, ...), custom_call_target="tpu_custom_call", output_to_operand_aliasing={{}: (2, {})} | custom-call | flops 811008 | bytes 2703360 | tf_op jit(solution)/shard_map/finish/pallas_call | solution.py:169
  207.3 10.7 %collective-permute-done.13.refs_5_ = bf16[1,512,1024]{2,1,0:T(8,128)(2,1)S(1)} collective-permute-done((bf16[1,512,1024]{2,1,0:T(8,128)(2,1)S(1)}, bf16[1,512,1024]{2,1,0:T(8,128)(2,1)S(1)}, u32[]{:S(2)}, u32[]{:S(2)}) %collective-permute-start.13) | collective-permute-done | bytes 1048608 | tf_op jit(solution)/shard_map/ppermute | solution.py:252
  218.0 1.0 copy-done.6
  218.9 7.0 %attend.15 = (f32[528,512]{1,0:T(8,128)}, bf16[528,512]{1,0:T(8,128)(2,1)}) custom-call(s32[1]{0:T(128)} %bitcast.place.refs_0_, s32[4,8]{1,0:T(4,128)} %pad_add_fusion.refs_1_, bf16[2048,512]{1,0:T(8,128)(2,1)} %get-tuple-element.31.refs_2_, bf16[2048,512]{1,0:T(8,128)(2,1)} %get-tuple-element.32.refs_3_, f32[2048,512]{1,0:T(8,128)} %get-tuple-element.33.refs_4_, ...), custom_call_target="tpu_custom_call" | custom-call | flops 1107296256 | bytes 6455296 | tf_op jit(solution)/shard_map/attend/pallas_call | solution.py:120
  225.9 1.5 collective-permute-start.14
  228.2 3.3 %finish.14.refs_2_ = bf16[2048,512]{1,0:T(8,128)(2,1)} custom-call(s32[1]{0:T(128)} %bitcast.place.refs_0_, s32[4,8]{1,0:T(4,128)} %pad_add_fusion.refs_1_, bf16[2048,512]{1,0:T(8,128)(2,1)} %finish.13.refs_2_, f32[528,512]{1,0:T(8,128)} %get-tuple-element.52.refs_5_.refs_3_, bf16[528,512]{1,0:T(8,128)(2,1)} %copy-done.11, ...), custom_call_target="tpu_custom_call", output_to_operand_aliasing={{}: (2, {})} | custom-call | flops 811008 | bytes 2703360 | tf_op jit(solution)/shard_map/finish/pallas_call | solution.py:169
  231.5 8.0 %collective-permute-done.14.refs_4_ = bf16[528,512]{1,0:T(8,128)(2,1)S(1)} collective-permute-done((bf16[528,512]{1,0:T(8,128)(2,1)}, bf16[528,512]{1,0:T(8,128)(2,1)S(1)}, u32[]{:S(2)}, u32[]{:S(2)}) %collective-permute-start.14) | collective-permute-done | bytes 540704 | tf_op jit(solution)/shard_map/ppermute | solution.py:286
  240.3 3.3 %finish.15 = bf16[2048,512]{1,0:T(8,128)(2,1)} custom-call(s32[1]{0:T(128)} %bitcast.place.refs_0_, s32[4,8]{1,0:T(4,128)} %pad_add_fusion.refs_1_, bf16[2048,512]{1,0:T(8,128)(2,1)} %finish.14.refs_2_, f32[528,512]{1,0:T(8,128)} %get-tuple-element.55.refs_5_.refs_3_, bf16[528,512]{1,0:T(8,128)(2,1)} %copy-done.14), custom_call_target="tpu_custom_call", output_to_operand_aliasing={{}: (2, {})} | custom-call | flops 811008 | bytes 2703360 | tf_op jit(solution)/shard_map/finish/pallas_call | solution.py:169
  (52 shorter events, 7.2 us)
Async XLA Ops:
  17.3 70.4 %collective-permute-start.3 = (bf16[1,512,1024]{2,1,0:T(8,128)(2,1)}, bf16[1,512,1024]{2,1,0:T(8,128)(2,1)S(1)}, u32[]{:S(2)}, u32[]{:S(2)}) collective-permute-start(bf16[1,512,1024]{2,1,0:T(8,128)(2,1)} %pick.8.rest_0_), channel_id=1, source_target_pairs={{0,14},{2,12},{4,10},{6,8},{8,6},{10,4},{12,2},{14,0},{1,15},{3,13... | collective-permute-start | bytes 3145736 | tf_op jit(solution)/shard_map/ppermute | solution.py:252
  20.3 81.0 %collective-permute-start.5 = (bf16[1,512,1024]{2,1,0:T(8,128)(2,1)}, bf16[1,512,1024]{2,1,0:T(8,128)(2,1)S(1)}, u32[]{:S(2)}, u32[]{:S(2)}) collective-permute-start(bf16[1,512,1024]{2,1,0:T(8,128)(2,1)} %pick.9.rest_0_), channel_id=1, source_target_pairs={{0,6},{2,4},{4,2},{6,0},{8,14},{10,12},{12,10},{14,8},{1,7},{3,5},... | collective-permute-start | bytes 3145736 | tf_op jit(solution)/shard_map/ppermute | solution.py:252
  33.0 3.6 %copy-start.7 = (bf16[512,1024]{1,0:T(8,128)(2,1)S(1)}, bf16[512,1024]{1,0:T(8,128)(2,1)}, u32[]{:S(2)}) copy-start(bf16[512,1024]{1,0:T(8,128)(2,1)} %param.15) | copy-start | bytes 3145732
  36.2 36.8 %collective-permute-start.1 = (bf16[1,512,1024]{2,1,0:T(8,128)(2,1)}, bf16[1,512,1024]{2,1,0:T(8,128)(2,1)}, u32[]{:S(2)}, u32[]{:S(2)}) collective-permute-start(bf16[1,512,1024]{2,1,0:T(8,128)(2,1)} %pick.14.rest_0_), channel_id=1, source_target_pairs={{0,2},{2,0},{4,6},{6,4},{8,10},{10,8},{12,14},{14,12},{1,3},{3,1},... | collective-permute-start | bytes 3145736 | tf_op jit(solution)/shard_map/ppermute | solution.py:252
  37.8 18.5 %copy-start.15 = (s32[1,2048]{1,0:T(1,128)S(1)}, s32[1,2048]{1,0:T(1,128)}, u32[]{:S(2)}) copy-start(s32[1,2048]{1,0:T(1,128)} %param.9) | copy-start | bytes 24580
  68.4 13.4 %collective-permute-start = (bf16[528,512]{1,0:T(8,128)(2,1)}, bf16[528,512]{1,0:T(8,128)(2,1)S(1)}, u32[]{:S(2)}, u32[]{:S(2)}) collective-permute-start(bf16[528,512]{1,0:T(8,128)(2,1)} %get-tuple-element.35), channel_id=1, source_target_pairs={{0,1},{1,0},{2,3},{3,2},{4,5},{5,4},{6,7},{7,6},{8,9},{9,8},{10,11... | collective-permute-start | bytes 1622024 | tf_op jit(solution)/shard_map/ppermute | solution.py:286
  73.0 7.6 %copy-start.3 = (bf16[1,512,1024]{2,1,0:T(8,128)(2,1)S(1)}, bf16[1,512,1024]{2,1,0:T(8,128)(2,1)}, u32[]{:S(2)}) copy-start(bf16[1,512,1024]{2,1,0:T(8,128)(2,1)} %pick.10.rest_0_) | copy-start | bytes 3145732
  73.0 8.8 %copy-start.2 = (bf16[1,512,1024]{2,1,0:T(8,128)(2,1)S(1)}, bf16[1,512,1024]{2,1,0:T(8,128)(2,1)}, u32[]{:S(2)}) copy-start(bf16[1,512,1024]{2,1,0:T(8,128)(2,1)} %pick.11.rest_0_) | copy-start | bytes 3145732
  80.1 17.1 %collective-permute-start.2 = (bf16[528,512]{1,0:T(8,128)(2,1)}, bf16[528,512]{1,0:T(8,128)(2,1)S(1)}, u32[]{:S(2)}, u32[]{:S(2)}) collective-permute-start(bf16[528,512]{1,0:T(8,128)(2,1)} %get-tuple-element.38), channel_id=1, source_target_pairs={{0,1},{1,0},{2,3},{3,2},{4,5},{5,4},{6,7},{7,6},{8,9},{9,8},{10,11... | collective-permute-start | bytes 1622024 | tf_op jit(solution)/shard_map/ppermute | solution.py:286
  80.6 36.6 %collective-permute-start.7 = (bf16[1,512,1024]{2,1,0:T(8,128)(2,1)S(1)}, bf16[1,512,1024]{2,1,0:T(8,128)(2,1)}, u32[]{:S(2)}, u32[]{:S(2)}) collective-permute-start(bf16[1,512,1024]{2,1,0:T(8,128)(2,1)S(1)} %copy-done.3), channel_id=1, source_target_pairs={{0,12},{2,14},{4,8},{6,10},{8,4},{10,6},{12,0},{14,2},{1,13},{3,15... | collective-permute-start | bytes 3145736 | tf_op jit(solution)/shard_map/ppermute | solution.py:252
  81.8 2.5 %copy-start.8 = (bf16[528,512]{1,0:T(8,128)(2,1)}, bf16[528,512]{1,0:T(8,128)(2,1)S(1)}, u32[]{:S(2)}) copy-start(bf16[528,512]{1,0:T(8,128)(2,1)S(1)} %collective-permute-done.refs_4_) | copy-start | bytes 1622020
  81.8 47.8 %collective-permute-start.9 = (bf16[1,512,1024]{2,1,0:T(8,128)(2,1)S(1)}, bf16[1,512,1024]{2,1,0:T(8,128)(2,1)}, u32[]{:S(2)}, u32[]{:S(2)}) collective-permute-start(bf16[1,512,1024]{2,1,0:T(8,128)(2,1)S(1)} %copy-done.2), channel_id=1, source_target_pairs={{0,4},{2,6},{4,0},{6,2},{8,12},{10,14},{12,8},{14,10},{1,5},{3,7},... | collective-permute-start | bytes 3145736 | tf_op jit(solution)/shard_map/ppermute | solution.py:252
  87.7 1.0 copy-start.5
  95.6 15.3 %collective-permute-start.4 = (bf16[528,512]{1,0:T(8,128)(2,1)}, bf16[528,512]{1,0:T(8,128)(2,1)S(1)}, u32[]{:S(2)}, u32[]{:S(2)}) collective-permute-start(bf16[528,512]{1,0:T(8,128)(2,1)} %get-tuple-element.41), channel_id=1, source_target_pairs={{0,1},{1,0},{2,3},{3,2},{4,5},{5,4},{6,7},{7,6},{8,9},{9,8},{10,11... | collective-permute-start | bytes 1622024 | tf_op jit(solution)/shard_map/ppermute | solution.py:286
  97.2 0.8 copy-start.9
  101.3 7.0 %copy-start.1 = (bf16[1,512,1024]{2,1,0:T(8,128)(2,1)S(1)}, bf16[1,512,1024]{2,1,0:T(8,128)(2,1)}, u32[]{:S(2)}) copy-start(bf16[1,512,1024]{2,1,0:T(8,128)(2,1)} %pick.12.rest_0_) | copy-start | bytes 3145732
  101.3 9.5 %copy-start = (bf16[1,512,1024]{2,1,0:T(8,128)(2,1)S(1)}, bf16[1,512,1024]{2,1,0:T(8,128)(2,1)}, u32[]{:S(2)}) copy-start(bf16[1,512,1024]{2,1,0:T(8,128)(2,1)} %pick.13.rest_0_) | copy-start | bytes 3145732
  101.3 1.0 copy-start.4
  107.9 16.3 %collective-permute-start.6 = (bf16[528,512]{1,0:T(8,128)(2,1)}, bf16[528,512]{1,0:T(8,128)(2,1)}, u32[]{:S(2)}, u32[]{:S(2)}) collective-permute-start(bf16[528,512]{1,0:T(8,128)(2,1)} %get-tuple-element.44), channel_id=1, source_target_pairs={{0,1},{1,0},{2,3},{3,2},{4,5},{5,4},{6,7},{7,6},{8,9},{9,8},{10,11... | collective-permute-start | bytes 1622024 | tf_op jit(solution)/shard_map/ppermute | solution.py:286
  108.3 86.4 %collective-permute-start.11 = (bf16[1,512,1024]{2,1,0:T(8,128)(2,1)S(1)}, bf16[1,512,1024]{2,1,0:T(8,128)(2,1)}, u32[]{:S(2)}, u32[]{:S(2)}) collective-permute-start(bf16[1,512,1024]{2,1,0:T(8,128)(2,1)S(1)} %copy-done.1), channel_id=1, source_target_pairs={{0,10},{2,8},{4,14},{6,12},{8,2},{10,0},{12,6},{14,4},{1,11},{3,9}... | collective-permute-start | bytes 3145736 | tf_op jit(solution)/shard_map/ppermute | solution.py:252
  110.8 3.1 %copy-start.10 = (bf16[528,512]{1,0:T(8,128)(2,1)}, bf16[528,512]{1,0:T(8,128)(2,1)S(1)}, u32[]{:S(2)}) copy-start(bf16[528,512]{1,0:T(8,128)(2,1)S(1)} %collective-permute-done.4.refs_4_) | copy-start | bytes 1622020
  110.8 107.1 %collective-permute-start.13 = (bf16[1,512,1024]{2,1,0:T(8,128)(2,1)S(1)}, bf16[1,512,1024]{2,1,0:T(8,128)(2,1)S(1)}, u32[]{:S(2)}, u32[]{:S(2)}) collective-permute-start(bf16[1,512,1024]{2,1,0:T(8,128)(2,1)S(1)} %copy-done), channel_id=1, source_target_pairs={{0,8},{2,10},{4,12},{6,14},{8,0},{10,2},{12,4},{14,6},{1,9},{3,11}... | collective-permute-start | bytes 3145736 | tf_op jit(solution)/shard_map/ppermute | solution.py:252
  122.7 16.8 %collective-permute-start.8 = (bf16[528,512]{1,0:T(8,128)(2,1)}, bf16[528,512]{1,0:T(8,128)(2,1)S(1)}, u32[]{:S(2)}, u32[]{:S(2)}) collective-permute-start(bf16[528,512]{1,0:T(8,128)(2,1)} %get-tuple-element.47), channel_id=1, source_target_pairs={{0,1},{1,0},{2,3},{3,2},{4,5},{5,4},{6,7},{7,6},{8,9},{9,8},{10,11... | collective-permute-start | bytes 1622024 | tf_op jit(solution)/shard_map/ppermute | solution.py:286
  138.0 65.2 %collective-permute-start.10 = (bf16[528,512]{1,0:T(8,128)(2,1)}, bf16[528,512]{1,0:T(8,128)(2,1)S(1)}, u32[]{:S(2)}, u32[]{:S(2)}) collective-permute-start(bf16[528,512]{1,0:T(8,128)(2,1)} %get-tuple-element.50), channel_id=1, source_target_pairs={{0,1},{1,0},{2,3},{3,2},{4,5},{5,4},{6,7},{7,6},{8,9},{9,8},{10,11... | collective-permute-start | bytes 1622024 | tf_op jit(solution)/shard_map/ppermute | solution.py:286
  139.5 0.9 copy-start.12
  201.7 25.7 %collective-permute-start.12 = (bf16[528,512]{1,0:T(8,128)(2,1)}, bf16[528,512]{1,0:T(8,128)(2,1)S(1)}, u32[]{:S(2)}, u32[]{:S(2)}) collective-permute-start(bf16[528,512]{1,0:T(8,128)(2,1)} %get-tuple-element.53), channel_id=1, source_target_pairs={{0,1},{1,0},{2,3},{3,2},{4,5},{5,4},{6,7},{7,6},{8,9},{9,8},{10,11... | collective-permute-start | bytes 1622024 | tf_op jit(solution)/shard_map/ppermute | solution.py:286
  203.2 0.9 copy-start.13
  218.0 1.0 copy-start.6
  225.9 13.6 %collective-permute-start.14 = (bf16[528,512]{1,0:T(8,128)(2,1)}, bf16[528,512]{1,0:T(8,128)(2,1)S(1)}, u32[]{:S(2)}, u32[]{:S(2)}) collective-permute-start(bf16[528,512]{1,0:T(8,128)(2,1)} %get-tuple-element.56), channel_id=1, source_target_pairs={{0,1},{1,0},{2,3},{3,2},{4,5},{5,4},{6,7},{7,6},{8,9},{9,8},{10,11... | collective-permute-start | bytes 1622024 | tf_op jit(solution)/shard_map/ppermute | solution.py:286
  227.4 0.8 copy-start.11
  239.5 0.8 copy-start.14
where the time goes:
time: 245 us; the launch traced here: 244 us
  Pallas kernels  125 us (51%)
  waiting for transfers between devices  73 us (30%)
  starting transfers between devices  19.2 us (8%)
  local copies, waits for them, and re-layouts  12.4 us (5%)
  blocking collectives  10.6 us (4%)
  other arithmetic  2.78 us (1%)
    ppermute x7, waiting for transfers between devices, per_device(): picked = lax.ppermute(picked, 'req', [(i, i ^ m) for i in range(count)])  63.9 us
    pallas_call x8, Pallas kernels, attend(): pl.pallas_call(lambda *refs: attend_kernel(tile, m, *refs), grid_spec=plt...  55.8 us
    pallas_call x8, Pallas kernels, finish(): pl.pallas_call(lambda *refs: finish_kernel(m, 1 + len(peers), *refs), gri...  26.2 us
    pallas_call x8, Pallas kernels, pick(): pl.pallas_call(pick_kernel, grid_spec=pltpu.PrefetchScalarGridSpec(num_sc...  24.2 us
    pallas_call x1, Pallas kernels, project(): pl.pallas_call(project_kernel, grid=(rows // tile,), in_specs=[pl.BlockSp...  18.5 us
    unnamed x1, blocking collectives  10.6 us
    ppermute x8, starting transfers between devices, per_device(): lax.ppermute(peer, 'head', [(i, (i + k) % ways) for i in range(ways)])  10 us
    ppermute x7, starting transfers between devices, per_device(): picked = lax.ppermute(picked, 'req', [(i, i ^ m) for i in range(count)])  9.22 us
  transfers between devices with their start and end apart: 15, of which 5 were waited for; matrix products, arithmetic and copies ran while one was open for 2% of the time, Pallas kernels for 49%

commit v1 on v0

--- a/solution.py
+++ b/solution.py
@@ -11,7 +11,7 @@
 BLOCK = 128
 MOSTC = 512
 EPSILON = 1e-05
-VMEM_LIMIT = 58 * 1024 * 1024
+VMEM_LIMIT = 24000 * 1024
 
 
 def silu_half(y):
@@ -71,84 +71,88 @@
     )(candidates, w_in)
 
 
-def attend_kernel(tile, m, place, infos, q_ref, g_ref, self_ref, kv_ref, w_ref, own_ref, *rest):
+def window_rows(m, offset, tile):
+    def index(i, place, infos):
+        first = infos[0, jnp.bitwise_xor(place[0], m)]
+        return pl.multiple_of(first + offset + i * tile, 16), 0
+
+    return index
+
+
+def attend_kernel(m, offset, place, infos, q_ref, g_ref, self_ref, kv_ref, w_ref, own_ref, *rest):
     peer_refs, gated = rest[:-1], rest[-1]
-    window, width = q_ref.shape
+    tile, width = q_ref.shape
     heads = width // HD
     tokens = kv_ref.shape[1]
     columns = own_ref.shape[1]
     scale = 1.0 / math.sqrt(HD)
     who = jnp.bitwise_xor(place[0], m)
-    first, start, end = infos[0, who], infos[1, who], infos[2, who]
+    low = infos[0, who] + offset + pl.program_id(0) * tile
     live = lax.broadcasted_iota(jnp.int32, (1, tokens), 1) < infos[3, who]
 
-    def one_tile(t):
-        rows = slice(t * tile, (t + 1) * tile)
+    @pl.when(jnp.logical_and(low < infos[2, who], low + tile > infos[1, who]))
+    def _():
         for h in range(heads):
             cols = slice(h * HD, (h + 1) * HD)
             keys = kv_ref[0, :, 2 * h * HD : (2 * h + 1) * HD]
             values = kv_ref[0, :, (2 * h + 1) * HD : (2 * h + 2) * HD]
             scores = lax.dot_general(
-                q_ref[rows, cols], keys, (((1,), (1,)), ((), ())), preferred_element_type=jnp.float32
+                q_ref[:, cols], keys, (((1,), (1,)), ((), ())), preferred_element_type=jnp.float32
             )
             weights = silu_half(scores * (0.5 * scale))
             weights = jnp.where(live, weights, 0.0).astype(jnp.bfloat16)
             mixed = jnp.dot(weights, values, preferred_element_type=jnp.float32)
-            normed = normalize(self_ref[rows, cols] + mixed)
-            gated[rows, cols] = (normed * g_ref[rows, cols].astype(jnp.float32)).astype(jnp.bfloat16)
-        partial = jnp.dot(gated[rows, :], w_ref[...], preferred_element_type=jnp.float32)
-        own_ref[rows, :] = partial[:, :columns]
+            normed = normalize(self_ref[:, cols] + mixed)
+            gated[:, cols] = (normed * g_ref[:, cols].astype(jnp.float32)).astype(jnp.bfloat16)
+        partial = jnp.dot(gated[...], w_ref[...], preferred_element_type=jnp.float32)
+        own_ref[...] = partial[:, :columns]
         for k, peer_ref in enumerate(peer_refs, 1):
-            peer_ref[rows, :] = partial[:, k * columns : (k + 1) * columns].astype(jnp.bfloat16)
-
-    for t in range(window // tile):
-        low = first + t * tile
-        pl.when(jnp.logical_and(low < end, low + tile > start))(lambda t=t: one_tile(t))
-
-
-def attend(place, infos, m, queries, gates, selfs, cached, w_turned, window, ways):
+            peer_ref[...] = partial[:, k * columns : (k + 1) * columns].astype(jnp.bfloat16)
+
+
+def attend(place, infos, m, offset, size, tile, queries, gates, selfs, cached, w_turned, ways):
     width = queries.shape[1]
     columns = w_turned.shape[1] // ways
     tokens, kvw = cached.shape[1:]
-    tile = window // 3 if window % 48 == 0 else window
-    rows = lambda i, place, infos: (
-        pl.multiple_of(infos[0, jnp.bitwise_xor(place[0], m)], 16),
-        0,
-    )
-    view = pl.BlockSpec((pl.Element(window), pl.Element(width)), rows)
-    whole = pl.BlockSpec((window, columns), lambda i, place, infos: (0, 0))
+    view = pl.BlockSpec((pl.Element(tile), pl.Element(width)), window_rows(m, offset, tile))
+    part = pl.BlockSpec((tile, columns), lambda i, place, infos: (i, 0))
     return pl.pallas_call(
-        lambda *refs: attend_kernel(tile, m, *refs),
+        lambda *refs: attend_kernel(m, offset, *refs),
         grid_spec=pltpu.PrefetchScalarGridSpec(
             num_scalar_prefetch=2,
-            grid=(1,),
+            grid=(size // tile,),
             in_specs=[
                 view,
                 view,
                 view,
-                pl.BlockSpec((1, tokens, kvw), lambda i, place, infos: (0, 0, 0)),
-                pl.BlockSpec(w_turned.shape, lambda i, place, infos: (0, 0)),
+                pl.BlockSpec(
+                    (1, tokens, kvw), lambda i, place, infos: (0, 0, 0), pipeline_mode=pl.Buffered(1)
+                ),
+                pl.BlockSpec(
+                    w_turned.shape, lambda i, place, infos: (0, 0), pipeline_mode=pl.Buffered(1)
+                ),
             ],
-            out_specs=[whole] * ways,
-            scratch_shapes=[pltpu.VMEM((window, width), jnp.bfloat16)],
-        ),
-        out_shape=[jax.ShapeDtypeStruct((window, columns), jnp.float32)]
-        + [jax.ShapeDtypeStruct((window, columns), jnp.bfloat16)] * (ways - 1),
+            out_specs=[part] * ways,
+            scratch_shapes=[pltpu.VMEM((tile, width), jnp.bfloat16)],
+        ),
+        out_shape=[jax.ShapeDtypeStruct((size, columns), jnp.float32)]
+        + [jax.ShapeDtypeStruct((size, columns), jnp.bfloat16)] * (ways - 1),
         cost_estimate=pl.CostEstimate(
-            flops=4 * window * tokens * width + 2 * window * width * ways * columns,
-            bytes_accessed=8 * window * width + 2 * tokens * kvw + 6 * window * ways * columns,
-            transcendentals=window * tokens * width // HD,
+            flops=4 * size * tokens * width + 2 * size * width * ways * columns,
+            bytes_accessed=8 * size * width + 2 * tokens * kvw + 6 * size * ways * columns,
+            transcendentals=size * tokens * width // HD,
         ),
         compiler_params=pltpu.CompilerParams(vmem_limit_bytes=VMEM_LIMIT),
         name="attend",
     )(place, infos, queries, gates, selfs, cached, w_turned)
 
 
-def finish_kernel(m, ways, place, infos, total_ref, own_ref, *rest):
+def finish_kernel(m, offset, ways, place, infos, total_ref, own_ref, *rest):
     peer_refs, out_ref = rest[: ways - 1], rest[-1]
     who = jnp.bitwise_xor(place[0], m)
-    window = own_ref.shape[0]
-    position = infos[0, who] + lax.broadcasted_iota(jnp.int32, (window, 1), 0)
+    tile = own_ref.shape[0]
+    low = infos[0, who] + offset + pl.program_id(0) * tile
+    position = low + lax.broadcasted_iota(jnp.int32, (tile, 1), 0)
     mine = jnp.logical_and(position >= infos[1, who], position < infos[2, who])
     before = total_ref[...].astype(jnp.float32)
     total = own_ref[...]
@@ -157,33 +161,28 @@
     out_ref[...] = jnp.where(mine, total + before, before).astype(out_ref.dtype)
 
 
-def finish(place, infos, m, own, peers, total, after=None):
-    window, columns = own.shape
-    late = [] if after is None else [after]
-    rows = lambda i, place, infos: (
-        pl.multiple_of(infos[0, jnp.bitwise_xor(place[0], m)], 16),
-        0,
-    )
-    view = pl.BlockSpec((pl.Element(window), pl.Element(columns)), rows)
-    whole = pl.BlockSpec((window, columns), lambda i, place, infos: (0, 0))
+def finish(place, infos, m, offset, tile, own, peers, total, after=()):
+    size, columns = own.shape
+    view = pl.BlockSpec((pl.Element(tile), pl.Element(columns)), window_rows(m, offset, tile))
+    part = pl.BlockSpec((tile, columns), lambda i, place, infos: (i, 0))
     return pl.pallas_call(
-        lambda *refs: finish_kernel(m, 1 + len(peers), *refs),
+        lambda *refs: finish_kernel(m, offset, 1 + len(peers), *refs),
         grid_spec=pltpu.PrefetchScalarGridSpec(
             num_scalar_prefetch=2,
-            grid=(1,),
+            grid=(size // tile,),
             in_specs=[view]
-            + [whole] * (1 + len(peers))
-            + [pl.BlockSpec(memory_space=pl.ANY)] * len(late),
+            + [part] * (1 + len(peers))
+            + [pl.BlockSpec(memory_space=pl.ANY)] * len(after),
             out_specs=view,
         ),
         out_shape=jax.ShapeDtypeStruct(total.shape, total.dtype),
         input_output_aliases={2: 0},
         cost_estimate=pl.CostEstimate(
-            flops=3 * window * columns, bytes_accessed=10 * window * columns, transcendentals=0
+            flops=3 * size * columns, bytes_accessed=10 * size * columns, transcendentals=0
         ),
         compiler_params=pltpu.CompilerParams(vmem_limit_bytes=VMEM_LIMIT),
         name="finish",
-    )(place, infos, total, own, *peers, *late)
+    )(place, infos, total, own, *peers, *after)
 
 
 def pick_kernel(place, table, kv_ref, *rest):
@@ -191,17 +190,18 @@
 
 
 def pick(place, table, kv_cache, m, after):
-    user = lambda i, place, table: (table[jnp.bitwise_xor(place[0], m), place[0]], 0, 0)
-    block = (1,) + kv_cache.shape[1:]
+    user = lambda i, place, table: (table[jnp.bitwise_xor(place[0], m), place[0]], i, 0)
+    tokens, kvw = kv_cache.shape[1:]
+    block = (1, tokens // 4, kvw)
     return pl.pallas_call(
         pick_kernel,
         grid_spec=pltpu.PrefetchScalarGridSpec(
             num_scalar_prefetch=2,
-            grid=(1,),
+            grid=(4,),
             in_specs=[pl.BlockSpec(block, user)] + [pl.BlockSpec(memory_space=pl.ANY)] * len(after),
-            out_specs=pl.BlockSpec(block, lambda i, place, table: (0, 0, 0)),
-        ),
-        out_shape=jax.ShapeDtypeStruct(block, kv_cache.dtype),
+            out_specs=pl.BlockSpec(block, lambda i, place, table: (0, i, 0)),
+        ),
+        out_shape=jax.ShapeDtypeStruct((1, tokens, kvw), kv_cache.dtype),
         compiler_params=pltpu.CompilerParams(vmem_limit_bytes=VMEM_LIMIT),
         name="pick",
     )(place, table, kv_cache, *after)
@@ -272,25 +272,30 @@
     )
     ranked = lax.dynamic_slice_in_dim(candidates, side * columns, columns, 1)
     sequence = [0, 1] + order
+    tile = window // 3 if window % 48 == 0 else window
+    steps = [(m, 0, window) for m in sequence[:-1]]
+    steps += [(sequence[-1], offset, tile) for offset in range(0, window, tile)]
     pending = []
     ready = []
-    for m in sequence:
+    for m, offset, size in steps:
+        current = infos
         if ready:
-            table_in, *ready = lax.optimization_barrier((infos, *ready))
-        else:
-            table_in = infos
+            current, *ready = lax.optimization_barrier((infos, *ready))
         own, *peers = attend(
-            place, table_in, m, queries, gates, selfs, arrived[m], turned, window, ways
+            place, current, m, offset, size, tile, queries, gates, selfs, arrived[m], turned, ways
         )
         landed = [
             lax.ppermute(peer, "head", [(i, (i + k) % ways) for i in range(ways)])
             for k, peer in enumerate(peers, 1)
         ]
-        if pending:
-            ranked = finish(place, infos, *pending.pop(), ranked, after=own)
-        pending.append((m, own, landed))
-        ready = [own, ranked]
-    return finish(place, infos, *pending.pop(), ranked)
+        ready = [own]
+        if pending and m != sequence[-1]:
+            ranked = finish(place, infos, *pending.pop(0), ranked, after=[own])
+            ready = [own, ranked]
+        pending.append((m, offset, tile, own, landed))
+    for one in pending:
+        ranked = finish(place, infos, *one, ranked, after=ready[:1])
+    return ranked
 
 
 def solution(mesh):

time: 245 us -> 221 us (0.902)
  Pallas kernels: 125 us -> 93.1 us
  local copies, waits for them, and re-layouts: 12.4 us -> 22.8 us
  starting transfers between devices: 19.2 us -> 16.6 us
    pallas_call x16 -> x20, Pallas kernels: 82 us -> 66.1 us  [the longest x10 35 us: attend(): pl.pallas_call(lambda *refs: attend_kernel(m, offset, *refs), grid_spec=p...]
    unnamed x35 -> x43, local copies, waits for them, and re-layouts: 8.63 us -> 21 us
    pallas_call x8, Pallas kernels: 24.2 us -> 11.9 us  [pick(): pl.pallas_call(pick_kernel, grid_spec=pltpu.PrefetchScalarGridSpec(num_sc...]
    ppermute x7, starting transfers between devices: 9.22 us -> 4.82 us  [per_device(): picked = lax.ppermute(picked, 'req', [(i, i ^ m) for i in range(count)])]
    pallas_call x1, Pallas kernels: 18.5 us -> 15.1 us  [project(): pl.pallas_call(project_kernel, grid=(rows // tile,), in_specs=[pl.BlockSp...]
    ppermute x7, waiting for transfers between devices: 63.9 us -> 66.7 us  [per_device(): picked = lax.ppermute(picked, 'req', [(i, i ^ m) for i in range(count)])]
    ppermute x8 -> x10, starting transfers between devices: 10 us -> 11.8 us  [per_device(): lax.ppermute(peer, 'head', [(i, (i + k) % ways) for i in range(ways)])]
    ppermute x8 -> x10, waiting for transfers between devices: 9.08 us -> 8.07 us  [per_device(): lax.ppermute(peer, 'head', [(i, (i + k) % ways) for i in range(ways)])]
  transfers between devices with their start and end apart: 15 -> 17, of which waited for: 5 -> 6; matrix products, arithmetic and copies ran while one was open for 2% -> 1% of each run, Pallas kernels for 49% -> 40%
where the time goes in v1:
time: 221 us; the launch traced here: 220 us
  Pallas kernels  93.1 us (42%)
  waiting for transfers between devices  74.8 us (34%)
  local copies, waits for them, and re-layouts  22.8 us (10%)
  starting transfers between devices  16.6 us (8%)
  blocking collectives  10.6 us (5%)
    ppermute x7, waiting for transfers between devices, per_device(): picked = lax.ppermute(picked, 'req', [(i, i ^ m) for i in range(count)])  66.7 us
    pallas_call x10, Pallas kernels, attend(): pl.pallas_call(lambda *refs: attend_kernel(m, offset, *refs), grid_spec=p...  35 us
    pallas_call x10, Pallas kernels, finish(): pl.pallas_call(lambda *refs: finish_kernel(m, offset, 1 + len(peers), *re...  31.1 us
    unnamed x43, local copies, waits for them, and re-layouts  21 us
    pallas_call x1, Pallas kernels, project(): pl.pallas_call(project_kernel, grid=(rows // tile,), in_specs=[pl.BlockSp...  15.1 us
    pallas_call x8, Pallas kernels, pick(): pl.pallas_call(pick_kernel, grid_spec=pltpu.PrefetchScalarGridSpec(num_sc...  11.9 us
    ppermute x10, starting transfers between devices, per_device(): lax.ppermute(peer, 'head', [(i, (i + k) % ways) for i in range(ways)])  11.8 us
    unnamed x1, blocking collectives  10.6 us
  transfers between devices with their start and end apart: 17, of which 6 were waited for; matrix products, arithmetic and copies ran while one was open for 1% of the time, Pallas kernels for 40%

profile of v1, /device:TPU:0, one launch (start us, length us, event | category | flops | bytes accessed | tf_op | source)
XLA Modules:
  0.0 219.9 jit_solution(15987597860250833273)
XLA Ops:
  0.0 1.2 dynamic-slice
  1.9 0.8 select_reduce_fusion
  3.0 10.6 %all-reduce = s32[64]{0:T(128)S(1)} all-reduce(s32[64]{0:T(128)S(1)} %dynamic-update-slice), channel_id=2, replica_groups=mesh['groups'=2,'req'=8,'head'=2,'rep'=1] {'req'}, use_global_device_ids=true, to_apply=%add | all-reduce | flops 64 | bytes 512
  13.7 3.4 %copy-done = bf16[8,512,1024]{2,1,0:T(8,128)(2,1)S(1)} copy-done((bf16[8,512,1024]{2,1,0:T(8,128)(2,1)S(1)}, bf16[8,512,1024]{2,1,0:T(8,128)(2,1)}, u32[]{:S(2)}) %copy-start) | copy-done | bytes 8388632
  17.1 2.2 pick.8.rest_0_
  19.3 2.2 %pick.9.rest_0_ = bf16[1,512,1024]{2,1,0:T(8,128)(2,1)} custom-call(s32[1]{0:T(128)} %bitcast.place.refs_0_, s32[8,8]{1,0:T(8,128)S(1)} %reshape.87.table, bf16[8,512,1024]{2,1,0:T(8,128)(2,1)S(1)} %copy-done, bf16[1,512,1024]{2,1,0:T(8,128)(2,1)} %pick.8.rest_0_), custom_call_target="tpu_custom_call" | custom-call | tf_op jit(solution)/shard_map/pick/pallas_call | solution.py:196
  22.1 2.2 %pick.10.rest_0_ = bf16[1,512,1024]{2,1,0:T(8,128)(2,1)} custom-call(s32[1]{0:T(128)} %bitcast.place.refs_0_, s32[8,8]{1,0:T(8,128)S(1)} %reshape.87.table, bf16[8,512,1024]{2,1,0:T(8,128)(2,1)S(1)} %copy-done, bf16[1,512,1024]{2,1,0:T(8,128)(2,1)} %pick.9.rest_0_), custom_call_target="tpu_custom_call" | custom-call | tf_op jit(solution)/shard_map/pick/pallas_call | solution.py:196
  25.9 1.0 copy-done.11
  27.7 1.0 copy-done.9
  28.6 2.2 pick.14.rest_0_
  31.2 2.2 copy-done.15
  33.4 2.2 copy-done.17
  35.5 15.1 %project.1 = (bf16[2048,512]{1,0:T(8,128)(2,1)S(1)}, bf16[2048,512]{1,0:T(8,128)(2,1)S(1)}, f32[2048,512]{1,0:T(8,128)S(1)}) custom-call(bf16[2048,1024]{1,0:T(8,128)(2,1)S(1)} %copy-done.15, bf16[1024,2048]{1,0:T(8,128)(2,1)S(1)} %copy-done.17), custom_call_target="tpu_custom_call" | custom-call | flops 8589934592 | bytes 16777216 | tf_op jit(solution)/shard_map/project/pallas_call | solution.py:51
  51.7 4.5 %copy-done.1 = bf16[8,512,1024]{2,1,0:T(8,128)(2,1)S(1)} copy-done((bf16[8,512,1024]{2,1,0:T(8,128)(2,1)S(1)}, bf16[8,512,1024]{2,1,0:T(8,128)(2,1)}, u32[]{:S(2)}) %copy-start.1) | copy-done | bytes 8388632
  57.0 5.6 %attend.10 = (f32[528,512]{1,0:T(8,128)S(1)}, bf16[528,512]{1,0:T(8,128)(2,1)}) custom-call(s32[1]{0:T(128)} %bitcast.place.refs_0_, s32[4,8]{1,0:T(4,128)S(1)} %pad_add_fusion.refs_1_, bf16[2048,512]{1,0:T(8,128)(2,1)S(1)} %get-tuple-element.37.refs_2_, bf16[2048,512]{1,0:T(8,128)(2,1)S(1)} %get-tuple-element.38.refs_3_, ...), custom_call_target="tpu_custom_call" | custom-call | flops 1107296256 | bytes 6455296 | tf_op jit(solution)/shard_map/attend/pallas_call | solution.py:119
  62.6 1.0 copy-done.13
  63.5 1.5 collective-permute-start
  65.8 2.2 copy-done.3
  68.0 1.6 copy-done.5
  69.6 5.0 %attend.11 = (f32[528,512]{1,0:T(8,128)S(1)}, bf16[528,512]{1,0:T(8,128)(2,1)S(1)}) custom-call(s32[1]{0:T(128)} %bitcast.place.refs_0_, s32[4,8]{1,0:T(4,128)S(1)} %pad_add_fusion.refs_1_, bf16[2048,512]{1,0:T(8,128)(2,1)S(1)} %get-tuple-element.37.refs_2_, bf16[2048,512]{1,0:T(8,128)(2,1)S(1)} %copy-done.5, f32[2048,512]{1,0:T(8,128)S(1)} %copy-done.3, ...), custom_call_target="tpu_custom_call" | custom-call | flops 1107296256 | bytes 6455296 | tf_op jit(solution)/shard_map/attend/pallas_call | solution.py:119
  75.2 1.6 constant_dynamic-slice_fusion.2.refs_2_
  76.8 2.4 %collective-permute-start.9 = (bf16[1,512,1024]{2,1,0:T(8,128)(2,1)S(1)}, bf16[1,512,1024]{2,1,0:T(8,128)(2,1)S(1)}, u32[]{:S(2)}, u32[]{:S(2)}) collective-permute-start(bf16[1,512,1024]{2,1,0:T(8,128)(2,1)S(1)} %copy-done.12), channel_id=1, source_target_pairs={{0,4},{2,6},{4,0},{6,2},{8,12},{10,14},{12,8},{14,10},{1,5},{3,7},... | collective-permute-start | bytes 3145736 | tf_op jit(solution)/shard_map/ppermute | solution.py:252
  79.2 3.7 %finish.10.refs_2_ = bf16[2048,512]{1,0:T(8,128)(2,1)} custom-call(s32[1]{0:T(128)} %bitcast.place.refs_0_, s32[4,8]{1,0:T(4,128)S(1)} %pad_add_fusion.refs_1_, bf16[2048,512]{1,0:T(8,128)(2,1)} %constant_dynamic-slice_fusion.2.refs_2_, f32[528,512]{1,0:T(8,128)S(1)} %copy-done.14, ...), custom_call_target="tpu_custom_call", output_to_operand_aliasing={{}: (2, {})} | custom-call | flops 811008 | bytes 2703360 | tf_op jit(solution)/shard_map/finish/pallas_call | solution.py:168
  82.9 4.7 %attend.12 = (f32[528,512]{1,0:T(8,128)S(1)}, bf16[528,512]{1,0:T(8,128)(2,1)S(1)}) custom-call(s32[1]{0:T(128)} %bitcast.place.refs_0_, s32[4,8]{1,0:T(4,128)S(1)} %pad_add_fusion.refs_1_, bf16[2048,512]{1,0:T(8,128)(2,1)S(1)} %get-tuple-element.37.refs_2_, bf16[2048,512]{1,0:T(8,128)(2,1)S(1)} %copy-done.6, f32[2048,512]{1,0:T(8,128)S(1)} %copy-done.3, ...), custom_call_target="tpu_custom_call" | custom-call | flops 1107296256 | bytes 6455296 | tf_op jit(solution)/shard_map/attend/pallas_call | solution.py:119
  87.6 2.5 %collective-permute-start.4 = (bf16[528,512]{1,0:T(8,128)(2,1)S(1)}, bf16[528,512]{1,0:T(8,128)(2,1)S(1)}, u32[]{:S(2)}, u32[]{:S(2)}) collective-permute-start(bf16[528,512]{1,0:T(8,128)(2,1)S(1)} %get-tuple-element.47), channel_id=1, source_target_pairs={{0,1},{1,0},{2,3},{3,2},{4,5},{5,4},{6,7},{7,6},{8,9},{9,8},{10,11... | collective-permute-start | bytes 1622024 | tf_op jit(solution)/shard_map/ppermute | solution.py:288
  90.8 3.4 %finish.11.refs_2_ = bf16[2048,512]{1,0:T(8,128)(2,1)} custom-call(s32[1]{0:T(128)} %bitcast.place.refs_0_, s32[4,8]{1,0:T(4,128)S(1)} %pad_add_fusion.refs_1_, bf16[2048,512]{1,0:T(8,128)(2,1)} %finish.10.refs_2_, f32[528,512]{1,0:T(8,128)S(1)} %get-tuple-element.43.refs_5_.refs_3_, ...), custom_call_target="tpu_custom_call", output_to_operand_aliasing={{}: (2, {})} | custom-call | flops 811008 | bytes 2703360 | tf_op jit(solution)/shard_map/finish/pallas_call | solution.py:168
  94.3 3.3 %attend.13 = (f32[528,512]{1,0:T(8,128)S(1)}, bf16[528,512]{1,0:T(8,128)(2,1)S(1)}) custom-call(s32[1]{0:T(128)} %bitcast.place.refs_0_, s32[4,8]{1,0:T(4,128)S(1)} %pad_add_fusion.refs_1_, bf16[2048,512]{1,0:T(8,128)(2,1)S(1)} %get-tuple-element.37.refs_2_, bf16[2048,512]{1,0:T(8,128)(2,1)S(1)} %copy-done.6, f32[2048,512]{1,0:T(8,128)S(1)} %copy-done.3, ...), custom_call_target="tpu_custom_call" | custom-call | flops 1107296256 | bytes 6455296 | tf_op jit(solution)/shard_map/attend/pallas_call | solution.py:119
  98.2 4.1 %collective-permute-done.4.refs_4_ = bf16[528,512]{1,0:T(8,128)(2,1)S(1)} collective-permute-done((bf16[528,512]{1,0:T(8,128)(2,1)S(1)}, bf16[528,512]{1,0:T(8,128)(2,1)S(1)}, u32[]{:S(2)}, u32[]{:S(2)}) %collective-permute-start.4) | collective-permute-done | bytes 540704 | tf_op jit(solution)/shard_map/ppermute | solution.py:288
  102.3 3.4 %finish.12.refs_2_ = bf16[2048,512]{1,0:T(8,128)(2,1)} custom-call(s32[1]{0:T(128)} %bitcast.place.refs_0_, s32[4,8]{1,0:T(4,128)S(1)} %pad_add_fusion.refs_1_, bf16[2048,512]{1,0:T(8,128)(2,1)} %finish.11.refs_2_, f32[528,512]{1,0:T(8,128)S(1)} %get-tuple-element.46.refs_5_.refs_3_, ...), custom_call_target="tpu_custom_call", output_to_operand_aliasing={{}: (2, {})} | custom-call | flops 811008 | bytes 2703360 | tf_op jit(solution)/shard_map/finish/pallas_call | solution.py:168
  105.7 3.3 %attend.14 = (f32[528,512]{1,0:T(8,128)S(1)}, bf16[528,512]{1,0:T(8,128)(2,1)S(1)}) custom-call(s32[1]{0:T(128)} %bitcast.place.refs_0_, s32[4,8]{1,0:T(4,128)S(1)} %pad_add_fusion.refs_1_, bf16[2048,512]{1,0:T(8,128)(2,1)S(1)} %get-tuple-element.37.refs_2_, bf16[2048,512]{1,0:T(8,128)(2,1)S(1)} %copy-done.6, f32[2048,512]{1,0:T(8,128)S(1)} %copy-done.3, ...), custom_call_target="tpu_custom_call" | custom-call | flops 1107296256 | bytes 6455296 | tf_op jit(solution)/shard_map/attend/pallas_call | solution.py:119
  109.0 1.6 collective-permute-start.8
  110.6 2.3 %collective-permute-done.6.refs_4_ = bf16[528,512]{1,0:T(8,128)(2,1)S(1)} collective-permute-done((bf16[528,512]{1,0:T(8,128)(2,1)S(1)}, bf16[528,512]{1,0:T(8,128)(2,1)S(1)}, u32[]{:S(2)}, u32[]{:S(2)}) %collective-permute-start.6) | collective-permute-done | bytes 540704 | tf_op jit(solution)/shard_map/ppermute | solution.py:288
  112.9 3.4 %finish.13.refs_2_ = bf16[2048,512]{1,0:T(8,128)(2,1)} custom-call(s32[1]{0:T(128)} %bitcast.place.refs_0_, s32[4,8]{1,0:T(4,128)S(1)} %pad_add_fusion.refs_1_, bf16[2048,512]{1,0:T(8,128)(2,1)} %finish.12.refs_2_, f32[528,512]{1,0:T(8,128)S(1)} %get-tuple-element.49.refs_5_.refs_3_, ...), custom_call_target="tpu_custom_call", output_to_operand_aliasing={{}: (2, {})} | custom-call | flops 811008 | bytes 2703360 | tf_op jit(solution)/shard_map/finish/pallas_call | solution.py:168
  116.3 4.9 %attend.15 = (f32[528,512]{1,0:T(8,128)S(1)}, bf16[528,512]{1,0:T(8,128)(2,1)S(1)}) custom-call(s32[1]{0:T(128)} %bitcast.place.refs_0_, s32[4,8]{1,0:T(4,128)S(1)} %pad_add_fusion.refs_1_, bf16[2048,512]{1,0:T(8,128)(2,1)S(1)} %get-tuple-element.37.refs_2_, bf16[2048,512]{1,0:T(8,128)(2,1)S(1)} %copy-done.6, f32[2048,512]{1,0:T(8,128)S(1)} %copy-done.3, ...), custom_call_target="tpu_custom_call" | custom-call | flops 1107296256 | bytes 6455296 | tf_op jit(solution)/shard_map/attend/pallas_call | solution.py:119
  121.2 1.6 collective-permute-start.10
  122.8 1.7 collective-permute-done.8.refs_4_
  124.4 3.4 %finish.14.refs_2_ = bf16[2048,512]{1,0:T(8,128)(2,1)} custom-call(s32[1]{0:T(128)} %bitcast.place.refs_0_, s32[4,8]{1,0:T(4,128)S(1)} %pad_add_fusion.refs_1_, bf16[2048,512]{1,0:T(8,128)(2,1)} %finish.13.refs_2_, f32[528,512]{1,0:T(8,128)S(1)} %get-tuple-element.52.refs_5_.refs_3_, ...), custom_call_target="tpu_custom_call", output_to_operand_aliasing={{}: (2, {})} | custom-call | flops 811008 | bytes 2703360 | tf_op jit(solution)/shard_map/finish/pallas_call | solution.py:168
  127.9 50.5 %collective-permute-done.11.refs_5_ = bf16[1,512,1024]{2,1,0:T(8,128)(2,1)S(1)} collective-permute-done((bf16[1,512,1024]{2,1,0:T(8,128)(2,1)S(1)}, bf16[1,512,1024]{2,1,0:T(8,128)(2,1)S(1)}, u32[]{:S(2)}, u32[]{:S(2)}) %collective-permute-start.11) | collective-permute-done | bytes 1048608 | tf_op jit(solution)/shard_map/ppermute | solution.py:252
  178.4 3.7 %attend.16 = (f32[528,512]{1,0:T(8,128)S(1)}, bf16[528,512]{1,0:T(8,128)(2,1)S(1)}) custom-call(s32[1]{0:T(128)} %bitcast.place.refs_0_, s32[4,8]{1,0:T(4,128)S(1)} %pad_add_fusion.refs_1_, bf16[2048,512]{1,0:T(8,128)(2,1)S(1)} %get-tuple-element.37.refs_2_, bf16[2048,512]{1,0:T(8,128)(2,1)S(1)} %copy-done.6, f32[2048,512]{1,0:T(8,128)S(1)} %copy-done.3, ...), custom_call_target="tpu_custom_call" | custom-call | flops 1107296256 | bytes 6455296 | tf_op jit(solution)/shard_map/attend/pallas_call | solution.py:119
  182.7 3.4 %finish.15.refs_2_ = bf16[2048,512]{1,0:T(8,128)(2,1)} custom-call(s32[1]{0:T(128)} %bitcast.place.refs_0_, s32[4,8]{1,0:T(4,128)S(1)} %pad_add_fusion.refs_1_, bf16[2048,512]{1,0:T(8,128)(2,1)} %finish.14.refs_2_, f32[528,512]{1,0:T(8,128)S(1)} %get-tuple-element.55.refs_5_.refs_3_, ...), custom_call_target="tpu_custom_call", output_to_operand_aliasing={{}: (2, {})} | custom-call | flops 811008 | bytes 2703360 | tf_op jit(solution)/shard_map/finish/pallas_call | solution.py:168
  186.2 16.2 %collective-permute-done.13.refs_5_ = bf16[1,512,1024]{2,1,0:T(8,128)(2,1)S(1)} collective-permute-done((bf16[1,512,1024]{2,1,0:T(8,128)(2,1)S(1)}, bf16[1,512,1024]{2,1,0:T(8,128)(2,1)S(1)}, u32[]{:S(2)}, u32[]{:S(2)}) %collective-permute-start.13) | collective-permute-done | bytes 1048608 | tf_op jit(solution)/shard_map/ppermute | solution.py:252
  202.3 2.0 attend.17
  205.0 2.0 attend.18
  206.9 1.5 collective-permute-start.15
  209.7 3.4 %finish.16.refs_2_ = bf16[2048,512]{1,0:T(8,128)(2,1)} custom-call(s32[1]{0:T(128)} %bitcast.place.refs_0_, s32[4,8]{1,0:T(4,128)S(1)} %pad_add_fusion.refs_1_, bf16[2048,512]{1,0:T(8,128)(2,1)} %finish.15.refs_2_, f32[528,512]{1,0:T(8,128)S(1)} %get-tuple-element.58.refs_5_.refs_3_, ...), custom_call_target="tpu_custom_call", output_to_operand_aliasing={{}: (2, {})} | custom-call | flops 811008 | bytes 2703360 | tf_op jit(solution)/shard_map/finish/pallas_call | solution.py:168
  213.2 2.3 %finish.17.refs_2_ = bf16[2048,512]{1,0:T(8,128)(2,1)} custom-call(s32[1]{0:T(128)} %bitcast.place.refs_0_, s32[4,8]{1,0:T(4,128)S(1)} %pad_add_fusion.refs_1_, bf16[2048,512]{1,0:T(8,128)(2,1)} %finish.16.refs_2_, f32[176,512]{1,0:T(8,128)S(1)} %get-tuple-element.61.refs_3_, ...), custom_call_target="tpu_custom_call", output_to_operand_aliasing={{}: (2, {})} | custom-call | flops 270336 | bytes 901120 | tf_op jit(solution)/shard_map/finish/pallas_call | solution.py:168
  215.4 2.3 %finish.18.refs_2_ = bf16[2048,512]{1,0:T(8,128)(2,1)} custom-call(s32[1]{0:T(128)} %bitcast.place.refs_0_, s32[4,8]{1,0:T(4,128)S(1)} %pad_add_fusion.refs_1_, bf16[2048,512]{1,0:T(8,128)(2,1)} %finish.17.refs_2_, f32[176,512]{1,0:T(8,128)S(1)} %get-tuple-element.63.refs_3_, ...), custom_call_target="tpu_custom_call", output_to_operand_aliasing={{}: (2, {})} | custom-call | flops 270336 | bytes 901120 | tf_op jit(solution)/shard_map/finish/pallas_call | solution.py:168
  217.7 2.3 %finish.19 = bf16[2048,512]{1,0:T(8,128)(2,1)} custom-call(s32[1]{0:T(128)} %bitcast.place.refs_0_, s32[4,8]{1,0:T(4,128)S(1)} %pad_add_fusion.refs_1_, bf16[2048,512]{1,0:T(8,128)(2,1)} %finish.18.refs_2_, f32[176,512]{1,0:T(8,128)S(1)} %get-tuple-element.65.refs_5_.refs_3_, ...), custom_call_target="tpu_custom_call", output_to_operand_aliasing={{}: (2, {})} | custom-call | flops 270336 | bytes 901120 | tf_op jit(solution)/shard_map/finish/pallas_call | solution.py:168
  (68 shorter events, 10.6 us)
Async XLA Ops:
  13.7 3.4 %copy-start = (bf16[8,512,1024]{2,1,0:T(8,128)(2,1)S(1)}, bf16[8,512,1024]{2,1,0:T(8,128)(2,1)}, u32[]{:S(2)}) copy-start(bf16[8,512,1024]{2,1,0:T(8,128)(2,1)} %kv_ref.15) | copy-start | bytes 25165828
  19.3 63.6 %collective-permute-start.3 = (bf16[1,512,1024]{2,1,0:T(8,128)(2,1)}, bf16[1,512,1024]{2,1,0:T(8,128)(2,1)}, u32[]{:S(2)}, u32[]{:S(2)}) collective-permute-start(bf16[1,512,1024]{2,1,0:T(8,128)(2,1)} %pick.8.rest_0_), channel_id=1, source_target_pairs={{0,14},{2,12},{4,10},{6,8},{8,6},{10,4},{12,2},{14,0},{1,15},{3,13... | collective-permute-start | bytes 3145736 | tf_op jit(solution)/shard_map/ppermute | solution.py:252
  21.5 72.8 %collective-permute-start.5 = (bf16[1,512,1024]{2,1,0:T(8,128)(2,1)}, bf16[1,512,1024]{2,1,0:T(8,128)(2,1)}, u32[]{:S(2)}, u32[]{:S(2)}) collective-permute-start(bf16[1,512,1024]{2,1,0:T(8,128)(2,1)} %pick.9.rest_0_), channel_id=1, source_target_pairs={{0,6},{2,4},{4,2},{6,0},{8,14},{10,12},{12,10},{14,8},{1,7},{3,5},... | collective-permute-start | bytes 3145736 | tf_op jit(solution)/shard_map/ppermute | solution.py:252
  25.9 1.0 copy-start.11
  27.6 1.0 copy-start.9
  28.6 2.2 copy-start.7
  30.8 35.0 %collective-permute-start.1 = (bf16[1,512,1024]{2,1,0:T(8,128)(2,1)}, bf16[1,512,1024]{2,1,0:T(8,128)(2,1)}, u32[]{:S(2)}, u32[]{:S(2)}) collective-permute-start(bf16[1,512,1024]{2,1,0:T(8,128)(2,1)} %pick.14.rest_0_), channel_id=1, source_target_pairs={{0,2},{2,0},{4,6},{6,4},{8,10},{10,8},{12,14},{14,12},{1,3},{3,1},... | collective-permute-start | bytes 3145736 | tf_op jit(solution)/shard_map/ppermute | solution.py:252
  31.2 2.2 copy-start.15
  33.4 2.2 copy-start.17
  35.5 15.1 %copy-start.18 = (bf16[512,1024]{1,0:T(8,128)(2,1)S(1)}, bf16[512,1024]{1,0:T(8,128)(2,1)}, u32[]{:S(2)}) copy-start(bf16[512,1024]{1,0:T(8,128)(2,1)} %param.15) | copy-start | bytes 3145732
  50.6 6.3 %copy-start.2 = (f32[2048,512]{1,0:T(8,128)}, f32[2048,512]{1,0:T(8,128)S(1)}, u32[]{:S(2)}) copy-start(f32[2048,512]{1,0:T(8,128)S(1)} %get-tuple-element.39.refs_4_) | copy-start | bytes 12582916
  50.7 6.3 %copy-start.4 = (bf16[2048,512]{1,0:T(8,128)(2,1)}, bf16[2048,512]{1,0:T(8,128)(2,1)S(1)}, u32[]{:S(2)}) copy-start(bf16[2048,512]{1,0:T(8,128)(2,1)S(1)} %get-tuple-element.38.refs_3_) | copy-start | bytes 6291460
  50.7 0.7 copy-start.19
  51.6 4.5 %copy-start.1 = (bf16[8,512,1024]{2,1,0:T(8,128)(2,1)S(1)}, bf16[8,512,1024]{2,1,0:T(8,128)(2,1)}, u32[]{:S(2)}) copy-start(bf16[8,512,1024]{2,1,0:T(8,128)(2,1)} %kv_ref.15) | copy-start | bytes 25165828
  62.6 1.0 copy-start.13
  63.5 13.3 %collective-permute-start = (bf16[528,512]{1,0:T(8,128)(2,1)}, bf16[528,512]{1,0:T(8,128)(2,1)}, u32[]{:S(2)}, u32[]{:S(2)}) collective-permute-start(bf16[528,512]{1,0:T(8,128)(2,1)} %get-tuple-element.41), channel_id=1, source_target_pairs={{0,1},{1,0},{2,3},{3,2},{4,5},{5,4},{6,7},{7,6},{8,9},{9,8},{10,11... | collective-permute-start | bytes 1622024 | tf_op jit(solution)/shard_map/ppermute | solution.py:288
  65.1 40.7 %collective-permute-start.7 = (bf16[1,512,1024]{2,1,0:T(8,128)(2,1)}, bf16[1,512,1024]{2,1,0:T(8,128)(2,1)}, u32[]{:S(2)}, u32[]{:S(2)}) collective-permute-start(bf16[1,512,1024]{2,1,0:T(8,128)(2,1)} %pick.10.rest_0_), channel_id=1, source_target_pairs={{0,12},{2,14},{4,8},{6,10},{8,4},{10,6},{12,0},{14,2},{1,13},{3,15... | collective-permute-start | bytes 3145736 | tf_op jit(solution)/shard_map/ppermute | solution.py:252
  65.8 2.2 copy-start.3
  68.0 1.6 copy-start.5
  69.6 5.6 %copy-start.16 = (bf16[2048,1024]{1,0:T(8,128)(2,1)S(1)}, bf16[2048,1024]{1,0:T(8,128)(2,1)}, u32[]{:S(2)}) copy-start(bf16[2048,1024]{1,0:T(8,128)(2,1)} %cand_ref.1) | copy-start | bytes 12582916
  74.5 2.3 %copy-start.12 = (bf16[1,512,1024]{2,1,0:T(8,128)(2,1)S(1)}, bf16[1,512,1024]{2,1,0:T(8,128)(2,1)}, u32[]{:S(2)}) copy-start(bf16[1,512,1024]{2,1,0:T(8,128)(2,1)} %copy-done.11) | copy-start | bytes 3145732
  74.6 4.6 %copy-start.14 = (f32[528,512]{1,0:T(8,128)S(1)}, f32[528,512]{1,0:T(8,128)}, u32[]{:S(2)}) copy-start(f32[528,512]{1,0:T(8,128)} %copy-done.13) | copy-start | bytes 3244036
  74.6 15.5 %collective-permute-start.2 = (bf16[528,512]{1,0:T(8,128)(2,1)S(1)}, bf16[528,512]{1,0:T(8,128)(2,1)S(1)}, u32[]{:S(2)}, u32[]{:S(2)}) collective-permute-start(bf16[528,512]{1,0:T(8,128)(2,1)S(1)} %get-tuple-element.44), channel_id=1, source_target_pairs={{0,1},{1,0},{2,3},{3,2},{4,5},{5,4},{6,7},{7,6},{8,9},{9,8},{10,11... | collective-permute-start | bytes 1622024 | tf_op jit(solution)/shard_map/ppermute | solution.py:288
  76.8 39.5 %collective-permute-start.9 = (bf16[1,512,1024]{2,1,0:T(8,128)(2,1)S(1)}, bf16[1,512,1024]{2,1,0:T(8,128)(2,1)S(1)}, u32[]{:S(2)}, u32[]{:S(2)}) collective-permute-start(bf16[1,512,1024]{2,1,0:T(8,128)(2,1)S(1)} %copy-done.12), channel_id=1, source_target_pairs={{0,4},{2,6},{4,0},{6,2},{8,12},{10,14},{12,8},{14,10},{1,5},{3,7},... | collective-permute-start | bytes 3145736 | tf_op jit(solution)/shard_map/ppermute | solution.py:252
  79.2 3.7 %copy-start.6 = (bf16[2048,512]{1,0:T(8,128)(2,1)S(1)}, bf16[2048,512]{1,0:T(8,128)(2,1)}, u32[]{:S(2)}) copy-start(bf16[2048,512]{1,0:T(8,128)(2,1)} %copy-done.4) | copy-start | bytes 6291460
  82.8 7.2 %copy-start.10 = (bf16[1,512,1024]{2,1,0:T(8,128)(2,1)S(1)}, bf16[1,512,1024]{2,1,0:T(8,128)(2,1)}, u32[]{:S(2)}) copy-start(bf16[1,512,1024]{2,1,0:T(8,128)(2,1)} %copy-done.9) | copy-start | bytes 3145732
  87.6 14.7 %collective-permute-start.4 = (bf16[528,512]{1,0:T(8,128)(2,1)S(1)}, bf16[528,512]{1,0:T(8,128)(2,1)S(1)}, u32[]{:S(2)}, u32[]{:S(2)}) collective-permute-start(bf16[528,512]{1,0:T(8,128)(2,1)S(1)} %get-tuple-element.47), channel_id=1, source_target_pairs={{0,1},{1,0},{2,3},{3,2},{4,5},{5,4},{6,7},{7,6},{8,9},{9,8},{10,11... | collective-permute-start | bytes 1622024 | tf_op jit(solution)/shard_map/ppermute | solution.py:288
  90.1 88.4 %collective-permute-start.11 = (bf16[1,512,1024]{2,1,0:T(8,128)(2,1)S(1)}, bf16[1,512,1024]{2,1,0:T(8,128)(2,1)S(1)}, u32[]{:S(2)}, u32[]{:S(2)}) collective-permute-start(bf16[1,512,1024]{2,1,0:T(8,128)(2,1)S(1)} %copy-done.10), channel_id=1, source_target_pairs={{0,10},{2,8},{4,14},{6,12},{8,2},{10,0},{12,6},{14,4},{1,11},{3,9}... | collective-permute-start | bytes 3145736 | tf_op jit(solution)/shard_map/ppermute | solution.py:252
  94.3 8.0 %copy-start.8 = (bf16[1,512,1024]{2,1,0:T(8,128)(2,1)S(1)}, bf16[1,512,1024]{2,1,0:T(8,128)(2,1)}, u32[]{:S(2)}) copy-start(bf16[1,512,1024]{2,1,0:T(8,128)(2,1)} %copy-done.7) | copy-start | bytes 3145732
  97.6 15.3 %collective-permute-start.6 = (bf16[528,512]{1,0:T(8,128)(2,1)S(1)}, bf16[528,512]{1,0:T(8,128)(2,1)S(1)}, u32[]{:S(2)}, u32[]{:S(2)}) collective-permute-start(bf16[528,512]{1,0:T(8,128)(2,1)S(1)} %get-tuple-element.50), channel_id=1, source_target_pairs={{0,1},{1,0},{2,3},{3,2},{4,5},{5,4},{6,7},{7,6},{8,9},{9,8},{10,11... | collective-permute-start | bytes 1622024 | tf_op jit(solution)/shard_map/ppermute | solution.py:288
  102.3 100.1 %collective-permute-start.13 = (bf16[1,512,1024]{2,1,0:T(8,128)(2,1)S(1)}, bf16[1,512,1024]{2,1,0:T(8,128)(2,1)S(1)}, u32[]{:S(2)}, u32[]{:S(2)}) collective-permute-start(bf16[1,512,1024]{2,1,0:T(8,128)(2,1)S(1)} %copy-done.8), channel_id=1, source_target_pairs={{0,8},{2,10},{4,12},{6,14},{8,0},{10,2},{12,4},{14,6},{1,9},{3,11}... | collective-permute-start | bytes 3145736 | tf_op jit(solution)/shard_map/ppermute | solution.py:252
  109.0 15.4 %collective-permute-start.8 = (bf16[528,512]{1,0:T(8,128)(2,1)S(1)}, bf16[528,512]{1,0:T(8,128)(2,1)S(1)}, u32[]{:S(2)}, u32[]{:S(2)}) collective-permute-start(bf16[528,512]{1,0:T(8,128)(2,1)S(1)} %get-tuple-element.53), channel_id=1, source_target_pairs={{0,1},{1,0},{2,3},{3,2},{4,5},{5,4},{6,7},{7,6},{8,9},{9,8},{10,11... | collective-permute-start | bytes 1622024 | tf_op jit(solution)/shard_map/ppermute | solution.py:288
  121.2 61.5 %collective-permute-start.10 = (bf16[528,512]{1,0:T(8,128)(2,1)S(1)}, bf16[528,512]{1,0:T(8,128)(2,1)S(1)}, u32[]{:S(2)}, u32[]{:S(2)}) collective-permute-start(bf16[528,512]{1,0:T(8,128)(2,1)S(1)} %get-tuple-element.56), channel_id=1, source_target_pairs={{0,1},{1,0},{2,3},{3,2},{4,5},{5,4},{6,7},{7,6},{8,9},{9,8},{10,11... | collective-permute-start | bytes 1622024 | tf_op jit(solution)/shard_map/ppermute | solution.py:288
  182.1 27.6 %collective-permute-start.12 = (bf16[528,512]{1,0:T(8,128)(2,1)S(1)}, bf16[528,512]{1,0:T(8,128)(2,1)S(1)}, u32[]{:S(2)}, u32[]{:S(2)}) collective-permute-start(bf16[528,512]{1,0:T(8,128)(2,1)S(1)} %get-tuple-element.59), channel_id=1, source_target_pairs={{0,1},{1,0},{2,3},{3,2},{4,5},{5,4},{6,7},{7,6},{8,9},{9,8},{10,11... | collective-permute-start | bytes 1622024 | tf_op jit(solution)/shard_map/ppermute | solution.py:288
  204.3 8.8 %collective-permute-start.14 = (bf16[176,512]{1,0:T(8,128)(2,1)S(1)}, bf16[176,512]{1,0:T(8,128)(2,1)S(1)}, u32[]{:S(2)}, u32[]{:S(2)}) collective-permute-start(bf16[176,512]{1,0:T(8,128)(2,1)S(1)} %get-tuple-element.66), channel_id=1, source_target_pairs={{0,1},{1,0},{2,3},{3,2},{4,5},{5,4},{6,7},{7,6},{8,9},{9,8},{10,11... | collective-permute-start | bytes 540680 | tf_op jit(solution)/shard_map/ppermute | solution.py:288
  206.9 8.5 %collective-permute-start.15 = (bf16[176,512]{1,0:T(8,128)(2,1)S(1)}, bf16[176,512]{1,0:T(8,128)(2,1)S(1)}, u32[]{:S(2)}, u32[]{:S(2)}) collective-permute-start(bf16[176,512]{1,0:T(8,128)(2,1)S(1)} %get-tuple-element.67), channel_id=1, source_target_pairs={{0,1},{1,0},{2,3},{3,2},{4,5},{5,4},{6,7},{7,6},{8,9},{9,8},{10,11... | collective-permute-start | bytes 540680 | tf_op jit(solution)/shard_map/ppermute | solution.py:288
  209.1 8.6 %collective-permute-start.16 = (bf16[176,512]{1,0:T(8,128)(2,1)S(1)}, bf16[176,512]{1,0:T(8,128)(2,1)S(1)}, u32[]{:S(2)}, u32[]{:S(2)}) collective-permute-start(bf16[176,512]{1,0:T(8,128)(2,1)S(1)} %get-tuple-element.68), channel_id=1, source_target_pairs={{0,1},{1,0},{2,3},{3,2},{4,5},{5,4},{6,7},{7,6},{8,9},{9,8},{10,11... | collective-permute-start | bytes 540680 | tf_op jit(solution)/shard_map/ppermute | solution.py:288

commit v2 on v1

--- a/solution.py
+++ b/solution.py
@@ -12,6 +12,7 @@
 MOSTC = 512
 EPSILON = 1e-05
 VMEM_LIMIT = 24000 * 1024
+PICK_VMEM_LIMIT = 58 * 1024 * 1024
 
 
 def silu_half(y):
@@ -79,12 +80,9 @@
     return index
 
 
-def attend_kernel(m, offset, place, infos, q_ref, g_ref, self_ref, kv_ref, w_ref, own_ref, *rest):
-    peer_refs, gated = rest[:-1], rest[-1]
+def attend_kernel(m, offset, place, infos, q_ref, g_ref, self_ref, kv_ref, gated_ref):
     tile, width = q_ref.shape
-    heads = width // HD
     tokens = kv_ref.shape[1]
-    columns = own_ref.shape[1]
     scale = 1.0 / math.sqrt(HD)
     who = jnp.bitwise_xor(place[0], m)
     low = infos[0, who] + offset + pl.program_id(0) * tile
@@ -92,7 +90,7 @@
 
     @pl.when(jnp.logical_and(low < infos[2, who], low + tile > infos[1, who]))
     def _():
-        for h in range(heads):
+        for h in range(width // HD):
             cols = slice(h * HD, (h + 1) * HD)
             keys = kv_ref[0, :, 2 * h * HD : (2 * h + 1) * HD]
             values = kv_ref[0, :, (2 * h + 1) * HD : (2 * h + 2) * HD]
@@ -103,19 +101,17 @@
             weights = jnp.where(live, weights, 0.0).astype(jnp.bfloat16)
             mixed = jnp.dot(weights, values, preferred_element_type=jnp.float32)
             normed = normalize(self_ref[:, cols] + mixed)
-            gated[:, cols] = (normed * g_ref[:, cols].astype(jnp.float32)).astype(jnp.bfloat16)
-        partial = jnp.dot(gated[...], w_ref[...], preferred_element_type=jnp.float32)
-        own_ref[...] = partial[:, :columns]
-        for k, peer_ref in enumerate(peer_refs, 1):
-            peer_ref[...] = partial[:, k * columns : (k + 1) * columns].astype(jnp.bfloat16)
-
-
-def attend(place, infos, m, offset, size, tile, queries, gates, selfs, cached, w_turned, ways):
-    width = queries.shape[1]
-    columns = w_turned.shape[1] // ways
+            gated_ref[:, cols] = (normed * g_ref[:, cols].astype(jnp.float32)).astype(jnp.bfloat16)
+
+
+def attend(place, infos, m, offset, size, tile, side, sides, queries, gates, selfs, cached):
+    width = queries.shape[1] // sides
     tokens, kvw = cached.shape[1:]
-    view = pl.BlockSpec((pl.Element(tile), pl.Element(width)), window_rows(m, offset, tile))
-    part = pl.BlockSpec((tile, columns), lambda i, place, infos: (i, 0))
+    rows = window_rows(m, offset, tile)
+    view = pl.BlockSpec(
+        (pl.Element(tile), pl.Element(width)),
+        lambda i, place, infos: (rows(i, place, infos)[0], side * width),
+    )
     return pl.pallas_call(
         lambda *refs: attend_kernel(m, offset, *refs),
         grid_spec=pltpu.PrefetchScalarGridSpec(
@@ -128,70 +124,79 @@
                 pl.BlockSpec(
                     (1, tokens, kvw), lambda i, place, infos: (0, 0, 0), pipeline_mode=pl.Buffered(1)
                 ),
-                pl.BlockSpec(
-                    w_turned.shape, lambda i, place, infos: (0, 0), pipeline_mode=pl.Buffered(1)
-                ),
             ],
-            out_specs=[part] * ways,
-            scratch_shapes=[pltpu.VMEM((tile, width), jnp.bfloat16)],
-        ),
-        out_shape=[jax.ShapeDtypeStruct((size, columns), jnp.float32)]
-        + [jax.ShapeDtypeStruct((size, columns), jnp.bfloat16)] * (ways - 1),
+            out_specs=pl.BlockSpec((tile, width), lambda i, place, infos: (i, 0)),
+        ),
+        out_shape=jax.ShapeDtypeStruct((size, width), jnp.bfloat16),
         cost_estimate=pl.CostEstimate(
-            flops=4 * size * tokens * width + 2 * size * width * ways * columns,
-            bytes_accessed=8 * size * width + 2 * tokens * kvw + 6 * size * ways * columns,
+            flops=4 * size * tokens * width,
+            bytes_accessed=10 * size * width + 2 * tokens * kvw,
             transcendentals=size * tokens * width // HD,
         ),
         compiler_params=pltpu.CompilerParams(vmem_limit_bytes=VMEM_LIMIT),
         name="attend",
-    )(place, infos, queries, gates, selfs, cached, w_turned)
-
-
-def finish_kernel(m, offset, ways, place, infos, total_ref, own_ref, *rest):
-    peer_refs, out_ref = rest[: ways - 1], rest[-1]
+    )(place, infos, queries, gates, selfs, cached)
+
+
+def finish_kernel(m, offset, slots, place, infos, total_ref, w_ref, *rest):
+    gated_refs, out_ref = rest[: len(slots)], rest[-1]
     who = jnp.bitwise_xor(place[0], m)
-    tile = own_ref.shape[0]
+    tile = total_ref.shape[0]
     low = infos[0, who] + offset + pl.program_id(0) * tile
     position = low + lax.broadcasted_iota(jnp.int32, (tile, 1), 0)
     mine = jnp.logical_and(position >= infos[1, who], position < infos[2, who])
     before = total_ref[...].astype(jnp.float32)
-    total = own_ref[...]
-    for peer_ref in peer_refs:
-        total = total + peer_ref[...].astype(jnp.float32)
-    out_ref[...] = jnp.where(mine, total + before, before).astype(out_ref.dtype)
-
-
-def finish(place, infos, m, offset, tile, own, peers, total, after=()):
-    size, columns = own.shape
+    total = before
+    for (k, row), ref in zip(slots, gated_refs):
+        total = total + jnp.dot(
+            ref[...], w_ref[k, row : row + ref.shape[1], :], preferred_element_type=jnp.float32
+        )
+    out_ref[...] = jnp.where(mine, total, before).astype(out_ref.dtype)
+
+
+def finish(place, infos, m, offset, size, tile, slots, gated, total, turned, after=()):
+    columns = total.shape[1]
     view = pl.BlockSpec((pl.Element(tile), pl.Element(columns)), window_rows(m, offset, tile))
-    part = pl.BlockSpec((tile, columns), lambda i, place, infos: (i, 0))
+    blocks = [
+        pl.BlockSpec((tile, g.shape[1]), lambda i, place, infos, skip=skip: (i + skip, 0))
+        for g, skip in gated
+    ]
+    arrays = [g for g, _ in gated]
+    work = sum(g.shape[1] for g in arrays)
     return pl.pallas_call(
-        lambda *refs: finish_kernel(m, offset, 1 + len(peers), *refs),
+        lambda *refs: finish_kernel(m, offset, slots, *refs),
         grid_spec=pltpu.PrefetchScalarGridSpec(
             num_scalar_prefetch=2,
             grid=(size // tile,),
-            in_specs=[view]
-            + [part] * (1 + len(peers))
+            in_specs=[
+                view,
+                pl.BlockSpec(
+                    turned.shape, lambda i, place, infos: (0, 0, 0), pipeline_mode=pl.Buffered(1)
+                ),
+            ]
+            + blocks
             + [pl.BlockSpec(memory_space=pl.ANY)] * len(after),
             out_specs=view,
         ),
         out_shape=jax.ShapeDtypeStruct(total.shape, total.dtype),
         input_output_aliases={2: 0},
         cost_estimate=pl.CostEstimate(
-            flops=3 * size * columns, bytes_accessed=10 * size * columns, transcendentals=0
+            flops=2 * size * columns * work,
+            bytes_accessed=4 * size * columns + 2 * size * work + 2 * work * columns,
+            transcendentals=0,
         ),
         compiler_params=pltpu.CompilerParams(vmem_limit_bytes=VMEM_LIMIT),
         name="finish",
-    )(place, infos, total, own, *peers, *after)
+    )(place, infos, total, turned, *arrays, *after)
 
 
 def pick_kernel(place, table, kv_ref, *rest):
     rest[-1][...] = kv_ref[...]
 
 
-def pick(place, table, kv_cache, m, after):
-    user = lambda i, place, table: (table[jnp.bitwise_xor(place[0], m), place[0]], i, 0)
-    tokens, kvw = kv_cache.shape[1:]
+def pick(place, table, count, kv_cache, m, side, sides, after):
+    user = lambda i, place, table: (table[jnp.bitwise_xor(place[0], m) * count + place[0]], i, side)
+    tokens, kvw = kv_cache.shape[1], kv_cache.shape[2] // sides
     block = (1, tokens // 4, kvw)
     return pl.pallas_call(
         pick_kernel,
@@ -202,7 +207,7 @@
             out_specs=pl.BlockSpec(block, lambda i, place, table: (0, i, 0)),
         ),
         out_shape=jax.ShapeDtypeStruct((1, tokens, kvw), kv_cache.dtype),
-        compiler_params=pltpu.CompilerParams(vmem_limit_bytes=VMEM_LIMIT),
+        compiler_params=pltpu.CompilerParams(vmem_limit_bytes=PICK_VMEM_LIMIT),
         name="pick",
     )(place, table, kv_cache, *after)
 
@@ -239,18 +244,23 @@
     everyone = jnp.arange(count, dtype=jnp.int32)
     names = (owners[None, :] == everyone[:, None]).astype(jnp.int32)
     wanted = jnp.sum(names * request_user[None, :], axis=1)
-    table = lax.all_gather(wanted, "req", axis=0, tiled=False)
+    spread = jnp.where(everyone[:, None] == myself, wanted[None, :], 0)
+    table = lax.psum(spread.reshape(-1), "req")
     place = myself[None].astype(jnp.int32)
 
     order = exchange_order(count)
     arrived = {}
     after = []
+    last = order[-1]
     for m in order + [1, 0]:
-        picked = pick(place, table, kv_cache, m, after)
-        after = [picked]
-        if m:
-            picked = lax.ppermute(picked, "req", [(i, i ^ m) for i in range(count)])
-        arrived[m] = picked
+        sides = 2 if m == last else 1
+        arrived[m] = []
+        for part in range(sides):
+            picked = pick(place, table, count, kv_cache, m, part, sides, after)
+            after = [picked]
+            if m:
+                picked = lax.ppermute(picked, "req", [(i, i ^ m) for i in range(count)])
+            arrived[m].append(picked)
 
     segment = candidate_request[0]
     served = jnp.sum(names * jnp.arange(owners.shape[0], dtype=jnp.int32)[None, :], axis=1)
@@ -263,38 +273,53 @@
     infos = jnp.stack([firsts, starts, ends, live])
 
     queries, gates, selfs = project(candidates, w_in)
-    turned = jnp.concatenate(
-        [
-            lax.dynamic_slice_in_dim(w_out, ((side + k) % ways) * columns, columns, 1)
-            for k in range(ways)
-        ],
-        axis=1,
-    )
+
+    def to_peer(value, k):
+        return lax.ppermute(value, "head", [(i, (i + k) % ways) for i in range(ways)])
+
+    turned = []
+    for k in range(ways):
+        piece = lax.dynamic_slice_in_dim(w_out, ((side + k) % ways) * columns, columns, 1)
+        turned.append(to_peer(piece, k) if k else piece)
+    turned = jnp.stack(turned)
     ranked = lax.dynamic_slice_in_dim(candidates, side * columns, columns, 1)
     sequence = [0, 1] + order
     tile = window // 3 if window % 48 == 0 else window
-    steps = [(m, 0, window) for m in sequence[:-1]]
-    steps += [(sequence[-1], offset, tile) for offset in range(0, window, tile)]
-    pending = []
-    ready = []
-    for m, offset, size in steps:
+    half = w_out.shape[0] // 2
+
+    def run(m, offset, size, part, sides, ready):
         current = infos
         if ready:
             current, *ready = lax.optimization_barrier((infos, *ready))
-        own, *peers = attend(
-            place, current, m, offset, size, tile, queries, gates, selfs, arrived[m], turned, ways
+        gated = attend(
+            place, current, m, offset, size, tile, part, sides, queries, gates, selfs, arrived[m][part]
         )
-        landed = [
-            lax.ppermute(peer, "head", [(i, (i + k) % ways) for i in range(ways)])
-            for k, peer in enumerate(peers, 1)
-        ]
-        ready = [own]
-        if pending and m != sequence[-1]:
-            ranked = finish(place, infos, *pending.pop(0), ranked, after=[own])
-            ready = [own, ranked]
-        pending.append((m, offset, tile, own, landed))
-    for one in pending:
-        ranked = finish(place, infos, *one, ranked, after=ready[:1])
+        return [gated] + [to_peer(gated, k) for k in range(1, ways)]
+
+    def add(m, offset, size, slots, gated, ranked, after):
+        return finish(place, infos, m, offset, size, tile, slots, gated, ranked, turned, after)
+
+    full = [(k, 0) for k in range(ways)]
+    pending = None
+    ready = []
+    for m in sequence[:-1]:
+        sent = run(m, 0, window, 0, 1, ready)
+        ready = [sent[0]]
+        if pending is not None:
+            ranked = add(pending[0], 0, window, full, [(g, 0) for g in pending[1]], ranked, ready)
+            ready = [sent[0], ranked]
+        pending = (m, sent)
+    early = run(last, 0, window, 0, 2, ready)
+    ranked = add(pending[0], 0, window, full, [(g, 0) for g in pending[1]], ranked, early[:1])
+    ready = [early[0], ranked]
+    late = []
+    for offset in range(0, window, tile):
+        late.append(run(last, offset, tile, 1, 2, ready))
+        ready = [late[-1][0]]
+    slots = full + [(k, half) for k in range(ways)]
+    for number, sent in enumerate(late):
+        gated = [(g, number) for g in early] + [(g, 0) for g in sent]
+        ranked = add(last, number * tile, tile, slots, gated, ranked, ready)
     return ranked
 
 

time: 221 us -> 237 us (1.072)
  Pallas kernels: 93.1 us -> 116 us
  waiting for transfers between devices: 74.8 us -> 61.7 us
  starting transfers between devices: 16.6 us -> 24.3 us
  local copies, waits for them, and re-layouts: 22.8 us -> 19.7 us
    pallas_call x8 -> x9, Pallas kernels: 11.9 us -> 36.2 us  [pick(): pl.pallas_call(pick_kernel, grid_spec=pltpu.PrefetchScalarGridSpec(num_sc...]
    ppermute x7 -> x8, waiting for transfers between devices: 66.7 us -> 51.4 us  [per_device(): picked = lax.ppermute(picked, 'req', [(i, i ^ m) for i in range(count)])]
    psum x0 -> x1, blocking collectives: none -> 11.2 us  [per_device(): table = lax.psum(spread.reshape(-1), 'req')]
    unnamed x1 -> x0, blocking collectives: 10.6 us -> none
    ppermute x7 -> x8, starting transfers between devices: 4.82 us -> 10.5 us  [per_device(): picked = lax.ppermute(picked, 'req', [(i, i ^ m) for i in range(count)])]
    pallas_call x10 -> x11, Pallas kernels: 35 us -> 29.4 us  [attend(): pl.pallas_call(lambda *refs: attend_kernel(m, offset, *refs), grid_spec=p...]
    pallas_call x10, Pallas kernels: 31.1 us -> 35.1 us  [finish(): pl.pallas_call(lambda *refs: finish_kernel(m, offset, slots, *refs), grid...]
    unnamed x43 -> x42, local copies, waits for them, and re-layouts: 21 us -> 17 us
  transfers between devices with their start and end apart: 17 -> 20, of which waited for: 6 -> 6; matrix products, arithmetic and copies ran while one was open for 1% -> 2% of each run, Pallas kernels for 40% -> 46%
where the time goes in v2:
time: 237 us; the launch traced here: 235 us
  Pallas kernels  116 us (49%)
  waiting for transfers between devices  61.7 us (26%)
  starting transfers between devices  24.3 us (10%)
  local copies, waits for them, and re-layouts  19.7 us (8%)
  blocking collectives  11.2 us (5%)
    ppermute x8, waiting for transfers between devices, per_device(): picked = lax.ppermute(picked, 'req', [(i, i ^ m) for i in range(count)])  51.4 us
    pallas_call x9, Pallas kernels, pick(): pl.pallas_call(pick_kernel, grid_spec=pltpu.PrefetchScalarGridSpec(num_sc...  36.2 us
    pallas_call x10, Pallas kernels, finish(): pl.pallas_call(lambda *refs: finish_kernel(m, offset, slots, *refs), grid...  35.1 us
    pallas_call x11, Pallas kernels, attend(): pl.pallas_call(lambda *refs: attend_kernel(m, offset, *refs), grid_spec=p...  29.4 us
    unnamed x42, local copies, waits for them, and re-layouts  17 us
    pallas_call x1, Pallas kernels, project(): pl.pallas_call(project_kernel, grid=(rows // tile,), in_specs=[pl.BlockSp...  15.1 us
    ppermute x12, starting transfers between devices, to_peer(): lax.ppermute(value, 'head', [(i, (i + k) % ways) for i in range(ways)])  13.9 us
    psum x1, blocking collectives, per_device(): table = lax.psum(spread.reshape(-1), 'req')  11.2 us
  transfers between devices with their start and end apart: 20, of which 6 were waited for; matrix products, arithmetic and copies ran while one was open for 2% of the time, Pallas kernels for 46%

profile of v2, /device:TPU:0, one launch (start us, length us, event | category | flops | bytes accessed | tf_op | source)
XLA Modules:
  0.0 235.4 jit_solution(11012439406208531053)
XLA Ops:
  1.0 11.2 %psum.7.table = s32[64]{0:T(128)} all-reduce(s32[64]{0:T(128)S(1)} %select_n.58), channel_id=1, replica_groups=mesh['groups'=2,'req'=8,'head'=2,'rep'=1] {'req'}, use_global_device_ids=true, to_apply=%region_6.7 | all-reduce | flops 64 | bytes 512 | tf_op jit(solution)/shard_map/psum | solution.py:248
  12.1 4.0 %pick.9.rest_0_ = bf16[1,512,1024]{2,1,0:T(8,128)(2,1)} custom-call(s32[1]{0:T(128)} %bitcast.place.refs_0_, s32[64]{0:T(128)} %psum.7.table, bf16[8,512,1024]{2,1,0:T(8,128)(2,1)} %kv_ref.17), custom_call_target="tpu_custom_call" | custom-call | tf_op jit(solution)/shard_map/pick/pallas_call | solution.py:201
  16.2 4.0 %pick.10.rest_0_ = bf16[1,512,1024]{2,1,0:T(8,128)(2,1)} custom-call(s32[1]{0:T(128)} %bitcast.place.refs_0_, s32[64]{0:T(128)} %psum.7.table, bf16[8,512,1024]{2,1,0:T(8,128)(2,1)} %kv_ref.17, bf16[1,512,1024]{2,1,0:T(8,128)(2,1)} %pick.9.rest_0_), custom_call_target="tpu_custom_call" | custom-call | tf_op jit(solution)/shard_map/pick/pallas_call | solution.py:201
  20.8 4.0 %pick.11.rest_0_ = bf16[1,512,1024]{2,1,0:T(8,128)(2,1)} custom-call(s32[1]{0:T(128)} %bitcast.place.refs_0_, s32[64]{0:T(128)} %psum.7.table, bf16[8,512,1024]{2,1,0:T(8,128)(2,1)} %kv_ref.17, bf16[1,512,1024]{2,1,0:T(8,128)(2,1)} %pick.10.rest_0_), custom_call_target="tpu_custom_call" | custom-call | tf_op jit(solution)/shard_map/pick/pallas_call | solution.py:201
  24.9 4.1 %pick.12.rest_0_ = bf16[1,512,1024]{2,1,0:T(8,128)(2,1)} custom-call(s32[1]{0:T(128)} %bitcast.place.refs_0_, s32[64]{0:T(128)} %psum.7.table, bf16[8,512,1024]{2,1,0:T(8,128)(2,1)} %kv_ref.17, bf16[1,512,1024]{2,1,0:T(8,128)(2,1)} %pick.11.rest_0_), custom_call_target="tpu_custom_call" | custom-call | tf_op jit(solution)/shard_map/pick/pallas_call | solution.py:201
  28.9 4.0 %pick.13.rest_0_ = bf16[1,512,1024]{2,1,0:T(8,128)(2,1)} custom-call(s32[1]{0:T(128)} %bitcast.place.refs_0_, s32[64]{0:T(128)} %psum.7.table, bf16[8,512,1024]{2,1,0:T(8,128)(2,1)} %kv_ref.17, bf16[1,512,1024]{2,1,0:T(8,128)(2,1)} %pick.12.rest_0_), custom_call_target="tpu_custom_call" | custom-call | tf_op jit(solution)/shard_map/pick/pallas_call | solution.py:201
  33.0 3.8 %pick.14.rest_0_ = bf16[1,512,512]{2,1,0:T(8,128)(2,1)} custom-call(s32[1]{0:T(128)} %bitcast.place.refs_0_, s32[64]{0:T(128)} %psum.7.table, bf16[8,512,1024]{2,1,0:T(8,128)(2,1)} %kv_ref.17, bf16[1,512,1024]{2,1,0:T(8,128)(2,1)} %pick.13.rest_0_), custom_call_target="tpu_custom_call" | custom-call | tf_op jit(solution)/shard_map/pick/pallas_call | solution.py:201
  36.8 3.8 %pick.15.rest_0_ = bf16[1,512,512]{2,1,0:T(8,128)(2,1)} custom-call(s32[1]{0:T(128)} %bitcast.place.refs_0_, s32[64]{0:T(128)} %psum.7.table, bf16[8,512,1024]{2,1,0:T(8,128)(2,1)} %kv_ref.17, bf16[1,512,512]{2,1,0:T(8,128)(2,1)} %pick.14.rest_0_), custom_call_target="tpu_custom_call" | custom-call | tf_op jit(solution)/shard_map/pick/pallas_call | solution.py:201
  40.6 4.2 %pick.16.rest_0_ = bf16[1,512,1024]{2,1,0:T(8,128)(2,1)} custom-call(s32[1]{0:T(128)} %bitcast.place.refs_0_, s32[64]{0:T(128)} %psum.7.table, bf16[8,512,1024]{2,1,0:T(8,128)(2,1)} %kv_ref.17, bf16[1,512,512]{2,1,0:T(8,128)(2,1)} %pick.15.rest_0_), custom_call_target="tpu_custom_call" | custom-call | tf_op jit(solution)/shard_map/pick/pallas_call | solution.py:201
  47.7 2.2 copy-done.11
  49.9 2.2 copy-done.13
  52.1 15.1 %project.1 = (bf16[2048,512]{1,0:T(8,128)(2,1)S(1)}, bf16[2048,512]{1,0:T(8,128)(2,1)S(1)}, f32[2048,512]{1,0:T(8,128)S(1)}) custom-call(bf16[2048,1024]{1,0:T(8,128)(2,1)S(1)} %copy-done.11, bf16[1024,2048]{1,0:T(8,128)(2,1)S(1)} %copy-done.13), custom_call_target="tpu_custom_call" | custom-call | flops 8589934592 | bytes 16777216 | tf_op jit(solution)/shard_map/project/pallas_call | solution.py:52
  70.2 4.2 %pick.17.refs_5_ = bf16[1,512,1024]{2,1,0:T(8,128)(2,1)} custom-call(s32[1]{0:T(128)} %bitcast.place.refs_0_, s32[64]{0:T(128)} %psum.7.table, bf16[8,512,1024]{2,1,0:T(8,128)(2,1)} %kv_ref.17, bf16[1,512,1024]{2,1,0:T(8,128)(2,1)} %pick.16.rest_0_), custom_call_target="tpu_custom_call" | custom-call | tf_op jit(solution)/shard_map/pick/pallas_call | solution.py:201
  74.4 1.6 copy-done.3
  76.0 1.6 copy-done.7
  78.8 4.1 %attend.11.refs_4_ = bf16[528,512]{1,0:T(8,128)(2,1)S(1)} custom-call(s32[1]{0:T(128)} %bitcast.place.refs_0_, s32[4,8]{1,0:T(4,128)S(1)} %pad_add_fusion.refs_1_, bf16[2048,512]{1,0:T(8,128)(2,1)S(1)} %copy-done.3, bf16[2048,512]{1,0:T(8,128)(2,1)S(1)} %copy-done.7, f32[2048,512]{1,0:T(8,128)S(1)} %get-tuple-element.20.refs_4_, ...), custom_call_target="tpu_custom_call" | custom-call | flops 553648128 | bytes 3751936 | tf_op jit(solution)/shard_map/attend/pallas_call | solution.py:115
  84.2 2.2 copy-done.1
  86.4 1.6 copy-done.4
  88.0 1.6 copy-done.8
  89.6 4.5 %attend.12.refs_6_.refs_4_ = bf16[528,512]{1,0:T(8,128)(2,1)S(1)} custom-call(s32[1]{0:T(128)} %bitcast.place.refs_0_, s32[4,8]{1,0:T(4,128)S(1)} %pad_add_fusion.refs_1_, bf16[2048,512]{1,0:T(8,128)(2,1)S(1)} %copy-done.4, bf16[2048,512]{1,0:T(8,128)(2,1)S(1)} %copy-done.8, f32[2048,512]{1,0:T(8,128)S(1)} %copy-done.1, ...), custom_call_target="tpu_custom_call" | custom-call | flops 553648128 | bytes 3751936 | tf_op jit(solution)/shard_map/attend/pallas_call | solution.py:115
  94.1 1.6 collective-permute-start.3
  95.7 1.6 constant_dynamic-slice_fusion.1.refs_2_
  99.3 3.9 %finish.10.refs_2_ = bf16[2048,512]{1,0:T(8,128)(2,1)} custom-call(s32[1]{0:T(128)} %bitcast.place.refs_0_, s32[4,8]{1,0:T(4,128)S(1)} %pad_add_fusion.refs_1_, bf16[2048,512]{1,0:T(8,128)(2,1)} %constant_dynamic-slice_fusion.1.refs_2_, bf16[2,512,512]{2,1,0:T(8,128)(2,1)S(1)} %pad_maximum_fusion.refs_3_, ...), custom_call_target="tpu_custom_call", output_to_operand_aliasing={{}: (2, {})} | custom-call | flops 553648128 | bytes 3211264 | tf_op jit(solution)/shard_map/finish/pallas_call | solution.py:166
  103.3 4.2 %attend.13.refs_6_.refs_4_ = bf16[528,512]{1,0:T(8,128)(2,1)S(1)} custom-call(s32[1]{0:T(128)} %bitcast.place.refs_0_, s32[4,8]{1,0:T(4,128)S(1)} %pad_add_fusion.refs_1_, bf16[2048,512]{1,0:T(8,128)(2,1)S(1)} %copy-done.5, bf16[2048,512]{1,0:T(8,128)(2,1)S(1)} %copy-done.9, f32[2048,512]{1,0:T(8,128)S(1)} %copy-done.1, ...), custom_call_target="tpu_custom_call" | custom-call | flops 553648128 | bytes 3751936 | tf_op jit(solution)/shard_map/attend/pallas_call | solution.py:115
  109.9 3.9 %finish.11.refs_2_ = bf16[2048,512]{1,0:T(8,128)(2,1)} custom-call(s32[1]{0:T(128)} %bitcast.place.refs_0_, s32[4,8]{1,0:T(4,128)S(1)} %pad_add_fusion.refs_1_, bf16[2048,512]{1,0:T(8,128)(2,1)} %finish.10.refs_2_, bf16[2,512,512]{2,1,0:T(8,128)(2,1)S(1)} %pad_maximum_fusion.refs_3_, ...), custom_call_target="tpu_custom_call", output_to_operand_aliasing={{}: (2, {})} | custom-call | flops 553648128 | bytes 3211264 | tf_op jit(solution)/shard_map/finish/pallas_call | solution.py:166
  113.8 1.8 attend.14.refs_6_.refs_4_
  115.7 1.5 collective-permute-start.7
  117.2 4.4 %collective-permute-done.5.refs_5_ = bf16[528,512]{1,0:T(8,128)(2,1)S(1)} collective-permute-done((bf16[528,512]{1,0:T(8,128)(2,1)S(1)}, bf16[528,512]{1,0:T(8,128)(2,1)S(1)}, u32[]{:S(2)}, u32[]{:S(2)}) %collective-permute-start.5) | collective-permute-done | bytes 540704 | tf_op jit(solution)/shard_map/ppermute | solution.py:278
  121.6 3.9 %finish.12.refs_2_ = bf16[2048,512]{1,0:T(8,128)(2,1)} custom-call(s32[1]{0:T(128)} %bitcast.place.refs_0_, s32[4,8]{1,0:T(4,128)S(1)} %pad_add_fusion.refs_1_, bf16[2048,512]{1,0:T(8,128)(2,1)} %finish.11.refs_2_, bf16[2,512,512]{2,1,0:T(8,128)(2,1)S(1)} %pad_maximum_fusion.refs_3_, ...), custom_call_target="tpu_custom_call", output_to_operand_aliasing={{}: (2, {})} | custom-call | flops 553648128 | bytes 3211264 | tf_op jit(solution)/shard_map/finish/pallas_call | solution.py:166
  125.6 1.8 attend.15.refs_6_.refs_4_
  128.0 5.2 %collective-permute-done.7.refs_5_ = bf16[528,512]{1,0:T(8,128)(2,1)S(1)} collective-permute-done((bf16[528,512]{1,0:T(8,128)(2,1)S(1)}, bf16[528,512]{1,0:T(8,128)(2,1)S(1)}, u32[]{:S(2)}, u32[]{:S(2)}) %collective-permute-start.7) | collective-permute-done | bytes 540704 | tf_op jit(solution)/shard_map/ppermute | solution.py:278
  133.2 3.9 %finish.13.refs_2_ = bf16[2048,512]{1,0:T(8,128)(2,1)} custom-call(s32[1]{0:T(128)} %bitcast.place.refs_0_, s32[4,8]{1,0:T(4,128)S(1)} %pad_add_fusion.refs_1_, bf16[2048,512]{1,0:T(8,128)(2,1)} %finish.12.refs_2_, bf16[2,512,512]{2,1,0:T(8,128)(2,1)S(1)} %pad_maximum_fusion.refs_3_, ...), custom_call_target="tpu_custom_call", output_to_operand_aliasing={{}: (2, {})} | custom-call | flops 553648128 | bytes 3211264 | tf_op jit(solution)/shard_map/finish/pallas_call | solution.py:166
  137.2 4.1 %attend.16.refs_6_.refs_4_ = bf16[528,512]{1,0:T(8,128)(2,1)S(1)} custom-call(s32[1]{0:T(128)} %bitcast.place.refs_0_, s32[4,8]{1,0:T(4,128)S(1)} %pad_add_fusion.refs_1_, bf16[2048,512]{1,0:T(8,128)(2,1)S(1)} %copy-done.5, bf16[2048,512]{1,0:T(8,128)(2,1)S(1)} %copy-done.9, f32[2048,512]{1,0:T(8,128)S(1)} %copy-done.1, ...), custom_call_target="tpu_custom_call" | custom-call | flops 553648128 | bytes 3751936 | tf_op jit(solution)/shard_map/attend/pallas_call | solution.py:115
  141.9 6.1 %collective-permute-start.14 = (bf16[1,512,512]{2,1,0:T(8,128)(2,1)S(1)}, bf16[1,512,512]{2,1,0:T(8,128)(2,1)S(1)}, u32[]{:S(2)}, u32[]{:S(2)}) collective-permute-start(bf16[1,512,512]{2,1,0:T(8,128)(2,1)S(1)} %copy-done.17), channel_id=1, source_target_pairs={{0,8},{2,10},{4,12},{6,14},{8,0},{10,2},{12,4},{14,6},{1,9},{3,11}... | collective-permute-start | bytes 1572872 | tf_op jit(solution)/shard_map/ppermute | solution.py:262
  148.0 3.9 %finish.14.refs_2_ = bf16[2048,512]{1,0:T(8,128)(2,1)} custom-call(s32[1]{0:T(128)} %bitcast.place.refs_0_, s32[4,8]{1,0:T(4,128)S(1)} %pad_add_fusion.refs_1_, bf16[2048,512]{1,0:T(8,128)(2,1)} %finish.13.refs_2_, bf16[2,512,512]{2,1,0:T(8,128)(2,1)S(1)} %pad_maximum_fusion.refs_3_, ...), custom_call_target="tpu_custom_call", output_to_operand_aliasing={{}: (2, {})} | custom-call | flops 553648128 | bytes 3211264 | tf_op jit(solution)/shard_map/finish/pallas_call | solution.py:166
  151.9 34.0 %collective-permute-done.12.refs_5_ = bf16[1,512,1024]{2,1,0:T(8,128)(2,1)S(1)} collective-permute-done((bf16[1,512,1024]{2,1,0:T(8,128)(2,1)S(1)}, bf16[1,512,1024]{2,1,0:T(8,128)(2,1)S(1)}, u32[]{:S(2)}, u32[]{:S(2)}) %collective-permute-start.12) | collective-permute-done | bytes 1048608 | tf_op jit(solution)/shard_map/ppermute | solution.py:262
  185.9 3.2 %attend.17.refs_6_.refs_4_ = bf16[528,512]{1,0:T(8,128)(2,1)S(1)} custom-call(s32[1]{0:T(128)} %bitcast.place.refs_0_, s32[4,8]{1,0:T(4,128)S(1)} %pad_add_fusion.refs_1_, bf16[2048,512]{1,0:T(8,128)(2,1)S(1)} %copy-done.5, bf16[2048,512]{1,0:T(8,128)(2,1)S(1)} %copy-done.9, f32[2048,512]{1,0:T(8,128)S(1)} %copy-done.1, ...), custom_call_target="tpu_custom_call" | custom-call | flops 553648128 | bytes 3751936 | tf_op jit(solution)/shard_map/attend/pallas_call | solution.py:115
  191.5 3.9 %finish.15.refs_2_ = bf16[2048,512]{1,0:T(8,128)(2,1)} custom-call(s32[1]{0:T(128)} %bitcast.place.refs_0_, s32[4,8]{1,0:T(4,128)S(1)} %pad_add_fusion.refs_1_, bf16[2048,512]{1,0:T(8,128)(2,1)} %finish.14.refs_2_, bf16[2,512,512]{2,1,0:T(8,128)(2,1)S(1)} %pad_maximum_fusion.refs_3_, ...), custom_call_target="tpu_custom_call", output_to_operand_aliasing={{}: (2, {})} | custom-call | flops 553648128 | bytes 3211264 | tf_op jit(solution)/shard_map/finish/pallas_call | solution.py:166
  195.4 15.4 %collective-permute-done.14.refs_5_ = bf16[1,512,512]{2,1,0:T(8,128)(2,1)S(1)} collective-permute-done((bf16[1,512,512]{2,1,0:T(8,128)(2,1)S(1)}, bf16[1,512,512]{2,1,0:T(8,128)(2,1)S(1)}, u32[]{:S(2)}, u32[]{:S(2)}) %collective-permute-start.14) | collective-permute-done | bytes 524320 | tf_op jit(solution)/shard_map/ppermute | solution.py:262
  210.8 2.4 %attend.18.refs_6_.refs_4_ = bf16[528,256]{1,0:T(8,128)(2,1)S(1)} custom-call(s32[1]{0:T(128)} %bitcast.place.refs_0_, s32[4,8]{1,0:T(4,128)S(1)} %pad_add_fusion.refs_1_, bf16[2048,512]{1,0:T(8,128)(2,1)S(1)} %copy-done.5, bf16[2048,512]{1,0:T(8,128)(2,1)S(1)} %copy-done.9, f32[2048,512]{1,0:T(8,128)S(1)} %copy-done.1, ...), custom_call_target="tpu_custom_call" | custom-call | flops 276824064 | bytes 1875968 | tf_op jit(solution)/shard_map/attend/pallas_call | solution.py:115
  213.2 1.6 collective-permute-start.15
  214.8 3.9 %finish.16.refs_2_ = bf16[2048,512]{1,0:T(8,128)(2,1)} custom-call(s32[1]{0:T(128)} %bitcast.place.refs_0_, s32[4,8]{1,0:T(4,128)S(1)} %pad_add_fusion.refs_1_, bf16[2048,512]{1,0:T(8,128)(2,1)} %finish.15.refs_2_, bf16[2,512,512]{2,1,0:T(8,128)(2,1)S(1)} %pad_maximum_fusion.refs_3_, ...), custom_call_target="tpu_custom_call", output_to_operand_aliasing={{}: (2, {})} | custom-call | flops 553648128 | bytes 3211264 | tf_op jit(solution)/shard_map/finish/pallas_call | solution.py:166
  218.7 2.1 collective-permute-done.16.refs_5_
  222.1 1.6 collective-permute-start.17
  226.2 1.6 collective-permute-start.19
  227.8 2.5 %finish.17.refs_2_ = bf16[2048,512]{1,0:T(8,128)(2,1)} custom-call(s32[1]{0:T(128)} %bitcast.place.refs_0_, s32[4,8]{1,0:T(4,128)S(1)} %pad_add_fusion.refs_1_, bf16[2048,512]{1,0:T(8,128)(2,1)} %finish.16.refs_2_, bf16[2,512,512]{2,1,0:T(8,128)(2,1)S(1)} %pad_maximum_fusion.refs_3_, ...), custom_call_target="tpu_custom_call", output_to_operand_aliasing={{}: (2, {})} | custom-call | flops 184549376 | bytes 1769472 | tf_op jit(solution)/shard_map/finish/pallas_call | solution.py:166
  230.3 2.5 %finish.18.refs_2_ = bf16[2048,512]{1,0:T(8,128)(2,1)} custom-call(s32[1]{0:T(128)} %bitcast.place.refs_0_, s32[4,8]{1,0:T(4,128)S(1)} %pad_add_fusion.refs_1_, bf16[2048,512]{1,0:T(8,128)(2,1)} %finish.17.refs_2_, bf16[2,512,512]{2,1,0:T(8,128)(2,1)S(1)} %pad_maximum_fusion.refs_3_, ...), custom_call_target="tpu_custom_call", output_to_operand_aliasing={{}: (2, {})} | custom-call | flops 184549376 | bytes 1769472 | tf_op jit(solution)/shard_map/finish/pallas_call | solution.py:166
  232.9 2.5 %finish.19 = bf16[2048,512]{1,0:T(8,128)(2,1)} custom-call(s32[1]{0:T(128)} %bitcast.place.refs_0_, s32[4,8]{1,0:T(4,128)S(1)} %pad_add_fusion.refs_1_, bf16[2048,512]{1,0:T(8,128)(2,1)} %finish.18.refs_2_, bf16[2,512,512]{2,1,0:T(8,128)(2,1)S(1)} %pad_maximum_fusion.refs_3_, ...), custom_call_target="tpu_custom_call", output_to_operand_aliasing={{}: (2, {})} | custom-call | flops 184549376 | bytes 1769472 | tf_op jit(solution)/shard_map/finish/pallas_call | solution.py:166
  (77 shorter events, 22.0 us)
Async XLA Ops:
  16.2 87.1 %collective-permute-start.4 = (bf16[1,512,1024]{2,1,0:T(8,128)(2,1)}, bf16[1,512,1024]{2,1,0:T(8,128)(2,1)}, u32[]{:S(2)}, u32[]{:S(2)}) collective-permute-start(bf16[1,512,1024]{2,1,0:T(8,128)(2,1)} %pick.9.rest_0_), channel_id=1, source_target_pairs={{0,14},{2,12},{4,10},{6,8},{8,6},{10,4},{12,2},{14,0},{1,15},{3,13... | collective-permute-start | bytes 3145736 | tf_op jit(solution)/shard_map/ppermute | solution.py:262
  20.2 93.6 %collective-permute-start.6 = (bf16[1,512,1024]{2,1,0:T(8,128)(2,1)}, bf16[1,512,1024]{2,1,0:T(8,128)(2,1)S(1)}, u32[]{:S(2)}, u32[]{:S(2)}) collective-permute-start(bf16[1,512,1024]{2,1,0:T(8,128)(2,1)} %pick.10.rest_0_), channel_id=1, source_target_pairs={{0,6},{2,4},{4,2},{6,0},{8,14},{10,12},{12,10},{14,8},{1,7},{3,5},... | collective-permute-start | bytes 3145736 | tf_op jit(solution)/shard_map/ppermute | solution.py:262
  40.6 4.5 %copy-start.19 = (bf16[512,1024]{1,0:T(8,128)(2,1)S(1)}, bf16[512,1024]{1,0:T(8,128)(2,1)}, u32[]{:S(2)}) copy-start(bf16[512,1024]{1,0:T(8,128)(2,1)} %param.15) | copy-start | bytes 3145732
  44.8 38.8 %collective-permute-start.2 = (bf16[1,512,1024]{2,1,0:T(8,128)(2,1)}, bf16[1,512,1024]{2,1,0:T(8,128)(2,1)}, u32[]{:S(2)}, u32[]{:S(2)}) collective-permute-start(bf16[1,512,1024]{2,1,0:T(8,128)(2,1)} %pick.16.rest_0_), channel_id=1, source_target_pairs={{0,2},{2,0},{4,6},{6,4},{8,10},{10,8},{12,14},{14,12},{1,3},{3,1},... | collective-permute-start | bytes 3145736 | tf_op jit(solution)/shard_map/ppermute | solution.py:262
  46.2 47.9 %collective-permute-start = (bf16[512,512]{1,0:T(8,128)(2,1)}, bf16[512,512]{1,0:T(8,128)(2,1)}, u32[]{:S(2)}, u32[]{:S(2)}) collective-permute-start(bf16[512,512]{1,0:T(8,128)(2,1)} %get-tuple-element.38), channel_id=1, source_target_pairs={{0,1},{1,0},{2,3},{3,2},{4,5},{5,4},{6,7},{7,6},{8,9},{9,8},{10,11... | collective-permute-start | bytes 1572872 | tf_op jit(solution)/shard_map/ppermute | solution.py:278
  47.7 2.2 copy-start.11
  49.9 2.2 copy-start.13
  52.1 17.8 %copy-start.20 = (s32[1,2048]{1,0:T(1,128)S(1)}, s32[1,2048]{1,0:T(1,128)}, u32[]{:S(2)}) copy-start(s32[1,2048]{1,0:T(1,128)} %param.9) | copy-start | bytes 24580
  67.2 1.3 copy-start.2
  68.6 1.4 copy-start.6
  69.9 4.5 %copy-start = (f32[2048,512]{1,0:T(8,128)}, f32[2048,512]{1,0:T(8,128)S(1)}, u32[]{:S(2)}) copy-start(f32[2048,512]{1,0:T(8,128)S(1)} %get-tuple-element.20.refs_4_) | copy-start | bytes 12582916
  74.4 1.6 copy-start.3
  76.0 1.6 copy-start.7
  77.6 1.2 copy-start.10
  83.0 15.5 %collective-permute-start.1 = (bf16[528,512]{1,0:T(8,128)(2,1)S(1)}, bf16[528,512]{1,0:T(8,128)(2,1)S(1)}, u32[]{:S(2)}, u32[]{:S(2)}) collective-permute-start(bf16[528,512]{1,0:T(8,128)(2,1)S(1)} %attend.11.refs_4_), channel_id=1, source_target_pairs={{0,1},{1,0},{2,3},{3,2},{4,5},{5,4},{6,7},{7,6},{8,9},{9,8},{10,11... | collective-permute-start | bytes 1622024 | tf_op jit(solution)/shard_map/ppermute | solution.py:278
  83.6 42.0 %collective-permute-start.8 = (bf16[1,512,1024]{2,1,0:T(8,128)(2,1)}, bf16[1,512,1024]{2,1,0:T(8,128)(2,1)S(1)}, u32[]{:S(2)}, u32[]{:S(2)}) collective-permute-start(bf16[1,512,1024]{2,1,0:T(8,128)(2,1)} %pick.11.rest_0_), channel_id=1, source_target_pairs={{0,12},{2,14},{4,8},{6,10},{8,4},{10,6},{12,0},{14,2},{1,13},{3,15... | collective-permute-start | bytes 3145736 | tf_op jit(solution)/shard_map/ppermute | solution.py:262
  84.2 2.2 copy-start.1
  86.4 1.6 copy-start.4
  88.0 1.6 copy-start.8
  89.6 6.1 %copy-start.12 = (bf16[2048,1024]{1,0:T(8,128)(2,1)S(1)}, bf16[2048,1024]{1,0:T(8,128)(2,1)}, u32[]{:S(2)}) copy-start(bf16[2048,1024]{1,0:T(8,128)(2,1)} %cand_ref.1) | copy-start | bytes 12582916
  94.1 3.1 %copy-start.18 = (bf16[1,512,512]{2,1,0:T(8,128)(2,1)S(1)}, bf16[1,512,512]{2,1,0:T(8,128)(2,1)}, u32[]{:S(2)}) copy-start(bf16[1,512,512]{2,1,0:T(8,128)(2,1)} %get-tuple-element.37) | copy-start | bytes 1572868
  94.1 14.7 %collective-permute-start.3 = (bf16[528,512]{1,0:T(8,128)(2,1)S(1)}, bf16[528,512]{1,0:T(8,128)(2,1)S(1)}, u32[]{:S(2)}, u32[]{:S(2)}) collective-permute-start(bf16[528,512]{1,0:T(8,128)(2,1)S(1)} %attend.12.refs_6_.refs_4_), channel_id=1, source_target_pairs={{0,1},{1,0},{2,3},{3,2},{4,5},{5,4},{6,7},{7,6},{8,9},{9,8},{10,11... | collective-permute-start | bytes 1622024 | tf_op jit(solution)/shard_map/ppermute | solution.py:278
  97.2 1.4 copy-start.15
  98.4 4.8 %copy-start.5 = (bf16[2048,512]{1,0:T(8,128)(2,1)S(1)}, bf16[2048,512]{1,0:T(8,128)(2,1)}, u32[]{:S(2)}) copy-start(bf16[2048,512]{1,0:T(8,128)(2,1)} %copy-done.2) | copy-start | bytes 6291460
  98.5 4.8 %copy-start.9 = (bf16[2048,512]{1,0:T(8,128)(2,1)S(1)}, bf16[2048,512]{1,0:T(8,128)(2,1)}, u32[]{:S(2)}) copy-start(bf16[2048,512]{1,0:T(8,128)(2,1)} %copy-done.6) | copy-start | bytes 6291460
  98.6 38.6 %collective-permute-start.10 = (bf16[1,512,1024]{2,1,0:T(8,128)(2,1)S(1)}, bf16[1,512,1024]{2,1,0:T(8,128)(2,1)S(1)}, u32[]{:S(2)}, u32[]{:S(2)}) collective-permute-start(bf16[1,512,1024]{2,1,0:T(8,128)(2,1)S(1)} %copy-done.15), channel_id=1, source_target_pairs={{0,4},{2,6},{4,0},{6,2},{8,12},{10,14},{12,8},{14,10},{1,5},{3,7},... | collective-permute-start | bytes 3145736 | tf_op jit(solution)/shard_map/ppermute | solution.py:262
  103.3 5.5 %copy-start.14 = (bf16[1,512,1024]{2,1,0:T(8,128)(2,1)S(1)}, bf16[1,512,1024]{2,1,0:T(8,128)(2,1)}, u32[]{:S(2)}) copy-start(bf16[1,512,1024]{2,1,0:T(8,128)(2,1)} %pick.13.rest_0_) | copy-start | bytes 3145732
  107.5 14.2 %collective-permute-start.5 = (bf16[528,512]{1,0:T(8,128)(2,1)S(1)}, bf16[528,512]{1,0:T(8,128)(2,1)S(1)}, u32[]{:S(2)}, u32[]{:S(2)}) collective-permute-start(bf16[528,512]{1,0:T(8,128)(2,1)S(1)} %attend.13.refs_6_.refs_4_), channel_id=1, source_target_pairs={{0,1},{1,0},{2,3},{3,2},{4,5},{5,4},{6,7},{7,6},{8,9},{9,8},{10,11... | collective-permute-start | bytes 1622024 | tf_op jit(solution)/shard_map/ppermute | solution.py:278
  108.8 77.2 %collective-permute-start.12 = (bf16[1,512,1024]{2,1,0:T(8,128)(2,1)S(1)}, bf16[1,512,1024]{2,1,0:T(8,128)(2,1)S(1)}, u32[]{:S(2)}, u32[]{:S(2)}) collective-permute-start(bf16[1,512,1024]{2,1,0:T(8,128)(2,1)S(1)} %copy-done.14), channel_id=1, source_target_pairs={{0,10},{2,8},{4,14},{6,12},{8,2},{10,0},{12,6},{14,4},{1,11},{3,9}... | collective-permute-start | bytes 3145736 | tf_op jit(solution)/shard_map/ppermute | solution.py:262
  115.7 17.5 %collective-permute-start.7 = (bf16[528,512]{1,0:T(8,128)(2,1)S(1)}, bf16[528,512]{1,0:T(8,128)(2,1)S(1)}, u32[]{:S(2)}, u32[]{:S(2)}) collective-permute-start(bf16[528,512]{1,0:T(8,128)(2,1)S(1)} %attend.14.refs_6_.refs_4_), channel_id=1, source_target_pairs={{0,1},{1,0},{2,3},{3,2},{4,5},{5,4},{6,7},{7,6},{8,9},{9,8},{10,11... | collective-permute-start | bytes 1622024 | tf_op jit(solution)/shard_map/ppermute | solution.py:278
  127.4 20.6 %collective-permute-start.9 = (bf16[528,512]{1,0:T(8,128)(2,1)S(1)}, bf16[528,512]{1,0:T(8,128)(2,1)S(1)}, u32[]{:S(2)}, u32[]{:S(2)}) collective-permute-start(bf16[528,512]{1,0:T(8,128)(2,1)S(1)} %attend.15.refs_6_.refs_4_), channel_id=1, source_target_pairs={{0,1},{1,0},{2,3},{3,2},{4,5},{5,4},{6,7},{7,6},{8,9},{9,8},{10,11... | collective-permute-start | bytes 1622024 | tf_op jit(solution)/shard_map/ppermute | solution.py:278
  137.2 4.8 %copy-start.17 = (bf16[1,512,512]{2,1,0:T(8,128)(2,1)S(1)}, bf16[1,512,512]{2,1,0:T(8,128)(2,1)}, u32[]{:S(2)}) copy-start(bf16[1,512,512]{2,1,0:T(8,128)(2,1)} %pick.14.rest_0_) | copy-start | bytes 1572868
  141.3 50.2 %collective-permute-start.11 = (bf16[528,512]{1,0:T(8,128)(2,1)S(1)}, bf16[528,512]{1,0:T(8,128)(2,1)S(1)}, u32[]{:S(2)}, u32[]{:S(2)}) collective-permute-start(bf16[528,512]{1,0:T(8,128)(2,1)S(1)} %attend.16.refs_6_.refs_4_), channel_id=1, source_target_pairs={{0,1},{1,0},{2,3},{3,2},{4,5},{5,4},{6,7},{7,6},{8,9},{9,8},{10,11... | collective-permute-start | bytes 1622024 | tf_op jit(solution)/shard_map/ppermute | solution.py:278
  141.9 68.9 %collective-permute-start.14 = (bf16[1,512,512]{2,1,0:T(8,128)(2,1)S(1)}, bf16[1,512,512]{2,1,0:T(8,128)(2,1)S(1)}, u32[]{:S(2)}, u32[]{:S(2)}) collective-permute-start(bf16[1,512,512]{2,1,0:T(8,128)(2,1)S(1)} %copy-done.17), channel_id=1, source_target_pairs={{0,8},{2,10},{4,12},{6,14},{8,0},{10,2},{12,4},{14,6},{1,9},{3,11}... | collective-permute-start | bytes 1572872 | tf_op jit(solution)/shard_map/ppermute | solution.py:262
  151.9 38.7 %copy-start.16 = (bf16[1,512,512]{2,1,0:T(8,128)(2,1)S(1)}, bf16[1,512,512]{2,1,0:T(8,128)(2,1)}, u32[]{:S(2)}) copy-start(bf16[1,512,512]{2,1,0:T(8,128)(2,1)} %pick.15.rest_0_) | copy-start | bytes 1572868
  189.1 25.7 %collective-permute-start.13 = (bf16[528,512]{1,0:T(8,128)(2,1)S(1)}, bf16[528,512]{1,0:T(8,128)(2,1)S(1)}, u32[]{:S(2)}, u32[]{:S(2)}) collective-permute-start(bf16[528,512]{1,0:T(8,128)(2,1)S(1)} %attend.17.refs_6_.refs_4_), channel_id=1, source_target_pairs={{0,1},{1,0},{2,3},{3,2},{4,5},{5,4},{6,7},{7,6},{8,9},{9,8},{10,11... | collective-permute-start | bytes 1622024 | tf_op jit(solution)/shard_map/ppermute | solution.py:278
  190.6 30.2 %collective-permute-start.16 = (bf16[1,512,512]{2,1,0:T(8,128)(2,1)S(1)}, bf16[1,512,512]{2,1,0:T(8,128)(2,1)S(1)}, u32[]{:S(2)}, u32[]{:S(2)}) collective-permute-start(bf16[1,512,512]{2,1,0:T(8,128)(2,1)S(1)} %copy-done.16), channel_id=1, source_target_pairs={{0,8},{2,10},{4,12},{6,14},{8,0},{10,2},{12,4},{14,6},{1,9},{3,11}... | collective-permute-start | bytes 1572872 | tf_op jit(solution)/shard_map/ppermute | solution.py:262
  213.2 14.6 %collective-permute-start.15 = (bf16[528,256]{1,0:T(8,128)(2,1)S(1)}, bf16[528,256]{1,0:T(8,128)(2,1)S(1)}, u32[]{:S(2)}, u32[]{:S(2)}) collective-permute-start(bf16[528,256]{1,0:T(8,128)(2,1)S(1)} %attend.18.refs_6_.refs_4_), channel_id=1, source_target_pairs={{0,1},{1,0},{2,3},{3,2},{4,5},{5,4},{6,7},{7,6},{8,9},{9,8},{10,11... | collective-permute-start | bytes 811016 | tf_op jit(solution)/shard_map/ppermute | solution.py:278
  222.1 5.7 %collective-permute-start.17 = (bf16[176,256]{1,0:T(8,128)(2,1)S(1)}, bf16[176,256]{1,0:T(8,128)(2,1)S(1)}, u32[]{:S(2)}, u32[]{:S(2)}) collective-permute-start(bf16[176,256]{1,0:T(8,128)(2,1)S(1)} %attend.19.refs_6_), channel_id=1, source_target_pairs={{0,1},{1,0},{2,3},{3,2},{4,5},{5,4},{6,7},{7,6},{8,9},{9,8},{10,11... | collective-permute-start | bytes 270344 | tf_op jit(solution)/shard_map/ppermute | solution.py:278
  225.0 5.3 %collective-permute-start.18 = (bf16[176,256]{1,0:T(8,128)(2,1)S(1)}, bf16[176,256]{1,0:T(8,128)(2,1)S(1)}, u32[]{:S(2)}, u32[]{:S(2)}) collective-permute-start(bf16[176,256]{1,0:T(8,128)(2,1)S(1)} %attend.20.refs_6_), channel_id=1, source_target_pairs={{0,1},{1,0},{2,3},{3,2},{4,5},{5,4},{6,7},{7,6},{8,9},{9,8},{10,11... | collective-permute-start | bytes 270344 | tf_op jit(solution)/shard_map/ppermute | solution.py:278
  226.2 6.6 %collective-permute-start.19 = (bf16[176,256]{1,0:T(8,128)(2,1)S(1)}, bf16[176,256]{1,0:T(8,128)(2,1)S(1)}, u32[]{:S(2)}, u32[]{:S(2)}) collective-permute-start(bf16[176,256]{1,0:T(8,128)(2,1)S(1)} %attend.21.refs_8_.refs_6_), channel_id=1, source_target_pairs={{0,1},{1,0},{2,3},{3,2},{4,5},{5,4},{6,7},{7,6},{8,9},{9,8},{10,11... | collective-permute-start | bytes 270344 | tf_op jit(solution)/shard_map/ppermute | solution.py:278

commit v3 on v2

--- a/solution.py
+++ b/solution.py
@@ -197,12 +197,12 @@
 def pick(place, table, count, kv_cache, m, side, sides, after):
     user = lambda i, place, table: (table[jnp.bitwise_xor(place[0], m) * count + place[0]], i, side)
     tokens, kvw = kv_cache.shape[1], kv_cache.shape[2] // sides
-    block = (1, tokens // 4, kvw)
+    block = (1, tokens, kvw)
     return pl.pallas_call(
         pick_kernel,
         grid_spec=pltpu.PrefetchScalarGridSpec(
             num_scalar_prefetch=2,
-            grid=(4,),
+            grid=(1,),
             in_specs=[pl.BlockSpec(block, user)] + [pl.BlockSpec(memory_space=pl.ANY)] * len(after),
             out_specs=pl.BlockSpec(block, lambda i, place, table: (0, i, 0)),
         ),
@@ -277,6 +277,7 @@
     def to_peer(value, k):
         return lax.ppermute(value, "head", [(i, (i + k) % ways) for i in range(ways)])
 
+    w_out, _ = lax.optimization_barrier((w_out, after[0]))
     turned = []
     for k in range(ways):
         piece = lax.dynamic_slice_in_dim(w_out, ((side + k) % ways) * columns, columns, 1)

time: 237 us -> 219 us (0.924)
  Pallas kernels: 116 us -> 107 us
  local copies, waits for them, and re-layouts: 19.7 us -> 11.1 us
    pallas_call x9, Pallas kernels: 36.2 us -> 25.8 us  [pick(): pl.pallas_call(pick_kernel, grid_spec=pltpu.PrefetchScalarGridSpec(num_sc...]
    unnamed x42 -> x32, local copies, waits for them, and re-layouts: 17 us -> 8.32 us
where the time goes in v3:
time: 219 us; the launch traced here: 218 us
  Pallas kernels  107 us (49%)
  waiting for transfers between devices  60.8 us (28%)
  starting transfers between devices  25.7 us (12%)
  blocking collectives  11.2 us (5%)
  local copies, waits for them, and re-layouts  11.1 us (5%)
  other arithmetic  2.37 us (1%)
    ppermute x8, waiting for transfers between devices, per_device(): picked = lax.ppermute(picked, 'req', [(i, i ^ m) for i in range(count)])  51.2 us
    pallas_call x10, Pallas kernels, finish(): pl.pallas_call(lambda *refs: finish_kernel(m, offset, slots, *refs), grid...  35.1 us
    pallas_call x11, Pallas kernels, attend(): pl.pallas_call(lambda *refs: attend_kernel(m, offset, *refs), grid_spec=p...  30.6 us
    pallas_call x9, Pallas kernels, pick(): pl.pallas_call(pick_kernel, grid_spec=pltpu.PrefetchScalarGridSpec(num_sc...  25.8 us
    pallas_call x1, Pallas kernels, project(): pl.pallas_call(project_kernel, grid=(rows // tile,), in_specs=[pl.BlockSp...  15.1 us
    ppermute x12, starting transfers between devices, to_peer(): lax.ppermute(value, 'head', [(i, (i + k) % ways) for i in range(ways)])  13.3 us
    ppermute x8, starting transfers between devices, per_device(): picked = lax.ppermute(picked, 'req', [(i, i ^ m) for i in range(count)])  12.4 us
    psum x1, blocking collectives, per_device(): table = lax.psum(spread.reshape(-1), 'req')  11.2 us
  transfers between devices with their start and end apart: 20, of which 6 were waited for; matrix products, arithmetic and copies ran while one was open for 2% of the time, Pallas kernels for 46%

profile of v3, /device:TPU:0, one launch (start us, length us, event | category | flops | bytes accessed | tf_op | source)
XLA Modules:
  0.0 218.0 jit_solution(446790909037051975)
XLA Ops:
  1.0 11.2 %psum.7.table = s32[64]{0:T(128)} all-reduce(s32[64]{0:T(128)S(1)} %select_n.54), channel_id=1, replica_groups=mesh['groups'=2,'req'=8,'head'=2,'rep'=1] {'req'}, use_global_device_ids=true, to_apply=%region_6.7 | all-reduce | flops 64 | bytes 512 | tf_op jit(solution)/shard_map/psum | solution.py:248
  12.2 2.9 %pick.9.rest_0_ = bf16[1,512,1024]{2,1,0:T(8,128)(2,1)} custom-call(s32[1]{0:T(128)} %bitcast.place.refs_0_, s32[64]{0:T(128)} %psum.7.table, bf16[8,512,1024]{2,1,0:T(8,128)(2,1)} %kv_ref.17), custom_call_target="tpu_custom_call" | custom-call | tf_op jit(solution)/shard_map/pick/pallas_call | solution.py:201
  15.2 2.9 %pick.10.rest_0_ = bf16[1,512,1024]{2,1,0:T(8,128)(2,1)} custom-call(s32[1]{0:T(128)} %bitcast.place.refs_0_, s32[64]{0:T(128)} %psum.7.table, bf16[8,512,1024]{2,1,0:T(8,128)(2,1)} %kv_ref.17, bf16[1,512,1024]{2,1,0:T(8,128)(2,1)} %pick.9.rest_0_), custom_call_target="tpu_custom_call" | custom-call | tf_op jit(solution)/shard_map/pick/pallas_call | solution.py:201
  18.7 3.0 %pick.11.rest_0_ = bf16[1,512,1024]{2,1,0:T(8,128)(2,1)} custom-call(s32[1]{0:T(128)} %bitcast.place.refs_0_, s32[64]{0:T(128)} %psum.7.table, bf16[8,512,1024]{2,1,0:T(8,128)(2,1)} %kv_ref.17, bf16[1,512,1024]{2,1,0:T(8,128)(2,1)} %pick.10.rest_0_), custom_call_target="tpu_custom_call" | custom-call | tf_op jit(solution)/shard_map/pick/pallas_call | solution.py:201
  21.7 3.0 %pick.12.rest_0_ = bf16[1,512,1024]{2,1,0:T(8,128)(2,1)} custom-call(s32[1]{0:T(128)} %bitcast.place.refs_0_, s32[64]{0:T(128)} %psum.7.table, bf16[8,512,1024]{2,1,0:T(8,128)(2,1)} %kv_ref.17, bf16[1,512,1024]{2,1,0:T(8,128)(2,1)} %pick.11.rest_0_), custom_call_target="tpu_custom_call" | custom-call | tf_op jit(solution)/shard_map/pick/pallas_call | solution.py:201
  24.7 3.0 %pick.13.rest_0_ = bf16[1,512,1024]{2,1,0:T(8,128)(2,1)} custom-call(s32[1]{0:T(128)} %bitcast.place.refs_0_, s32[64]{0:T(128)} %psum.7.table, bf16[8,512,1024]{2,1,0:T(8,128)(2,1)} %kv_ref.17, bf16[1,512,1024]{2,1,0:T(8,128)(2,1)} %pick.12.rest_0_), custom_call_target="tpu_custom_call" | custom-call | tf_op jit(solution)/shard_map/pick/pallas_call | solution.py:201
  27.7 2.5 %pick.14.rest_0_ = bf16[1,512,512]{2,1,0:T(8,128)(2,1)} custom-call(s32[1]{0:T(128)} %bitcast.place.refs_0_, s32[64]{0:T(128)} %psum.7.table, bf16[8,512,1024]{2,1,0:T(8,128)(2,1)} %kv_ref.17, bf16[1,512,1024]{2,1,0:T(8,128)(2,1)} %pick.13.rest_0_), custom_call_target="tpu_custom_call" | custom-call | tf_op jit(solution)/shard_map/pick/pallas_call | solution.py:201
  30.2 2.5 %pick.15.rest_0_ = bf16[1,512,512]{2,1,0:T(8,128)(2,1)} custom-call(s32[1]{0:T(128)} %bitcast.place.refs_0_, s32[64]{0:T(128)} %psum.7.table, bf16[8,512,1024]{2,1,0:T(8,128)(2,1)} %kv_ref.17, bf16[1,512,512]{2,1,0:T(8,128)(2,1)} %pick.14.rest_0_), custom_call_target="tpu_custom_call" | custom-call | tf_op jit(solution)/shard_map/pick/pallas_call | solution.py:201
  32.7 2.9 %pick.16.rest_0_ = bf16[1,512,1024]{2,1,0:T(8,128)(2,1)} custom-call(s32[1]{0:T(128)} %bitcast.place.refs_0_, s32[64]{0:T(128)} %psum.7.table, bf16[8,512,1024]{2,1,0:T(8,128)(2,1)} %kv_ref.17, bf16[1,512,512]{2,1,0:T(8,128)(2,1)} %pick.15.rest_0_), custom_call_target="tpu_custom_call" | custom-call | tf_op jit(solution)/shard_map/pick/pallas_call | solution.py:201
  36.0 3.0 %pick.17.refs_5_ = bf16[1,512,1024]{2,1,0:T(8,128)(2,1)} custom-call(s32[1]{0:T(128)} %bitcast.place.refs_0_, s32[64]{0:T(128)} %psum.7.table, bf16[8,512,1024]{2,1,0:T(8,128)(2,1)} %kv_ref.17, bf16[1,512,1024]{2,1,0:T(8,128)(2,1)} %pick.16.rest_0_), custom_call_target="tpu_custom_call" | custom-call | tf_op jit(solution)/shard_map/pick/pallas_call | solution.py:201
  40.1 1.5 collective-permute-start
  41.6 2.2 %copy-done.6 = bf16[2048,1024]{1,0:T(8,128)(2,1)S(1)} copy-done((bf16[2048,1024]{1,0:T(8,128)(2,1)S(1)}, bf16[2048,1024]{1,0:T(8,128)(2,1)}, u32[]{:S(2)}) %copy-start.6) | copy-done | bytes 4194328
  43.8 2.2 %copy-done.8 = bf16[1024,2048]{1,0:T(8,128)(2,1)S(1)} copy-done((bf16[1024,2048]{1,0:T(8,128)(2,1)S(1)}, bf16[1024,2048]{1,0:T(8,128)(2,1)}, u32[]{:S(2)}) %copy-start.8) | copy-done | bytes 4194328
  46.0 15.1 %project.1 = (bf16[2048,512]{1,0:T(8,128)(2,1)S(1)}, bf16[2048,512]{1,0:T(8,128)(2,1)S(1)}, f32[2048,512]{1,0:T(8,128)S(1)}) custom-call(bf16[2048,1024]{1,0:T(8,128)(2,1)S(1)} %copy-done.6, bf16[1024,2048]{1,0:T(8,128)(2,1)S(1)} %copy-done.8), custom_call_target="tpu_custom_call" | custom-call | flops 8589934592 | bytes 16777216 | tf_op jit(solution)/shard_map/project/pallas_call | solution.py:52
  61.4 4.1 %attend.11.refs_4_ = bf16[528,512]{1,0:T(8,128)(2,1)S(1)} custom-call(s32[1]{0:T(128)} %bitcast.place.refs_0_, s32[4,8]{1,0:T(4,128)S(1)} %pad_add_fusion.refs_1_, bf16[2048,512]{1,0:T(8,128)(2,1)S(1)} %get-tuple-element.20.refs_2_, bf16[2048,512]{1,0:T(8,128)(2,1)S(1)} %get-tuple-element.21.refs_3_, f32[2048,512]{1,0:T(8,128)S(1)} %get-tuple-element.22.refs_4_, ...), custom_call_target="tpu_custom_call" | custom-call | flops 553648128 | bytes 3751936 | tf_op jit(solution)/shard_map/attend/pallas_call | solution.py:115
  67.2 2.2 %copy-done.1 = f32[2048,512]{1,0:T(8,128)S(1)} copy-done((f32[2048,512]{1,0:T(8,128)S(1)}, f32[2048,512]{1,0:T(8,128)}, u32[]{:S(2)}) %copy-start.1) | copy-done | bytes 4194328
  69.4 1.6 copy-done.3
  71.0 4.5 %attend.12.refs_6_.refs_4_ = bf16[528,512]{1,0:T(8,128)(2,1)S(1)} custom-call(s32[1]{0:T(128)} %bitcast.place.refs_0_, s32[4,8]{1,0:T(4,128)S(1)} %pad_add_fusion.refs_1_, bf16[2048,512]{1,0:T(8,128)(2,1)S(1)} %get-tuple-element.20.refs_2_, bf16[2048,512]{1,0:T(8,128)(2,1)S(1)} %copy-done.3, f32[2048,512]{1,0:T(8,128)S(1)} %copy-done.1, ...), custom_call_target="tpu_custom_call" | custom-call | flops 553648128 | bytes 3751936 | tf_op jit(solution)/shard_map/attend/pallas_call | solution.py:115
  75.5 1.6 collective-permute-start.3
  77.1 1.6 constant_dynamic-slice_fusion.1.refs_2_
  80.0 1.9 collective-permute-start.10
  81.8 3.9 %finish.10.refs_2_ = bf16[2048,512]{1,0:T(8,128)(2,1)} custom-call(s32[1]{0:T(128)} %bitcast.place.refs_0_, s32[4,8]{1,0:T(4,128)S(1)} %pad_add_fusion.refs_1_, bf16[2048,512]{1,0:T(8,128)(2,1)} %constant_dynamic-slice_fusion.1.refs_2_, bf16[2,512,512]{2,1,0:T(8,128)(2,1)S(1)} %pad_maximum_fusion.refs_3_, ...), custom_call_target="tpu_custom_call", output_to_operand_aliasing={{}: (2, {})} | custom-call | flops 553648128 | bytes 3211264 | tf_op jit(solution)/shard_map/finish/pallas_call | solution.py:166
  85.8 4.2 %attend.13.refs_6_.refs_4_ = bf16[528,512]{1,0:T(8,128)(2,1)S(1)} custom-call(s32[1]{0:T(128)} %bitcast.place.refs_0_, s32[4,8]{1,0:T(4,128)S(1)} %pad_add_fusion.refs_1_, bf16[2048,512]{1,0:T(8,128)(2,1)S(1)} %get-tuple-element.20.refs_2_, bf16[2048,512]{1,0:T(8,128)(2,1)S(1)} %copy-done.4, f32[2048,512]{1,0:T(8,128)S(1)} %copy-done.1, ...), custom_call_target="tpu_custom_call" | custom-call | flops 553648128 | bytes 3751936 | tf_op jit(solution)/shard_map/attend/pallas_call | solution.py:115
  91.4 3.9 %finish.11.refs_2_ = bf16[2048,512]{1,0:T(8,128)(2,1)} custom-call(s32[1]{0:T(128)} %bitcast.place.refs_0_, s32[4,8]{1,0:T(4,128)S(1)} %pad_add_fusion.refs_1_, bf16[2048,512]{1,0:T(8,128)(2,1)} %finish.10.refs_2_, bf16[2,512,512]{2,1,0:T(8,128)(2,1)S(1)} %pad_maximum_fusion.refs_3_, ...), custom_call_target="tpu_custom_call", output_to_operand_aliasing={{}: (2, {})} | custom-call | flops 553648128 | bytes 3211264 | tf_op jit(solution)/shard_map/finish/pallas_call | solution.py:166
  95.4 3.0 %attend.14.refs_6_.refs_4_ = bf16[528,512]{1,0:T(8,128)(2,1)S(1)} custom-call(s32[1]{0:T(128)} %bitcast.place.refs_0_, s32[4,8]{1,0:T(4,128)S(1)} %pad_add_fusion.refs_1_, bf16[2048,512]{1,0:T(8,128)(2,1)S(1)} %get-tuple-element.20.refs_2_, bf16[2048,512]{1,0:T(8,128)(2,1)S(1)} %copy-done.4, f32[2048,512]{1,0:T(8,128)S(1)} %copy-done.1, ...), custom_call_target="tpu_custom_call" | custom-call | flops 553648128 | bytes 3751936 | tf_op jit(solution)/shard_map/attend/pallas_call | solution.py:115
  98.4 1.6 collective-permute-start.7
  100.0 4.5 %collective-permute-done.5.refs_5_ = bf16[528,512]{1,0:T(8,128)(2,1)S(1)} collective-permute-done((bf16[528,512]{1,0:T(8,128)(2,1)S(1)}, bf16[528,512]{1,0:T(8,128)(2,1)S(1)}, u32[]{:S(2)}, u32[]{:S(2)}) %collective-permute-start.5) | collective-permute-done | bytes 540704 | tf_op jit(solution)/shard_map/ppermute | solution.py:278
  104.5 3.9 %finish.12.refs_2_ = bf16[2048,512]{1,0:T(8,128)(2,1)} custom-call(s32[1]{0:T(128)} %bitcast.place.refs_0_, s32[4,8]{1,0:T(4,128)S(1)} %pad_add_fusion.refs_1_, bf16[2048,512]{1,0:T(8,128)(2,1)} %finish.11.refs_2_, bf16[2,512,512]{2,1,0:T(8,128)(2,1)S(1)} %pad_maximum_fusion.refs_3_, ...), custom_call_target="tpu_custom_call", output_to_operand_aliasing={{}: (2, {})} | custom-call | flops 553648128 | bytes 3211264 | tf_op jit(solution)/shard_map/finish/pallas_call | solution.py:166
  108.4 1.8 attend.15.refs_6_.refs_4_
  110.9 4.7 %collective-permute-done.7.refs_5_ = bf16[528,512]{1,0:T(8,128)(2,1)S(1)} collective-permute-done((bf16[528,512]{1,0:T(8,128)(2,1)S(1)}, bf16[528,512]{1,0:T(8,128)(2,1)S(1)}, u32[]{:S(2)}, u32[]{:S(2)}) %collective-permute-start.7) | collective-permute-done | bytes 540704 | tf_op jit(solution)/shard_map/ppermute | solution.py:278
  115.6 3.9 %finish.13.refs_2_ = bf16[2048,512]{1,0:T(8,128)(2,1)} custom-call(s32[1]{0:T(128)} %bitcast.place.refs_0_, s32[4,8]{1,0:T(4,128)S(1)} %pad_add_fusion.refs_1_, bf16[2048,512]{1,0:T(8,128)(2,1)} %finish.12.refs_2_, bf16[2,512,512]{2,1,0:T(8,128)(2,1)S(1)} %pad_maximum_fusion.refs_3_, ...), custom_call_target="tpu_custom_call", output_to_operand_aliasing={{}: (2, {})} | custom-call | flops 553648128 | bytes 3211264 | tf_op jit(solution)/shard_map/finish/pallas_call | solution.py:166
  119.5 4.1 %attend.16.refs_6_.refs_4_ = bf16[528,512]{1,0:T(8,128)(2,1)S(1)} custom-call(s32[1]{0:T(128)} %bitcast.place.refs_0_, s32[4,8]{1,0:T(4,128)S(1)} %pad_add_fusion.refs_1_, bf16[2048,512]{1,0:T(8,128)(2,1)S(1)} %get-tuple-element.20.refs_2_, bf16[2048,512]{1,0:T(8,128)(2,1)S(1)} %copy-done.4, f32[2048,512]{1,0:T(8,128)S(1)} %copy-done.1, ...), custom_call_target="tpu_custom_call" | custom-call | flops 553648128 | bytes 3751936 | tf_op jit(solution)/shard_map/attend/pallas_call | solution.py:115
  124.4 6.3 %collective-permute-start.14 = (bf16[1,512,512]{2,1,0:T(8,128)(2,1)S(1)}, bf16[1,512,512]{2,1,0:T(8,128)(2,1)S(1)}, u32[]{:S(2)}, u32[]{:S(2)}) collective-permute-start(bf16[1,512,512]{2,1,0:T(8,128)(2,1)S(1)} %copy-done.12), channel_id=1, source_target_pairs={{0,8},{2,10},{4,12},{6,14},{8,0},{10,2},{12,4},{14,6},{1,9},{3,11}... | collective-permute-start | bytes 1572872 | tf_op jit(solution)/shard_map/ppermute | solution.py:262
  130.7 3.9 %finish.14.refs_2_ = bf16[2048,512]{1,0:T(8,128)(2,1)} custom-call(s32[1]{0:T(128)} %bitcast.place.refs_0_, s32[4,8]{1,0:T(4,128)S(1)} %pad_add_fusion.refs_1_, bf16[2048,512]{1,0:T(8,128)(2,1)} %finish.13.refs_2_, bf16[2,512,512]{2,1,0:T(8,128)(2,1)S(1)} %pad_maximum_fusion.refs_3_, ...), custom_call_target="tpu_custom_call", output_to_operand_aliasing={{}: (2, {})} | custom-call | flops 553648128 | bytes 3211264 | tf_op jit(solution)/shard_map/finish/pallas_call | solution.py:166
  134.6 33.7 %collective-permute-done.12.refs_5_ = bf16[1,512,1024]{2,1,0:T(8,128)(2,1)S(1)} collective-permute-done((bf16[1,512,1024]{2,1,0:T(8,128)(2,1)S(1)}, bf16[1,512,1024]{2,1,0:T(8,128)(2,1)S(1)}, u32[]{:S(2)}, u32[]{:S(2)}) %collective-permute-start.12) | collective-permute-done | bytes 1048608 | tf_op jit(solution)/shard_map/ppermute | solution.py:262
  168.4 3.0 %attend.17.refs_6_.refs_4_ = bf16[528,512]{1,0:T(8,128)(2,1)S(1)} custom-call(s32[1]{0:T(128)} %bitcast.place.refs_0_, s32[4,8]{1,0:T(4,128)S(1)} %pad_add_fusion.refs_1_, bf16[2048,512]{1,0:T(8,128)(2,1)S(1)} %get-tuple-element.20.refs_2_, bf16[2048,512]{1,0:T(8,128)(2,1)S(1)} %copy-done.4, f32[2048,512]{1,0:T(8,128)S(1)} %copy-done.1, ...), custom_call_target="tpu_custom_call" | custom-call | flops 553648128 | bytes 3751936 | tf_op jit(solution)/shard_map/attend/pallas_call | solution.py:115
  171.3 1.5 collective-permute-start.13
  173.9 3.9 %finish.15.refs_2_ = bf16[2048,512]{1,0:T(8,128)(2,1)} custom-call(s32[1]{0:T(128)} %bitcast.place.refs_0_, s32[4,8]{1,0:T(4,128)S(1)} %pad_add_fusion.refs_1_, bf16[2048,512]{1,0:T(8,128)(2,1)} %finish.14.refs_2_, bf16[2,512,512]{2,1,0:T(8,128)(2,1)S(1)} %pad_maximum_fusion.refs_3_, ...), custom_call_target="tpu_custom_call", output_to_operand_aliasing={{}: (2, {})} | custom-call | flops 553648128 | bytes 3211264 | tf_op jit(solution)/shard_map/finish/pallas_call | solution.py:166
  177.9 15.7 %collective-permute-done.14.refs_5_ = bf16[1,512,512]{2,1,0:T(8,128)(2,1)S(1)} collective-permute-done((bf16[1,512,512]{2,1,0:T(8,128)(2,1)S(1)}, bf16[1,512,512]{2,1,0:T(8,128)(2,1)S(1)}, u32[]{:S(2)}, u32[]{:S(2)}) %collective-permute-start.14) | collective-permute-done | bytes 524320 | tf_op jit(solution)/shard_map/ppermute | solution.py:262
  193.5 2.6 %attend.18.refs_6_.refs_4_ = bf16[528,256]{1,0:T(8,128)(2,1)S(1)} custom-call(s32[1]{0:T(128)} %bitcast.place.refs_0_, s32[4,8]{1,0:T(4,128)S(1)} %pad_add_fusion.refs_1_, bf16[2048,512]{1,0:T(8,128)(2,1)S(1)} %get-tuple-element.20.refs_2_, bf16[2048,512]{1,0:T(8,128)(2,1)S(1)} %copy-done.4, f32[2048,512]{1,0:T(8,128)S(1)} %copy-done.1, ...), custom_call_target="tpu_custom_call" | custom-call | flops 276824064 | bytes 1875968 | tf_op jit(solution)/shard_map/attend/pallas_call | solution.py:115
  196.2 1.5 collective-permute-start.15
  197.6 3.9 %finish.16.refs_2_ = bf16[2048,512]{1,0:T(8,128)(2,1)} custom-call(s32[1]{0:T(128)} %bitcast.place.refs_0_, s32[4,8]{1,0:T(4,128)S(1)} %pad_add_fusion.refs_1_, bf16[2048,512]{1,0:T(8,128)(2,1)} %finish.15.refs_2_, bf16[2,512,512]{2,1,0:T(8,128)(2,1)S(1)} %pad_maximum_fusion.refs_3_, ...), custom_call_target="tpu_custom_call", output_to_operand_aliasing={{}: (2, {})} | custom-call | flops 553648128 | bytes 3211264 | tf_op jit(solution)/shard_map/finish/pallas_call | solution.py:166
  201.6 1.8 collective-permute-done.16.refs_5_
  204.8 1.5 collective-permute-start.17
  208.9 1.5 collective-permute-start.19
  210.4 2.5 %finish.17.refs_2_ = bf16[2048,512]{1,0:T(8,128)(2,1)} custom-call(s32[1]{0:T(128)} %bitcast.place.refs_0_, s32[4,8]{1,0:T(4,128)S(1)} %pad_add_fusion.refs_1_, bf16[2048,512]{1,0:T(8,128)(2,1)} %finish.16.refs_2_, bf16[2,512,512]{2,1,0:T(8,128)(2,1)S(1)} %pad_maximum_fusion.refs_3_, ...), custom_call_target="tpu_custom_call", output_to_operand_aliasing={{}: (2, {})} | custom-call | flops 184549376 | bytes 1769472 | tf_op jit(solution)/shard_map/finish/pallas_call | solution.py:166
  212.9 2.5 %finish.18.refs_2_ = bf16[2048,512]{1,0:T(8,128)(2,1)} custom-call(s32[1]{0:T(128)} %bitcast.place.refs_0_, s32[4,8]{1,0:T(4,128)S(1)} %pad_add_fusion.refs_1_, bf16[2048,512]{1,0:T(8,128)(2,1)} %finish.17.refs_2_, bf16[2,512,512]{2,1,0:T(8,128)(2,1)S(1)} %pad_maximum_fusion.refs_3_, ...), custom_call_target="tpu_custom_call", output_to_operand_aliasing={{}: (2, {})} | custom-call | flops 184549376 | bytes 1769472 | tf_op jit(solution)/shard_map/finish/pallas_call | solution.py:166
  215.4 2.5 %finish.19 = bf16[2048,512]{1,0:T(8,128)(2,1)} custom-call(s32[1]{0:T(128)} %bitcast.place.refs_0_, s32[4,8]{1,0:T(4,128)S(1)} %pad_add_fusion.refs_1_, bf16[2048,512]{1,0:T(8,128)(2,1)} %finish.18.refs_2_, bf16[2,512,512]{2,1,0:T(8,128)(2,1)S(1)} %pad_maximum_fusion.refs_3_, ...), custom_call_target="tpu_custom_call", output_to_operand_aliasing={{}: (2, {})} | custom-call | flops 184549376 | bytes 1769472 | tf_op jit(solution)/shard_map/finish/pallas_call | solution.py:166
  (67 shorter events, 14.2 us)
Async XLA Ops:
  15.2 70.6 %collective-permute-start.4 = (bf16[1,512,1024]{2,1,0:T(8,128)(2,1)}, bf16[1,512,1024]{2,1,0:T(8,128)(2,1)}, u32[]{:S(2)}, u32[]{:S(2)}) collective-permute-start(bf16[1,512,1024]{2,1,0:T(8,128)(2,1)} %pick.9.rest_0_), channel_id=1, source_target_pairs={{0,14},{2,12},{4,10},{6,8},{8,6},{10,4},{12,2},{14,0},{1,15},{3,13... | collective-permute-start | bytes 3145736 | tf_op jit(solution)/shard_map/ppermute | solution.py:262
  18.1 77.3 %collective-permute-start.6 = (bf16[1,512,1024]{2,1,0:T(8,128)(2,1)}, bf16[1,512,1024]{2,1,0:T(8,128)(2,1)}, u32[]{:S(2)}, u32[]{:S(2)}) collective-permute-start(bf16[1,512,1024]{2,1,0:T(8,128)(2,1)} %pick.10.rest_0_), channel_id=1, source_target_pairs={{0,6},{2,4},{4,2},{6,0},{8,14},{10,12},{12,10},{14,8},{1,7},{3,5},... | collective-permute-start | bytes 3145736 | tf_op jit(solution)/shard_map/ppermute | solution.py:262
  35.7 3.3 %copy-start.14 = (bf16[512,1024]{1,0:T(8,128)(2,1)S(1)}, bf16[512,1024]{1,0:T(8,128)(2,1)}, u32[]{:S(2)}) copy-start(bf16[512,1024]{1,0:T(8,128)(2,1)} %param.15) | copy-start | bytes 3145732
  35.7 30.4 %collective-permute-start.2 = (bf16[1,512,1024]{2,1,0:T(8,128)(2,1)}, bf16[1,512,1024]{2,1,0:T(8,128)(2,1)}, u32[]{:S(2)}, u32[]{:S(2)}) collective-permute-start(bf16[1,512,1024]{2,1,0:T(8,128)(2,1)} %pick.16.rest_0_), channel_id=1, source_target_pairs={{0,2},{2,0},{4,6},{6,4},{8,10},{10,8},{12,14},{14,12},{1,3},{3,1},... | collective-permute-start | bytes 3145736 | tf_op jit(solution)/shard_map/ppermute | solution.py:262
  40.1 21.3 %copy-start.5 = (bf16[1,512,1024]{2,1,0:T(8,128)(2,1)S(1)}, bf16[1,512,1024]{2,1,0:T(8,128)(2,1)}, u32[]{:S(2)}) copy-start(bf16[1,512,1024]{2,1,0:T(8,128)(2,1)} %pick.17.refs_5_) | copy-start | bytes 3145732
  40.1 35.4 %collective-permute-start = (bf16[512,512]{1,0:T(8,128)(2,1)}, bf16[512,512]{1,0:T(8,128)(2,1)}, u32[]{:S(2)}, u32[]{:S(2)}) collective-permute-start(bf16[512,512]{1,0:T(8,128)(2,1)} %get-tuple-element.40), channel_id=1, source_target_pairs={{0,1},{1,0},{2,3},{3,2},{4,5},{5,4},{6,7},{7,6},{8,9},{9,8},{10,11... | collective-permute-start | bytes 1572872 | tf_op jit(solution)/shard_map/ppermute | solution.py:278
  41.6 2.2 %copy-start.6 = (bf16[2048,1024]{1,0:T(8,128)(2,1)S(1)}, bf16[2048,1024]{1,0:T(8,128)(2,1)}, u32[]{:S(2)}) copy-start(bf16[2048,1024]{1,0:T(8,128)(2,1)} %cand_ref.1) | copy-start | bytes 12582916
  43.8 2.2 %copy-start.8 = (bf16[1024,2048]{1,0:T(8,128)(2,1)S(1)}, bf16[1024,2048]{1,0:T(8,128)(2,1)}, u32[]{:S(2)}) copy-start(bf16[1024,2048]{1,0:T(8,128)(2,1)} %w_ref.1) | copy-start | bytes 12582916
  46.0 15.1 %copy-start.15 = (s32[1,2048]{1,0:T(1,128)S(1)}, s32[1,2048]{1,0:T(1,128)}, u32[]{:S(2)}) copy-start(s32[1,2048]{1,0:T(1,128)} %param.9) | copy-start | bytes 24580
  61.1 4.4 %copy-start = (f32[2048,512]{1,0:T(8,128)}, f32[2048,512]{1,0:T(8,128)S(1)}, u32[]{:S(2)}) copy-start(f32[2048,512]{1,0:T(8,128)S(1)} %get-tuple-element.22.refs_4_) | copy-start | bytes 12582916
  61.1 4.4 %copy-start.2 = (bf16[2048,512]{1,0:T(8,128)(2,1)}, bf16[2048,512]{1,0:T(8,128)(2,1)S(1)}, u32[]{:S(2)}) copy-start(bf16[2048,512]{1,0:T(8,128)(2,1)S(1)} %get-tuple-element.21.refs_3_) | copy-start | bytes 6291460
  65.5 14.4 %collective-permute-start.1 = (bf16[528,512]{1,0:T(8,128)(2,1)S(1)}, bf16[528,512]{1,0:T(8,128)(2,1)S(1)}, u32[]{:S(2)}, u32[]{:S(2)}) collective-permute-start(bf16[528,512]{1,0:T(8,128)(2,1)S(1)} %attend.11.refs_4_), channel_id=1, source_target_pairs={{0,1},{1,0},{2,3},{3,2},{4,5},{5,4},{6,7},{7,6},{8,9},{9,8},{10,11... | collective-permute-start | bytes 1622024 | tf_op jit(solution)/shard_map/ppermute | solution.py:278
  66.1 42.3 %collective-permute-start.8 = (bf16[1,512,1024]{2,1,0:T(8,128)(2,1)}, bf16[1,512,1024]{2,1,0:T(8,128)(2,1)S(1)}, u32[]{:S(2)}, u32[]{:S(2)}) collective-permute-start(bf16[1,512,1024]{2,1,0:T(8,128)(2,1)} %pick.11.rest_0_), channel_id=1, source_target_pairs={{0,12},{2,14},{4,8},{6,10},{8,4},{10,6},{12,0},{14,2},{1,13},{3,15... | collective-permute-start | bytes 3145736 | tf_op jit(solution)/shard_map/ppermute | solution.py:262
  67.2 2.2 %copy-start.1 = (f32[2048,512]{1,0:T(8,128)S(1)}, f32[2048,512]{1,0:T(8,128)}, u32[]{:S(2)}) copy-start(f32[2048,512]{1,0:T(8,128)} %copy-done) | copy-start | bytes 12582916
  69.4 1.6 copy-start.3
  71.0 6.1 %copy-start.7 = (bf16[2048,1024]{1,0:T(8,128)(2,1)S(1)}, bf16[2048,1024]{1,0:T(8,128)(2,1)}, u32[]{:S(2)}) copy-start(bf16[2048,1024]{1,0:T(8,128)(2,1)} %cand_ref.1) | copy-start | bytes 12582916
  75.5 3.1 %copy-start.13 = (bf16[1,512,512]{2,1,0:T(8,128)(2,1)S(1)}, bf16[1,512,512]{2,1,0:T(8,128)(2,1)}, u32[]{:S(2)}) copy-start(bf16[1,512,512]{2,1,0:T(8,128)(2,1)} %get-tuple-element.39) | copy-start | bytes 1572868
  75.5 14.9 %collective-permute-start.3 = (bf16[528,512]{1,0:T(8,128)(2,1)S(1)}, bf16[528,512]{1,0:T(8,128)(2,1)S(1)}, u32[]{:S(2)}, u32[]{:S(2)}) collective-permute-start(bf16[528,512]{1,0:T(8,128)(2,1)S(1)} %attend.12.refs_6_.refs_4_), channel_id=1, source_target_pairs={{0,1},{1,0},{2,3},{3,2},{4,5},{5,4},{6,7},{7,6},{8,9},{9,8},{10,11... | collective-permute-start | bytes 1622024 | tf_op jit(solution)/shard_map/ppermute | solution.py:278
  78.6 1.4 copy-start.10
  79.8 5.9 %copy-start.4 = (bf16[2048,512]{1,0:T(8,128)(2,1)S(1)}, bf16[2048,512]{1,0:T(8,128)(2,1)}, u32[]{:S(2)}) copy-start(bf16[2048,512]{1,0:T(8,128)(2,1)} %copy-done.2) | copy-start | bytes 6291460
  80.0 39.5 %collective-permute-start.10 = (bf16[1,512,1024]{2,1,0:T(8,128)(2,1)S(1)}, bf16[1,512,1024]{2,1,0:T(8,128)(2,1)S(1)}, u32[]{:S(2)}, u32[]{:S(2)}) collective-permute-start(bf16[1,512,1024]{2,1,0:T(8,128)(2,1)S(1)} %copy-done.10), channel_id=1, source_target_pairs={{0,4},{2,6},{4,0},{6,2},{8,12},{10,14},{12,8},{14,10},{1,5},{3,7},... | collective-permute-start | bytes 3145736 | tf_op jit(solution)/shard_map/ppermute | solution.py:262
  85.8 4.6 %copy-start.9 = (bf16[1,512,1024]{2,1,0:T(8,128)(2,1)S(1)}, bf16[1,512,1024]{2,1,0:T(8,128)(2,1)}, u32[]{:S(2)}) copy-start(bf16[1,512,1024]{2,1,0:T(8,128)(2,1)} %pick.13.rest_0_) | copy-start | bytes 3145732
  90.0 14.5 %collective-permute-start.5 = (bf16[528,512]{1,0:T(8,128)(2,1)S(1)}, bf16[528,512]{1,0:T(8,128)(2,1)S(1)}, u32[]{:S(2)}, u32[]{:S(2)}) collective-permute-start(bf16[528,512]{1,0:T(8,128)(2,1)S(1)} %attend.13.refs_6_.refs_4_), channel_id=1, source_target_pairs={{0,1},{1,0},{2,3},{3,2},{4,5},{5,4},{6,7},{7,6},{8,9},{9,8},{10,11... | collective-permute-start | bytes 1622024 | tf_op jit(solution)/shard_map/ppermute | solution.py:278
  90.4 78.0 %collective-permute-start.12 = (bf16[1,512,1024]{2,1,0:T(8,128)(2,1)S(1)}, bf16[1,512,1024]{2,1,0:T(8,128)(2,1)S(1)}, u32[]{:S(2)}, u32[]{:S(2)}) collective-permute-start(bf16[1,512,1024]{2,1,0:T(8,128)(2,1)S(1)} %copy-done.9), channel_id=1, source_target_pairs={{0,10},{2,8},{4,14},{6,12},{8,2},{10,0},{12,6},{14,4},{1,11},{3,9}... | collective-permute-start | bytes 3145736 | tf_op jit(solution)/shard_map/ppermute | solution.py:262
  98.4 17.2 %collective-permute-start.7 = (bf16[528,512]{1,0:T(8,128)(2,1)S(1)}, bf16[528,512]{1,0:T(8,128)(2,1)S(1)}, u32[]{:S(2)}, u32[]{:S(2)}) collective-permute-start(bf16[528,512]{1,0:T(8,128)(2,1)S(1)} %attend.14.refs_6_.refs_4_), channel_id=1, source_target_pairs={{0,1},{1,0},{2,3},{3,2},{4,5},{5,4},{6,7},{7,6},{8,9},{9,8},{10,11... | collective-permute-start | bytes 1622024 | tf_op jit(solution)/shard_map/ppermute | solution.py:278
  110.2 20.5 %collective-permute-start.9 = (bf16[528,512]{1,0:T(8,128)(2,1)S(1)}, bf16[528,512]{1,0:T(8,128)(2,1)S(1)}, u32[]{:S(2)}, u32[]{:S(2)}) collective-permute-start(bf16[528,512]{1,0:T(8,128)(2,1)S(1)} %attend.15.refs_6_.refs_4_), channel_id=1, source_target_pairs={{0,1},{1,0},{2,3},{3,2},{4,5},{5,4},{6,7},{7,6},{8,9},{9,8},{10,11... | collective-permute-start | bytes 1622024 | tf_op jit(solution)/shard_map/ppermute | solution.py:278
  119.5 4.9 %copy-start.12 = (bf16[1,512,512]{2,1,0:T(8,128)(2,1)S(1)}, bf16[1,512,512]{2,1,0:T(8,128)(2,1)}, u32[]{:S(2)}) copy-start(bf16[1,512,512]{2,1,0:T(8,128)(2,1)} %pick.14.rest_0_) | copy-start | bytes 1572868
  123.7 50.3 %collective-permute-start.11 = (bf16[528,512]{1,0:T(8,128)(2,1)S(1)}, bf16[528,512]{1,0:T(8,128)(2,1)S(1)}, u32[]{:S(2)}, u32[]{:S(2)}) collective-permute-start(bf16[528,512]{1,0:T(8,128)(2,1)S(1)} %attend.16.refs_6_.refs_4_), channel_id=1, source_target_pairs={{0,1},{1,0},{2,3},{3,2},{4,5},{5,4},{6,7},{7,6},{8,9},{9,8},{10,11... | collective-permute-start | bytes 1622024 | tf_op jit(solution)/shard_map/ppermute | solution.py:278
  124.4 69.1 %collective-permute-start.14 = (bf16[1,512,512]{2,1,0:T(8,128)(2,1)S(1)}, bf16[1,512,512]{2,1,0:T(8,128)(2,1)S(1)}, u32[]{:S(2)}, u32[]{:S(2)}) collective-permute-start(bf16[1,512,512]{2,1,0:T(8,128)(2,1)S(1)} %copy-done.12), channel_id=1, source_target_pairs={{0,8},{2,10},{4,12},{6,14},{8,0},{10,2},{12,4},{14,6},{1,9},{3,11}... | collective-permute-start | bytes 1572872 | tf_op jit(solution)/shard_map/ppermute | solution.py:262
  134.6 38.2 %copy-start.11 = (bf16[1,512,512]{2,1,0:T(8,128)(2,1)S(1)}, bf16[1,512,512]{2,1,0:T(8,128)(2,1)}, u32[]{:S(2)}) copy-start(bf16[1,512,512]{2,1,0:T(8,128)(2,1)} %pick.15.rest_0_) | copy-start | bytes 1572868
  171.3 26.3 %collective-permute-start.13 = (bf16[528,512]{1,0:T(8,128)(2,1)S(1)}, bf16[528,512]{1,0:T(8,128)(2,1)S(1)}, u32[]{:S(2)}, u32[]{:S(2)}) collective-permute-start(bf16[528,512]{1,0:T(8,128)(2,1)S(1)} %attend.17.refs_6_.refs_4_), channel_id=1, source_target_pairs={{0,1},{1,0},{2,3},{3,2},{4,5},{5,4},{6,7},{7,6},{8,9},{9,8},{10,11... | collective-permute-start | bytes 1622024 | tf_op jit(solution)/shard_map/ppermute | solution.py:278
  172.9 30.6 %collective-permute-start.16 = (bf16[1,512,512]{2,1,0:T(8,128)(2,1)S(1)}, bf16[1,512,512]{2,1,0:T(8,128)(2,1)S(1)}, u32[]{:S(2)}, u32[]{:S(2)}) collective-permute-start(bf16[1,512,512]{2,1,0:T(8,128)(2,1)S(1)} %copy-done.11), channel_id=1, source_target_pairs={{0,8},{2,10},{4,12},{6,14},{8,0},{10,2},{12,4},{14,6},{1,9},{3,11}... | collective-permute-start | bytes 1572872 | tf_op jit(solution)/shard_map/ppermute | solution.py:262
  196.2 14.2 %collective-permute-start.15 = (bf16[528,256]{1,0:T(8,128)(2,1)S(1)}, bf16[528,256]{1,0:T(8,128)(2,1)S(1)}, u32[]{:S(2)}, u32[]{:S(2)}) collective-permute-start(bf16[528,256]{1,0:T(8,128)(2,1)S(1)} %attend.18.refs_6_.refs_4_), channel_id=1, source_target_pairs={{0,1},{1,0},{2,3},{3,2},{4,5},{5,4},{6,7},{7,6},{8,9},{9,8},{10,11... | collective-permute-start | bytes 811016 | tf_op jit(solution)/shard_map/ppermute | solution.py:278
  204.8 5.6 %collective-permute-start.17 = (bf16[176,256]{1,0:T(8,128)(2,1)S(1)}, bf16[176,256]{1,0:T(8,128)(2,1)S(1)}, u32[]{:S(2)}, u32[]{:S(2)}) collective-permute-start(bf16[176,256]{1,0:T(8,128)(2,1)S(1)} %attend.19.refs_6_), channel_id=1, source_target_pairs={{0,1},{1,0},{2,3},{3,2},{4,5},{5,4},{6,7},{7,6},{8,9},{9,8},{10,11... | collective-permute-start | bytes 270344 | tf_op jit(solution)/shard_map/ppermute | solution.py:278
  207.6 5.3 %collective-permute-start.18 = (bf16[176,256]{1,0:T(8,128)(2,1)S(1)}, bf16[176,256]{1,0:T(8,128)(2,1)S(1)}, u32[]{:S(2)}, u32[]{:S(2)}) collective-permute-start(bf16[176,256]{1,0:T(8,128)(2,1)S(1)} %attend.20.refs_6_), channel_id=1, source_target_pairs={{0,1},{1,0},{2,3},{3,2},{4,5},{5,4},{6,7},{7,6},{8,9},{9,8},{10,11... | collective-permute-start | bytes 270344 | tf_op jit(solution)/shard_map/ppermute | solution.py:278
  208.9 6.6 %collective-permute-start.19 = (bf16[176,256]{1,0:T(8,128)(2,1)S(1)}, bf16[176,256]{1,0:T(8,128)(2,1)S(1)}, u32[]{:S(2)}, u32[]{:S(2)}) collective-permute-start(bf16[176,256]{1,0:T(8,128)(2,1)S(1)} %attend.21.refs_8_.refs_6_), channel_id=1, source_target_pairs={{0,1},{1,0},{2,3},{3,2},{4,5},{5,4},{6,7},{7,6},{8,9},{9,8},{10,11... | collective-permute-start | bytes 270344 | tf_op jit(solution)/shard_map/ppermute | solution.py:278
